TPU v7x, 32 devices: a whole 2x2x4 slice. The times are simulated.
32 devices in a mesh: gx: 8 (over z, y), gy: 4 (over x, core).
Axes of the slice: x: 2, y: 2, z: 4, core: 2. Of those that a mesh axis runs over, the one named last changes fastest.
Arguments:
- strips: float32 [2048, 2, 16, 128], P(('gx', 'gy')), may hold values from -6 to 6
- routes: int32 [2048, 8], P(('gx', 'gy')), may hold values from 0 to 128, as said below
- conv1_weight: float32 [16, 1, 3, 3, 3], replicated, may hold values from -1.25 to 1.25
- conv1_bias: float32 [16], replicated, may hold values from -3 to 3
- conv2_weight: float32 [32, 16, 3, 3, 3], replicated, may hold values from -0.3125 to 0.3125
- conv2_bias: float32 [32], replicated, may hold values from -3 to 3
Outputs:
- features: float32 [32, 1, 512, 512], P(None, None, 'gx', 'gy')
Inputs may be any that keep to these rules, and one draw needn't show every extreme that they name: `routes`: slots with v = 0 are all zero. Each device's region receives exactly 64 live strips and their footprints cover every cell of it; one holder keeps at most 2 live strips for one destination, and exactly 2 for some; some holder keeps 64 live strips.
All inputs are finite; a program needn't handle non-finite values.
Results may differ from a plain program's by a relative error of at most 0.0003.
Values sent between devices are 32-bit elements; how exact they have to be, the bound alone decides.
No kernel may reach another device: no remote copies, remote signals or barrier semaphores. Data moves between devices by JAX's collectives and lax.ppermute only.
A program may use at most 192 MiB of HBM per device.

v0:
```python
import jax
import jax.numpy as jnp
from jax import lax
from jax.sharding import PartitionSpec as P

BY = 128
BX = 128
BLK = 2
STRIPS = 64


PRECISE = lax.Precision.HIGHEST


def padded_2(block, sides, width):
    for axis, dim in sides:
        count = lax.axis_size(axis)
        forward = [(i, i + 1) for i in range(count - 1)]
        backward = [(target, source) for source, target in forward]
        low = lax.ppermute(
            lax.slice_in_dim(block, block.shape[dim] - width, None, axis=dim), axis, forward
        )
        high = lax.ppermute(lax.slice_in_dim(block, 0, width, axis=dim), axis, backward)
        block = jnp.concatenate([low, block, high], axis=dim)
    return block


def from_behind(shard, axis, by):
    length = lax.axis_size(axis)
    pairs = [(i, i + by) for i in range(length) if 0 <= i + by < length]
    return lax.ppermute(shard, axis, pairs)


def interp_table(sixteenths, length):
    fraction = sixteenths.astype(jnp.float32) / 16.0
    out_pos = lax.broadcasted_iota(jnp.int32, (length, length), 0)
    in_pos = lax.broadcasted_iota(jnp.int32, (length, length), 1)
    on_diag = (in_pos == out_pos).astype(jnp.float32)
    off_diag = (in_pos == out_pos + 1).astype(jnp.float32)
    return (1.0 - fraction)[:, None, None] * on_diag[None] + fraction[:, None, None] * off_diag[
        None
    ]


def ramp_table(ramp_width, length):
    position = lax.broadcasted_iota(jnp.int32, (1, length), 1)
    to_edge = jnp.minimum(position + 1, length - position)
    return jnp.minimum(to_edge, ramp_width[:, None]).astype(jnp.float32)


def resample(strip_data, params):
    planes = strip_data.shape[1]
    strip_rows = strip_data.shape[2]
    strip_cols = strip_data.shape[3]
    along_x = (
        interp_table(params[:, 6], strip_cols) * ramp_table(params[:, 7], strip_cols)[:, :, None]
    )
    along_y = (
        interp_table(params[:, 5], strip_rows) * ramp_table(params[:, 7], strip_rows)[:, :, None]
    )
    along_z = interp_table(params[:, 4], planes)
    shifted = jnp.einsum("kzyc,kxc->kzyx", strip_data, along_x, precision=PRECISE)
    shifted = jnp.einsum("kzbx,kyb->kzyx", shifted, along_y, precision=PRECISE)
    return jnp.einsum("kza,kayx->kzyx", along_z, shifted, precision=PRECISE)


def place_all(pieces, params, region_rows, region_cols):
    strip_rows = pieces.shape[2]
    strip_cols = pieces.shape[3]
    grid_x = lax.broadcasted_iota(jnp.int32, (1, region_cols, strip_cols), 1)
    local_x = lax.broadcasted_iota(jnp.int32, (1, region_cols, strip_cols), 2)
    put_x = (grid_x == params[:, 3][:, None, None] + local_x).astype(jnp.float32)
    grid_y = lax.broadcasted_iota(jnp.int32, (1, region_rows, strip_rows), 1)
    local_y = lax.broadcasted_iota(jnp.int32, (1, region_rows, strip_rows), 2)
    put_y = (grid_y == params[:, 2][:, None, None] + local_y).astype(jnp.float32)
    widened = jnp.einsum("kzyx,kXx->kzyX", pieces, put_x, precision=PRECISE)
    numerator = jnp.einsum("kzyX,kYy->zYX", widened, put_y, precision=PRECISE)
    row_weight = jnp.einsum(
        "kYy,ky->kY", put_y, ramp_table(params[:, 7], strip_rows), precision=PRECISE
    )
    col_weight = jnp.einsum(
        "kXx,kx->kX", put_x, ramp_table(params[:, 7], strip_cols), precision=PRECISE
    )
    weight_total = jnp.einsum("kY,kX->YX", row_weight, col_weight, precision=PRECISE)
    return numerator / weight_total[None]


def live_order(params, needed):
    is_live = params[:, 1]
    live_rank = jnp.cumsum(is_live)
    wanted = lax.broadcasted_iota(jnp.int32, (needed, 1), 0) + 1
    slot_ids = lax.broadcasted_iota(jnp.int32, (1, is_live.shape[0]), 1)
    matches = (live_rank[None, :] == wanted) & (is_live[None, :] == 1)
    return jnp.sum(jnp.where(matches, slot_ids, 0), axis=1)


def bucketize(held_rows, params, targets, per_pair):
    destination = params[:, 0]
    is_live = params[:, 1]
    held_count = destination.shape[0]
    earlier = lax.broadcasted_iota(jnp.int32, (held_count, held_count), 1) < lax.broadcasted_iota(
        jnp.int32, (held_count, held_count), 0
    )
    same_dest = (destination[None, :] == destination[:, None]) & (is_live[None, :] == 1) & earlier
    order_in = jnp.sum(same_dest.astype(jnp.int32), axis=1)
    bucket_key = jnp.where(is_live == 1, destination * per_pair + order_in, -1)
    wanted = lax.broadcasted_iota(jnp.int32, (targets, 1), 0)
    slot_ids = lax.broadcasted_iota(jnp.int32, (1, held_count), 1)
    matches = bucket_key[None, :] == wanted
    picked = jnp.sum(jnp.where(matches, slot_ids, 0), axis=1)
    present = jnp.any(matches, axis=1)
    outgoing = (
        jnp.take(held_rows, picked, axis=0) * present.astype(jnp.float32)[:, None, None, None]
    )
    outgoing_params = jnp.take(params, picked, axis=0) * present.astype(jnp.int32)[:, None]
    return (outgoing, outgoing_params)


def convolve(volume, kernel, stride):
    result = lax.conv_general_dilated(
        volume[None],
        kernel,
        (stride, stride, stride),
        "VALID",
        dimension_numbers=("NCDHW", "OIDHW", "NCDHW"),
        precision=PRECISE,
    )
    return result[0]


def body(strips, routes, conv1_weight, conv1_bias, conv2_weight, conv2_bias):
    dev_rows = lax.axis_size("gx")
    dev_cols = lax.axis_size("gy")
    senders = dev_rows * dev_cols
    per_pair = max(1, STRIPS // senders)
    region_cols = BX * BLK
    held_rows = resample(strips, routes)
    outgoing, outgoing_params = bucketize(held_rows, routes, senders * per_pair, per_pair)
    arrived, arrived_params = (
        lax.all_to_all(outgoing, ("gx", "gy"), split_axis=0, concat_axis=0, tiled=True),
        lax.all_to_all(outgoing_params, ("gx", "gy"), split_axis=0, concat_axis=0, tiled=True),
    )
    live_slots = live_order(arrived_params, STRIPS)
    own_pieces = jnp.take(arrived, live_slots, axis=0)
    own_params = jnp.take(arrived_params, live_slots, axis=0)
    joined_volume = place_all(own_pieces, own_params, BY, region_cols)
    rimmed = padded_2(joined_volume, (("gx", 1), ("gy", 2)), 1)
    padded = jnp.pad(rimmed, ((1, 1), (0, 0), (0, 0)))
    hidden = jax.nn.relu(convolve(padded[None], conv1_weight, 1) + conv1_bias[:, None, None, None])
    left_column = from_behind(hidden[:, :, :, -1], "gy", 1)
    top_row, corner = from_behind((hidden[:, :, -1, :], left_column[:, :, -1]), "gx", 1)
    with_left = jnp.concatenate([left_column[:, :, :, None], hidden], axis=3)
    top_line = jnp.concatenate([corner[:, :, None], top_row], axis=2)
    extended = jnp.concatenate([top_line[:, :, None, :], with_left], axis=2)
    deepened = jnp.pad(extended, ((0, 0), (1, 0), (0, 0), (0, 0)))
    return convolve(deepened, conv2_weight, 2) + conv2_bias[:, None, None, None]


def solution(mesh):
    in_specs = (P(("gx", "gy"), None, None, None), P(("gx", "gy"), None), P(), P(), P(), P())
    out_specs = P(None, None, "gx", "gy")
    return jax.shard_map(body, mesh=mesh, in_specs=in_specs, out_specs=out_specs, check_vma=False)
```

profile of v0, /device:TPU:0, one launch (start us, length us, event | category | flops | bytes accessed | tf_op | source)
XLA Modules:
  0.0 620.9 jit_solution(6061613474841814860)
XLA Ops:
  0.0 0.8 slice_bitcast_fusion.3
  1.2 0.7 add_select_fusion
  2.1 0.8 copy.79
  3.0 0.6 gather_fusion
  3.6 0.7 select_multiply_fusion.1
  4.3 7.3 %all-to-all-start = ((s32[32,2,8]{2,1,0:T(2,128)}), s32[32,2,8]{2,1,0:T(2,128)S(1)}, u32[]{:S(2)}, u32[]{:S(2)}) async-start(s32[32,2,8]{2,1,0:T(2,128)} %bitcast.1), calls=%async_computation | async-start | bytes 65536 | tf_op jit(solution)/shard_map/all_to_all | solution.py:141
  11.6 0.8 broadcast_subtract_fusion.2
  12.4 0.8 multiply_bitcast_fusion.2
  13.5 5.3 all-to-all-done
  19.5 0.6 gather_fusion.1
  20.6 7.1 %fusion.40 = f32[64,2,16,128]{3,2,1,0:T(8,128)S(1)} fusion(f32[64,2,16,128]{3,2,1,0:T(8,128)S(1)} %copy-done, f32[64,128]{1,0:T(8,128)S(1)} %get-tuple-element.24, f32[128,128]{1,0:T(8,128)S(1)} %get-tuple-element.31, f32[64]{0:T(128)S(1)} %get-tuple-element.19, f32[128,128]{1,0:T(8,128)S(1)} %get-tuple-element.30, f32[64]{0:T(128)S(1)} %get-tuple-element.15), kind=kOutput, calls=%fused_computation.49 | convolution fusion | flops 406847488 | bytes 2261504 | tf_op jit(solution)/shard_map/kzyc,kxc->kzyx/dot_general | solution.py:62
  27.7 1.2 convolution_bitcast_fusion
  28.9 3.9 fusion.53
  32.7 1.7 gather_fusion.2
  34.4 1.5 select_multiply_fusion
  36.0 2.9 all-to-all-start.1
  39.4 3.9 fusion.14
  43.6 21.4 %all-to-all-done.1 = f32[64,2,16,128]{3,1,2,0:T(2,128)S(1)} async-done(((f32[64,2,16,128]{3,1,2,0:T(2,128)}), f32[64,2,16,128]{3,1,2,0:T(2,128)S(1)}, u32[]{:S(2)}, u32[]{:S(2)}) %all-to-all-start.1) | async-done | bytes 1048608 | tf_op jit(solution)/shard_map/all_to_all | solution.py:140
  65.1 1.7 gather_fusion.3
  67.3 4.7 fusion.16
  71.9 2.3 fusion.49
  74.3 3.4 collective-permute-start
  77.7 1.3 collective-permute-start.1
  79.0 4.2 collective-permute-done.1
  83.3 1.3 collective-permute-start.2
  84.6 1.3 collective-permute-start.3
  85.9 3.7 collective-permute-done.3
  90.5 16.4 %copy.85 = f32[1,4,130,1,8,33]{4,0,5,3,2,1:T(1,128)} copy(f32[1,4,130,1,8,33]{2,1,5,4,3,0:T(4,128)S(1)} %bitcast.126) | data formatting | bytes 1098240 | tf_op jit(solution)/shard_map/conv_general_dilated | solution.py:120
  106.9 2.2 slice.93
  109.2 18.9 %fusion.109 = f32[1,4,130,8,35]{3,0,4,2,1:T(1,128)S(1)} fusion(f32[1,4,130,1,7,2]{4,0,5,3,2,1:T(1,128)S(1)} %slice.93, f32[1,4,130,1,8,33]{4,0,5,3,2,1:T(1,128)} %copy.85), kind=kLoop, calls=%fused_computation.21.clone.clone.1 | loop fusion | flops 436800 | bytes 1160640 | tf_op jit(solution)/shard_map/conv_general_dilated | solution.py:120
  128.1 286.2 %convolution_select_fusion = f32[2,128,8,33,16]{4,2,3,1,0:T(8,128)} fusion(f32[16,1,3,3,3]{0,1,4,3,2:T(1,128)S(1)} %copy-done.6, pred[8,33]{0,1:T(8,128)(4,1)S(1)} %copy-done.7, f32[1,4,130,8,35]{3,0,4,2,1:T(1,128)S(1)} %fusion.109), kind=kOutput, calls=%fused_computation.13 | convolution fusion | flops 351436800 | bytes 4909768 | tf_op jit(solution)/shard_map/conv_general_dilated | solution.py:120
  414.3 20.2 %copy.86 = f32[2,128,8,33,16]{1,4,3,2,0:T(8,128)} copy(f32[2,128,8,33,16]{4,2,3,1,0:T(8,128)} %convolution_select_fusion) | data formatting | bytes 8650752 | tf_op jit(solution)/shard_map/conv_general_dilated | solution.py:120
  434.5 2.5 fusion.21
  437.1 5.5 collective-permute-start.4
  442.6 3.1 slice.97
  445.7 3.5 copy.88
  449.3 3.0 collective-permute-start.6
  452.5 1.9 collective-permute-start.5
  454.4 1.3 collective-permute-done.5
  455.9 3.8 copy.90
  459.6 9.2 %fusion.7 = f32[16,3,129,1,257]{2,0,4,1,3:T(8,128)} fusion(f32[16,2,1,257]{2,0,3,1:T(8,128)} %copy.90, f32[16,2,128,256]{2,0,3,1:T(8,128)} %copy-done.2, f32[16,2,128,1]{2,0,3,1:T(8,128)S(1)} %bitcast.130), kind=kLoop, calls=%fused_computation.15 | loop fusion | flops 9548064 | bytes 10608960 | tf_op jit(solution)/shard_map/broadcast_in_dim | solution.py:121
  468.9 11.4 %pad.12 = f32[16,3,129,1,272]{2,0,4,1,3:T(8,128)} pad(f32[16,3,129,1,257]{2,0,4,1,3:T(8,128)} %fusion.7, f32[]{:T(128)} %constant.17.clone.1), padding=0_0x0_0x0_0x0_0x0_15 | pad | bytes 13102276 | tf_op jit(solution)/shard_map/broadcast_in_dim | solution.py:121
  480.3 61.9 %copy.92 = f32[16,3,129,1,8,34]{0,4,5,2,1,3:T(8,128)} copy(f32[16,3,129,1,8,34]{2,0,5,4,1,3:T(8,128)} %bitcast.123) | data formatting | bytes 13473792 | tf_op jit(solution)/shard_map/conv_general_dilated | solution.py:120
  542.2 2.2 slice.98
  544.5 66.7 %broadcast_select_fusion = f32[1,64,8,17,32]{4,2,3,1,0:T(8,128)} fusion(pred[8,17]{0,1:T(8,128)(4,1)S(1)} %copy-done.8, f32[32,16,3,3,3]{0,1,4,3,2:T(8,128)S(1)} %copy-done.5, f32[16,3,129,1,7,2]{0,4,5,2,1,3:T(8,128)S(1)} %slice.98, f32[16,3,129,1,8,34]{0,4,5,2,1,3:T(8,128)} %copy.92), kind=kOutput, calls=%fused_computation.39 | convolution fusion | flops 1449517568 | bytes 8253192 | tf_op jit(solution)/shard_map/conv_general_dilated | solution.py:120
  611.2 4.0 copy.93
  615.2 1.7 fusion.30
  616.9 3.6 copy.94
  (65 shorter events, 4.9 us)
Async XLA Ops:
  0.0 20.6 %copy-start = (f32[64,2,16,128]{3,2,1,0:T(8,128)S(1)}, f32[64,2,16,128]{3,2,1,0:T(8,128)}, u32[]{:S(2)}) copy-start(f32[64,2,16,128]{3,2,1,0:T(8,128)} %param.10) | copy-start | bytes 3145732
  4.3 14.6 %all-to-all-start = ((s32[32,2,8]{2,1,0:T(2,128)}), s32[32,2,8]{2,1,0:T(2,128)S(1)}, u32[]{:S(2)}, u32[]{:S(2)}) async-start(s32[32,2,8]{2,1,0:T(2,128)} %bitcast.1), calls=%async_computation | async-start | bytes 65536 | tf_op jit(solution)/shard_map/all_to_all | solution.py:141
  36.0 29.1 %all-to-all-start.1 = ((f32[64,2,16,128]{3,1,2,0:T(2,128)}), f32[64,2,16,128]{3,1,2,0:T(2,128)S(1)}, u32[]{:S(2)}, u32[]{:S(2)}) async-start(f32[64,2,16,128]{3,1,2,0:T(2,128)} %select_multiply_fusion), calls=%async_computation.1 | async-start | bytes 2097152 | tf_op jit(solution)/shard_map/all_to_all | solution.py:140
  74.3 4.7 collective-permute-start
  77.7 5.5 collective-permute-start.1
  83.3 2.6 collective-permute-start.2
  84.6 5.0 collective-permute-start.3
  109.1 19.0 %copy-start.6 = (f32[16,1,3,3,3]{0,1,4,3,2:T(1,128)S(1)}, f32[16,1,3,3,3]{0,1,4,3,2:T(1,128)}, u32[]{:S(2)}) copy-start(f32[16,1,3,3,3]{0,1,4,3,2:T(1,128)} %param.12) | copy-start | bytes 5188
  109.2 19.0 %copy-start.7 = (pred[8,33]{0,1:T(8,128)(4,1)S(1)}, pred[8,33]{0,1:T(8,128)(4,1)}, u32[]{:S(2)}) copy-start(pred[8,33]{0,1:T(8,128)(4,1)} %constant.68) | copy-start | bytes 796
  414.3 20.2 %copy-start.3 = (f32[16]{0:T(128)S(1)}, f32[16]{0:T(128)}, u32[]{:S(2)}) copy-start(f32[16]{0:T(128)} %param.13) | copy-start | bytes 196
  437.1 5.6 copy-start.2
  437.1 15.2 %collective-permute-start.4 = (f32[16,2,128]{2,0,1:T(8,128)S(1)}, f32[16,2,128]{2,0,1:T(8,128)S(1)}, u32[]{:S(2)}, u32[]{:S(2)}) collective-permute-start(f32[16,2,128]{2,0,1:T(8,128)S(1)} %slice_bitcast_fusion.2), channel_id=1, source_target_pairs={{0,1},{1,2},{2,3},{4,5},{5,6},{6,7},{8,9},{9,10},{10,11},{12,13},{... | collective-permute-start | bytes 49160 | tf_op jit(solution)/shard_map/ppermute | solution.py:31
  449.3 6.5 %collective-permute-start.6 = (f32[16,2,256]{2,0,1:T(8,128)S(1)}, f32[16,2,256]{2,0,1:T(8,128)S(1)}, u32[]{:S(2)}, u32[]{:S(2)}) collective-permute-start(f32[16,2,256]{2,0,1:T(8,128)S(1)} %bitcast.131), channel_id=1, source_target_pairs={{0,4},{4,8},{8,12},{12,16},{16,20},{20,24},{24,28},{1,5},{5,9},{9,... | collective-permute-start | bytes 98312 | tf_op jit(solution)/shard_map/ppermute | solution.py:31
  452.5 3.2 collective-permute-start.5
  480.3 64.1 %copy-start.5 = (f32[32,16,3,3,3]{0,1,4,3,2:T(8,128)S(1)}, f32[32,16,3,3,3]{0,1,4,3,2:T(8,128)}, u32[]{:S(2)}) copy-start(f32[32,16,3,3,3]{0,1,4,3,2:T(8,128)} %param.14) | copy-start | bytes 165892
  480.3 64.1 %copy-start.8 = (pred[8,17]{0,1:T(8,128)(4,1)S(1)}, pred[8,17]{0,1:T(8,128)(4,1)}, u32[]{:S(2)}) copy-start(pred[8,17]{0,1:T(8,128)(4,1)} %constant.67) | copy-start | bytes 412
  544.4 70.8 %copy-start.4 = (f32[32]{0:T(128)S(1)}, f32[32]{0:T(128)}, u32[]{:S(2)}) copy-start(f32[32]{0:T(128)} %param.15) | copy-start | bytes 388
  544.5 76.1 %copy-start.1 = (f32[64,2,16,128]{3,2,1,0:T(8,128)S(1)}, f32[64,2,16,128]{3,2,1,0:T(8,128)}, u32[]{:S(2)}) copy-start(f32[64,2,16,128]{3,2,1,0:T(8,128)} %param.10) | copy-start | bytes 3145732
where the time goes:
time: 631 us; the launch traced here: 621 us
  matrix products  377 us (60%)
  local copies, waits for them, and re-layouts  140 us (22%)
  other arithmetic  39.6 us (6%)
  waiting for transfers between devices  35.9 us (6%)
  starting transfers between devices  28 us (4%)
    conv_general_dilated x2, matrix products, convolve(): lax.conv_general_dilated(volume[None], kernel, (stride, stride, stride),...  353 us
    conv_general_dilated x6, local copies, waits for them, and re-layouts, convolve(): lax.conv_general_dilated(volume[None], kernel, (stride, stride, stride),...  107 us
    all_to_all x1, waiting for transfers between devices, body(): lax.all_to_all(outgoing, ('gx', 'gy'), split_axis=0, concat_axis=0, tiled...  21.4 us
    conv_general_dilated x1, other arithmetic, convolve(): lax.conv_general_dilated(volume[None], kernel, (stride, stride, stride),...  18.9 us
  transfers between devices with their start and end apart: 9, of which 5 were waited for; matrix products, arithmetic and copies ran while one was open for 2% of the time, Pallas kernels for 0%

commit v1 on v0

v1 whole, which is shorter than its diff:
```python
import jax
import jax.numpy as jnp
import numpy as np
from jax import lax
from jax.experimental import pallas as pl
from jax.experimental.pallas import tpu as pltpu
from jax.sharding import PartitionSpec as P

BZ = 2
BY = 128
BX = 128
BLK = 2
STRIPS = 64
SY = 16
SX = 128
C1 = 16
C2 = 32

COLS = BX * BLK
HALF = COLS // 2
TOP = 2
SROW = 136
OUT_ROWS = 4
HID_ROWS = 9
WIN = 16
BLOCKS = BY // (2 * OUT_ROWS)
PHASES = 5
K1 = 3 * BZ * WIN
HID = HID_ROWS * C1 * BZ
K2 = 3 * HID
OUTM = OUT_ROWS * C2

EXACT = lax.Precision.HIGHEST
F32 = jnp.float32
BF16 = jnp.bfloat16


def iota(shape, dim):
    return lax.broadcasted_iota(jnp.int32, shape, dim)


def split_kernel(x):
    hi = x.astype(BF16)
    return hi, (x - hi.astype(F32)).astype(BF16)


def split_host(x):
    hi = lax.reduce_precision(x, 8, 7)
    return hi.astype(BF16), (x - hi).astype(BF16)


def pack_body(per_pair, slots, routes, strips, outgoing, outgoing_params, count):
    held = routes.shape[0]
    senders = slots // per_pair

    def clear(i, carry):
        count[i] = 0
        return carry

    lax.fori_loop(0, senders, clear, 0)
    if slots != STRIPS:
        outgoing[...] = jnp.zeros(outgoing.shape, F32)

        def clear_params(i, carry):
            for q in range(8):
                outgoing_params[i, q] = 0
            return carry

        lax.fori_loop(0, slots, clear_params, 0)

    def place(k, carry):
        @pl.when(routes[k, 1] == 1)
        def _():
            dest = routes[k, 0]
            rank = count[dest]
            count[dest] = rank + 1
            slot = jnp.minimum(dest * per_pair + rank, slots - 1)
            outgoing[slot] = strips[k]
            for q in range(8):
                outgoing_params[slot, q] = routes[k, q]

        return carry

    lax.fori_loop(0, held, place, 0)


def pack(strips, routes, senders, per_pair):
    slots = senders * per_pair
    held = strips.shape[0]
    rows = BZ * SY
    return pl.pallas_call(
        lambda *refs: pack_body(per_pair, slots, *refs),
        in_specs=[
            pl.BlockSpec(memory_space=pltpu.SMEM),
            pl.BlockSpec(memory_space=pltpu.VMEM),
        ],
        out_specs=[
            pl.BlockSpec(memory_space=pltpu.VMEM),
            pl.BlockSpec(memory_space=pltpu.SMEM),
        ],
        out_shape=[
            jax.ShapeDtypeStruct((slots, rows, SX), F32),
            jax.ShapeDtypeStruct((slots, 8), jnp.int32),
        ],
        scratch_shapes=[pltpu.SMEM((senders,), jnp.int32)],
        name="pack",
    )(routes, strips.reshape(held, rows, SX))


def join_body(slots, params, columns, strips, joined, right_message, left_message, data, place_y):
    lane = iota((SY, SX), 1)
    sub = iota((SY, SX), 0)
    row_lane = iota((SY, 256), 1)
    row_sub = iota((SY, 256), 0)

    def one(k, carry):
        live = params[k, 1].astype(F32)
        top = params[k, 2]
        left = params[k, 3]
        frac_z = params[k, 4].astype(F32) * (1.0 / 16.0)
        frac_y = params[k, 5].astype(F32) * (1.0 / 16.0)
        frac_x = params[k, 6].astype(F32) * (1.0 / 16.0)
        ramp = params[k, 7]
        weight = jnp.minimum(jnp.minimum(lane + 1, SX - lane), ramp).astype(F32)
        here = weight * (1.0 - frac_x)
        there = jnp.where(lane < SX - 1, weight * frac_x, 0.0)
        stay_z = live * (1.0 - frac_z)
        move_z = live * frac_z
        first = strips[k, :SY, :]
        second = strips[k, SY:, :]
        plane0 = stay_z * first + move_z * second
        plane1 = stay_z * second
        shift = left & (SX - 1)
        for z, plane in enumerate((plane0, plane1)):
            piece = here * plane + there * pltpu.roll(plane, SX - 1, 1)
            turned = pltpu.roll(piece, shift, 1)
            low = jnp.where(lane >= left, turned, 0.0)
            high = jnp.where(lane < left, turned, 0.0)
            for side, part in enumerate((low, high)):
                coarse, fine = split_kernel(part)
                at = z * COLS + side * SX
                data[pl.ds(k * SY, SY), at : at + SX] = coarse
                data[pl.ds(k * SY, SY), BZ * COLS + at : BZ * COLS + at + SX] = fine
        y = row_lane - TOP - top
        weight_y = jnp.minimum(jnp.minimum(y + 1, SY - y), ramp).astype(F32)
        spread = jnp.where(row_sub == y, weight_y * (1.0 - frac_y), 0.0) + jnp.where(
            row_sub == y + 1, weight_y * frac_y, 0.0
        )
        place_y[pl.ds(k * SY, SY), :] = spread.astype(BF16)
        return carry

    lax.fori_loop(0, slots, one, 0, unroll=4)

    live = columns[:, 1:2]
    top = columns[:, 2:3]
    left = columns[:, 3:4]
    ramp = columns[:, 7:8]
    y = iota((slots, 256), 1) - TOP - top
    weight_y = jnp.where((y >= 0) & (y < SY), jnp.minimum(jnp.minimum(y + 1, SY - y), ramp), 0)
    col = iota((slots, COLS), 1)
    x = jnp.where(col < HALF, 2 * col, 2 * (col - HALF) + 1) - left
    weight_x = jnp.where((x >= 0) & (x < SX), jnp.minimum(jnp.minimum(x + 1, SX - x), ramp), 0)
    weight_y = (weight_y * live).astype(F32).astype(BF16)
    weight_x = weight_x.astype(F32).astype(BF16)
    over_rows = (((0,), (0,)), ((), ()))
    total = lax.dot_general(weight_y, weight_x, over_rows, preferred_element_type=F32)[:SROW]
    sums = lax.dot_general(place_y[...], data[...], over_rows, preferred_element_type=F32)[:SROW]
    sums = sums[:, : BZ * COLS] + sums[:, BZ * COLS :]

    src = iota((COLS, COLS), 0)
    dst = iota((COLS, COLS), 1)
    order = (src == jnp.where(dst < HALF, 2 * dst, 2 * (dst - HALF) + 1)).astype(F32).astype(BF16)
    row = iota((SROW, COLS), 0)
    inside = (row >= TOP) & (row < TOP + BY)
    pick_row = iota((8, COLS), 0)
    pick_col = iota((8, COLS), 1)
    pick = jnp.where(
        ((pick_row == 0) & (pick_col == HALF - 1))
        | ((pick_row == 1) & (pick_col == COLS - 1))
        | ((pick_row == 2) & (pick_col == 0)),
        1.0,
        0.0,
    )
    edges = []
    for z in range(BZ):
        coarse, fine = split_kernel(sums[:, z * COLS : (z + 1) * COLS])
        ordered = jnp.dot(coarse, order, preferred_element_type=F32) + jnp.dot(
            fine, order, preferred_element_type=F32
        )
        value = jnp.where(inside, ordered / jnp.where(inside, total, 1.0), 0.0)
        joined[z] = value
        edges.append(
            lax.dot_general(
                pick, value, (((1,), (1,)), ((), ())), precision=EXACT, preferred_element_type=F32
            )
        )
    right_message[...] = jnp.concatenate(edges, axis=0)
    left_message[...] = jnp.concatenate(edges, axis=0)


def join(strips, params):
    slots = params.shape[0]
    vmem = pl.BlockSpec(memory_space=pltpu.VMEM)
    return pl.pallas_call(
        lambda *refs: join_body(slots, *refs),
        in_specs=[pl.BlockSpec(memory_space=pltpu.SMEM), vmem, vmem],
        out_specs=[vmem, vmem, vmem],
        out_shape=[
            jax.ShapeDtypeStruct((BZ, SROW, COLS), F32),
            jax.ShapeDtypeStruct((16, SROW), F32),
            jax.ShapeDtypeStruct((16, SROW), F32),
        ],
        scratch_shapes=[
            pltpu.VMEM((slots * SY, 2 * BZ * COLS), BF16),
            pltpu.VMEM((slots * SY, 256), BF16),
        ],
        compiler_params=pltpu.CompilerParams(vmem_limit_bytes=48 * 2**20),
        name="join",
    )(params, params, strips)


def phases_body(joined, from_left, from_right, phases, down_message, up_message):
    lane = iota((SROW, HALF), 1)
    row16 = iota((16, HALF), 0)
    lane16 = iota((16, HALF), 1)
    over_rows = (((0,), (0,)), ((), ()))
    for z in range(BZ):

        def column(message, row, lane_at):
            pick = jnp.where((row16 == 8 * z + row) & (lane16 == lane_at), 1.0, 0.0)
            return lax.dot_general(
                message[...], pick, over_rows, precision=EXACT, preferred_element_type=F32
            )

        even = joined[z, :, :HALF]
        odd = joined[z, :, HALF:]
        parts = (
            jnp.where(lane == 0, column(from_left, 0, 0), pltpu.roll(even, 1, 1)),
            jnp.where(lane == 0, column(from_left, 1, 0), pltpu.roll(odd, 1, 1)),
            even,
            odd,
            jnp.where(lane == HALF - 1, column(from_right, 2, HALF - 1), pltpu.roll(even, HALF - 1, 1)),
        )
        for j, part in enumerate(parts):
            phases[j, z] = part
            down_message[j, z] = part[BY : BY + 8]
            up_message[j, z] = part[0:8]


def make_phases(joined, from_left, from_right):
    vmem = pl.BlockSpec(memory_space=pltpu.VMEM)
    return pl.pallas_call(
        phases_body,
        in_specs=[vmem, vmem, vmem],
        out_specs=[vmem, vmem, vmem],
        out_shape=[
            jax.ShapeDtypeStruct((PHASES, BZ, SROW, HALF), F32),
            jax.ShapeDtypeStruct((PHASES, BZ, 8, HALF), F32),
            jax.ShapeDtypeStruct((PHASES, BZ, 8, HALF), F32),
        ],
        name="phases",
    )(joined, from_left, from_right)


def conv_body(edge, from_above, from_below, phases_in, first, second, bias, out, phases, coarse_h, fine_h):
    row8 = iota((8, HALF), 0)
    for j in range(PHASES):
        for z in range(BZ):
            phases[j, z, 8 : SROW - 8, :] = phases_in[j, z, 8 : SROW - 8, :]
            phases[j, z, 0:8, :] = jnp.where(row8 < TOP, from_above[j, z], phases_in[j, z, 0:8, :])
            below = jnp.where(row8 == 2, from_below[j, z], 0.0)
            phases[j, z, SROW - 8 : SROW, :] = jnp.where(
                row8 < 2, phases_in[j, z, SROW - 8 : SROW, :], below
            )
    no_row = edge[0] == 0
    no_col = edge[1] == 0
    lane = iota((HID, 256), 1)
    hid_row = iota((HID, 256), 0)
    ones = jnp.ones((16, 256), BF16)

    def pair(step, carry):
        blocks = (step, step + BLOCKS // 2)
        wide = {}
        for j in range(PHASES):
            for z in range(BZ):
                cut = [
                    phases[j, z, pl.ds(pl.multiple_of(8 * b, 8), WIN), :] for b in blocks
                ]
                wide[j, z] = split_kernel(jnp.concatenate(cut, axis=1))
        for group in range(3):
            coarse = [wide[group + dx, z][0] for dx in range(3) for z in range(BZ)]
            fine = [wide[group + dx, z][1] for dx in range(3) for z in range(BZ)]
            stacked = jnp.concatenate(coarse + fine + coarse + [ones], axis=0)
            hidden = jnp.dot(first[...], stacked, preferred_element_type=F32)
            hidden = jnp.maximum(hidden, 0.0)
            outside = no_row & (step == 0) & (hid_row < C1 * BZ) & (lane < HALF)
            if group == 0:
                outside = outside | (no_col & ((lane & (HALF - 1)) == 0))
            hidden = jnp.where(outside, 0.0, hidden)
            coarse, fine = split_kernel(hidden)
            coarse_h[group * HID : (group + 1) * HID, :] = coarse
            fine_h[group * HID : (group + 1) * HID, :] = fine
        both = jnp.dot(second[...], coarse_h[...], preferred_element_type=F32)
        rest = jnp.dot(second[:OUTM, :], fine_h[...], preferred_element_type=F32)
        result = both[:OUTM] + both[OUTM:] + rest
        for side, b in enumerate(blocks):
            for r in range(OUT_ROWS):
                at = OUT_ROWS * b + r
                out[pl.ds(at, C2, stride=BY // 2), :] = (
                    result[r * C2 : (r + 1) * C2, side * HALF : (side + 1) * HALF] + bias[...]
                )
        return carry

    lax.fori_loop(0, BLOCKS // 2, pair, 0)


def convolve(edge, from_above, from_below, phases, first, second, bias):
    vmem = pl.BlockSpec(memory_space=pltpu.VMEM)
    return pl.pallas_call(
        conv_body,
        in_specs=[pl.BlockSpec(memory_space=pltpu.SMEM)] + [vmem] * 6,
        out_specs=vmem,
        out_shape=jax.ShapeDtypeStruct((C2 * BY // 2, HALF), F32),
        scratch_shapes=[
            pltpu.VMEM((PHASES, BZ, SROW, HALF), F32),
            pltpu.VMEM((K2, 256), BF16),
            pltpu.VMEM((K2, 256), BF16),
        ],
        compiler_params=pltpu.CompilerParams(vmem_limit_bytes=48 * 2**20),
        name="convolve",
    )(edge, from_above, from_below, phases, first, second, bias)


def first_table(weight, bias):
    kernel = weight[:, 0]
    planes = jnp.stack([kernel[:, 1:3], kernel[:, 0:2]], axis=1)
    reach = np.zeros((HID_ROWS, 3, WIN), np.float32)
    for i in range(HID_ROWS):
        for dy in range(3):
            reach[i, dy, i + dy] = 1.0
    table = jnp.einsum("czpyx,iys->iczxps", planes, jnp.asarray(reach), precision=EXACT)
    coarse, fine = split_host(table.reshape(HID, K1))
    each = jnp.tile(jnp.repeat(bias, BZ), HID_ROWS)
    one = lax.reduce_precision(each, 8, 7)
    two = lax.reduce_precision(each - one, 8, 7)
    three = each - one - two
    tail = jnp.stack([one, two, three], axis=1).astype(BF16)
    tail = jnp.pad(tail, ((0, 0), (0, 16 - 3)))
    return jnp.concatenate([coarse, coarse, fine, tail], axis=1)


def second_table(weight):
    reach = np.zeros((OUT_ROWS, 3, HID_ROWS), np.float32)
    for i in range(OUT_ROWS):
        for dy in range(3):
            reach[i, dy, 2 * i + dy] = 1.0
    table = jnp.einsum("oczyx,iyh->ioxhcz", weight[:, :, 1:3], jnp.asarray(reach), precision=EXACT)
    coarse, fine = split_host(table.reshape(OUTM, K2))
    return jnp.concatenate([coarse, fine], axis=0)


def shift(values, axis, by):
    length = lax.axis_size(axis)
    pairs = [(i, i + by) for i in range(length) if 0 <= i + by < length]
    return lax.ppermute(values, axis, pairs)


def body(strips, routes, conv1_weight, conv1_bias, conv2_weight, conv2_bias):
    senders = lax.axis_size("gx") * lax.axis_size("gy")
    per_pair = max(1, STRIPS // senders)
    outgoing, outgoing_params = pack(strips, routes, senders, per_pair)
    axes = ("gx", "gy")
    arrived = lax.all_to_all(outgoing, axes, split_axis=0, concat_axis=0, tiled=True)
    arrived_params = lax.all_to_all(outgoing_params, axes, split_axis=0, concat_axis=0, tiled=True)
    first = first_table(conv1_weight, conv1_bias)
    second = second_table(conv2_weight)
    bias = jnp.broadcast_to(conv2_bias[:, None], (C2, HALF))
    edge = jnp.stack([lax.axis_index("gx"), lax.axis_index("gy")]).astype(jnp.int32)

    joined, right_message, left_message = join(arrived, arrived_params)
    from_left = shift(right_message, "gy", 1)
    from_right = shift(left_message, "gy", -1)
    phases, down_message, up_message = make_phases(joined, from_left, from_right)
    from_above = shift(down_message, "gx", 1)
    from_below = shift(up_message, "gx", -1)
    features = convolve(edge, from_above, from_below, phases, first, second, bias)
    return features.reshape(C2, 1, BY // 2, HALF)


def solution(mesh):
    in_specs = (P(("gx", "gy"), None, None, None), P(("gx", "gy"), None), P(), P(), P(), P())
    out_specs = P(None, None, "gx", "gy")
    return jax.shard_map(body, mesh=mesh, in_specs=in_specs, out_specs=out_specs, check_vma=False)
```

time: 631 us -> 86 us (0.14); the launches traced: 621 us -> 85 us
  matrix products: 377 us -> 3.73 us
  local copies, waits for them, and re-layouts: 140 us -> 7.65 us
  other arithmetic: 39.6 us -> 0.43 us
  Pallas kernels: 0 us -> 22 us
  starting transfers between devices: 28 us -> 9.9 us
  blocking collectives: 0 us -> 14.6 us
  waiting for transfers between devices: 35.9 us -> 26.4 us
    conv_general_dilated x2 -> x0, matrix products: 353 us -> none  [convolve(): lax.conv_general_dilated(volume[None], kernel, (stride, stride, stride),...]
    conv_general_dilated x6 -> x0, local copies, waits for them, and re-layouts: 107 us -> none  [convolve(): lax.conv_general_dilated(volume[None], kernel, (stride, stride, stride),...]
    pallas_call x0 -> x4, Pallas kernels: none -> 22 us  [the longest x1 9.97 us: convolve(): pl.pallas_call(conv_body, in_specs=[pl.BlockSpec(memory_space=pltpu.SMEM)...]
    dot_general x8 -> x2, matrix products: 23.7 us -> 3.73 us  [the longest x1 2.71 us: second_table(): jnp.einsum('oczyx,iyh->ioxhcz', weight[:, :, 1:3], jnp.asarray(reach), pr...]
    conv_general_dilated x1 -> x0, other arithmetic: 18.9 us -> none  [convolve(): lax.conv_general_dilated(volume[None], kernel, (stride, stride, stride),...]
    broadcast_in_dim x3 -> x2, local copies, waits for them, and re-layouts: 15.3 us -> 0.14 us  [the longest x1 0.07 us: first_table(): each = jnp.tile(jnp.repeat(bias, BZ), HID_ROWS)]
    all_to_all x0 -> x1, blocking collectives: none -> 14.6 us  [body(): lax.all_to_all(outgoing_params, axes, split_axis=0, concat_axis=0, tiled=...]
    ppermute x7 -> x4, starting transfers between devices: 17.8 us -> 7.26 us  [shift(): return lax.ppermute(values, axis, pairs)]
  transfers between devices with their start and end apart: 9 -> 5, of which waited for: 5 -> 4; matrix products, arithmetic and copies ran while one was open for 2% -> 9% of each run, Pallas kernels for 0% -> 0%
where the time goes in v1:
time: 86 us; the launch traced here: 85 us
  waiting for transfers between devices  26.4 us (31%)
  Pallas kernels  22 us (26%)
  blocking collectives  14.6 us (17%)
  starting transfers between devices  9.9 us (12%)
  local copies, waits for them, and re-layouts  7.65 us (9%)
  matrix products  3.73 us (4%)
    all_to_all x1, waiting for transfers between devices, body(): lax.all_to_all(outgoing, axes, split_axis=0, concat_axis=0, tiled=True)  18.4 us
    all_to_all x1, blocking collectives, body(): lax.all_to_all(outgoing_params, axes, split_axis=0, concat_axis=0, tiled=...  14.6 us
    pallas_call x1, Pallas kernels, convolve(): pl.pallas_call(conv_body, in_specs=[pl.BlockSpec(memory_space=pltpu.SMEM)...  9.97 us
    ppermute x4, waiting for transfers between devices, shift(): return lax.ppermute(values, axis, pairs)  8.02 us
    ppermute x4, starting transfers between devices, shift(): return lax.ppermute(values, axis, pairs)  7.26 us
    pallas_call x1, Pallas kernels, join(): pl.pallas_call(lambda *refs: join_body(slots, *refs), in_specs=[pl.BlockS...  5.32 us
    pallas_call x1, Pallas kernels, pack(): pl.pallas_call(lambda *refs: pack_body(per_pair, slots, *refs), in_specs=...  4.06 us
    unnamed x20, local copies, waits for them, and re-layouts  3.89 us
  transfers between devices with their start and end apart: 5, of which 4 were waited for; matrix products, arithmetic and copies ran while one was open for 9% of the time, Pallas kernels for 0%

profile of v1, /device:TPU:0, one launch (start us, length us, event | category | flops | bytes accessed | tf_op | source)
XLA Modules:
  0.0 85.0 jit_solution(8703570179526804710)
XLA Ops:
  0.0 0.0 slice-start
  0.0 1.4 %copy.34.refs_0_ = s32[64,8]{1,0:T(8,128)} copy(s32[64,8]{0,1:T(8,128)} %param.9) | data formatting | bytes 4096 | tf_op args[1]
  1.4 4.1 %pack.1 = (f32[64,32,128]{2,1,0:T(8,128)}, s32[64,8]{1,0:T(8,128)}) custom-call(s32[64,8]{1,0:T(8,128)} %copy.34.refs_0_, f32[64,32,128]{2,1,0:T(8,128)} %bitcast.39), custom_call_target="tpu_custom_call" | custom-call | tf_op jit(solution)/shard_map/pack/pallas_call | solution.py:91
  5.5 14.6 %all_to_all.16 = s32[32,2,8]{2,1,0:T(2,128)S(1)} all-to-all(s32[32,2,8]{2,1,0:T(2,128)} %bitcast.41), channel_id=1, replica_groups=mesh['gx'=8,'gy'=4] {'gx','gy'}, dimensions={0} | all-to-all | bytes 4096 | tf_op jit(solution)/shard_map/all_to_all | solution.py:374
  20.0 2.6 %all-to-all-start.1 = ((f32[64,32,128]{2,1,0:T(8,128)}), f32[64,32,128]{2,1,0:T(8,128)S(1)}, u32[]{:S(2)}, u32[]{:S(2)}) async-start(f32[64,32,128]{2,1,0:T(8,128)} %get-tuple-element.14), calls=%async_computation.1 | async-start | bytes 2097152 | tf_op jit(solution)/shard_map/all_to_all | solution.py:373
  22.7 0.0 copy-done.6
  22.7 0.0 slice-done
  22.7 2.7 %convolution_bitcast_fusion = f32[4,32,3,9,16,2]{1,3,2,5,4,0:T(8,128)S(1)} fusion(f32[4,3,9,1,1,1]{2,1,5,4,3,0:T(4,128)S(1)} %copy-done.6, f32[32,16,2,3,3]{0,1,4,3,2:T(8,128)S(1)} %slice-done), kind=kOutput, calls=%fused_computation | convolution fusion | flops 3981312 | bytes 479664 | tf_op jit(solution)/shard_map/oczyx,iyh->ioxhcz/dot_general | solution.py:357
  25.4 1.1 %copy.39 = f32[4,32,3,9,16,2]{1,0,5,4,3,2:T(4,128)S(1)} copy(f32[4,32,3,9,16,2]{1,3,2,5,4,0:T(8,128)S(1)} %convolution_bitcast_fusion) | data formatting | bytes 884736 | tf_op jit(solution)/shard_map/oczyx,iyh->ioxhcz/transpose | solution.py:357
  26.6 0.0 copy-start.7
  26.6 0.0 copy-start.5
  26.6 0.0 copy-start.2
  26.6 0.7 reshape.54
  27.4 0.2 copy.41
  27.6 0.0 copy-done.7
  27.6 0.1 broadcast_in_dim.4
  27.7 0.1 tile.10
  27.8 0.1 tile.12
  27.9 0.1 copy.37
  28.1 0.0 copy-done.5
  28.1 0.0 copy-done.2
  28.1 1.0 %convolution_bitcast_fusion.1 = f32[9,16,2,3,2,16]{5,1,0,3,4,2:T(8,128)S(1)} fusion(f32[9,3,16,1,1,1]{2,1,0,5,4,3:T(4,128)S(1)} %copy-done.2, f32[16,1,2,3,3]{0,3,4,2,1:T(4,128)S(1)} %get-tuple-element.26, f32[16,1,2,3,3]{0,3,4,2,1:T(4,128)S(1)} %get-tuple-element.25), kind=kOutput, calls=%fused_computation.1 | convolution fusion | flops 995904 | bytes 114624 | tf_op jit(solution)/shard_map/czpyx,iys->iczxps/dot_general | solution.py:341
  29.1 0.5 copy.36
  29.6 0.0 copy-start.8
  29.6 0.6 reshape.53
  30.2 0.2 copy.40
  30.4 0.1 fusion.7
  30.5 18.4 %all-to-all-done.1.refs_2_ = f32[64,32,128]{2,1,0:T(8,128)S(1)} async-done(((f32[64,32,128]{2,1,0:T(8,128)}), f32[64,32,128]{2,1,0:T(8,128)S(1)}, u32[]{:S(2)}, u32[]{:S(2)}) %all-to-all-start.1) | async-done | bytes 1048608 | tf_op jit(solution)/shard_map/all_to_all | solution.py:373
  48.9 5.3 %join.1 = (f32[2,136,256]{2,1,0:T(8,128)S(1)}, f32[16,136]{1,0:T(8,128)S(1)}, f32[16,136]{1,0:T(8,128)S(1)}) custom-call(s32[64,8]{1,0:T(8,128)S(1)} %bitcast.37, s32[64,8]{1,0:T(8,128)S(1)} %bitcast.38, f32[64,32,128]{2,1,0:T(8,128)S(1)} %all-to-all-done.1.refs_2_), custom_call_target="tpu_custom_call" | custom-call | tf_op jit(solution)/shard_map/join/pallas_call | solution.py:204
  54.2 0.7 copy-done.1
  55.0 1.3 %collective-permute-start = (f32[16,136]{1,0:T(8,128)S(1)}, f32[16,136]{1,0:T(8,128)S(1)}, u32[]{:S(2)}, u32[]{:S(2)}) collective-permute-start(f32[16,136]{1,0:T(8,128)S(1)} %get-tuple-element.16), channel_id=1, source_target_pairs={{0,1},{1,2},{2,3},{4,5},{5,6},{6,7},{8,9},{9,10},{10,11},{12,13},{... | collective-permute-start | bytes 26120 | tf_op jit(solution)/shard_map/ppermute | solution.py:365
  56.3 1.3 %collective-permute-start.1 = (f32[16,136]{1,0:T(8,128)S(1)}, f32[16,136]{1,0:T(8,128)S(1)}, u32[]{:S(2)}, u32[]{:S(2)}) collective-permute-start(f32[16,136]{1,0:T(8,128)S(1)} %get-tuple-element.17), channel_id=1, source_target_pairs={{1,0},{2,1},{3,2},{5,4},{6,5},{7,6},{9,8},{10,9},{11,10},{13,12},{... | collective-permute-start | bytes 26120 | tf_op jit(solution)/shard_map/ppermute | solution.py:365
  57.6 0.2 fusion.1.first
  57.8 0.0 collective-permute-done.from_left
  57.8 0.0 copy-start.3
  57.8 3.3 %collective-permute-done.1.from_right = f32[16,136]{1,0:T(8,128)S(1)} collective-permute-done((f32[16,136]{1,0:T(8,128)S(1)}, f32[16,136]{1,0:T(8,128)S(1)}, u32[]{:S(2)}, u32[]{:S(2)}) %collective-permute-start.1) | collective-permute-done | bytes 8736 | tf_op jit(solution)/shard_map/ppermute | solution.py:365
  61.1 0.0 copy-done.3
  61.1 0.6 copy-done.4
  61.7 2.7 %phases.1 = (f32[5,2,136,128]{3,2,1,0:T(8,128)}, f32[5,2,8,128]{3,2,1,0:T(8,128)}, f32[5,2,8,128]{3,2,1,0:T(8,128)}) custom-call(f32[2,136,256]{2,1,0:T(8,128)} %copy-done.1, f32[16,136]{1,0:T(8,128)} %copy-done.3, f32[16,136]{1,0:T(8,128)} %copy-done.4), custom_call_target="tpu_custom_call" | custom-call | tf_op jit(solution)/shard_map/phases/pallas_call | solution.py:252
  64.4 3.4 %collective-permute-start.2 = (f32[5,2,8,128]{3,2,1,0:T(8,128)}, f32[5,2,8,128]{3,2,1,0:T(8,128)S(1)}, u32[]{:S(2)}, u32[]{:S(2)}) collective-permute-start(f32[5,2,8,128]{3,2,1,0:T(8,128)} %get-tuple-element.18), channel_id=1, source_target_pairs={{0,4},{4,8},{8,12},{12,16},{16,20},{20,24},{24,28},{1,5},{5,9},{9,... | collective-permute-start | bytes 122888 | tf_op jit(solution)/shard_map/ppermute | solution.py:365
  67.8 1.3 %collective-permute-start.3 = (f32[5,2,8,128]{3,2,1,0:T(8,128)}, f32[5,2,8,128]{3,2,1,0:T(8,128)S(1)}, u32[]{:S(2)}, u32[]{:S(2)}) collective-permute-start(f32[5,2,8,128]{3,2,1,0:T(8,128)} %get-tuple-element.19), channel_id=1, source_target_pairs={{4,0},{8,4},{12,8},{16,12},{20,16},{24,20},{28,24},{5,1},{9,5},{13... | collective-permute-start | bytes 122888 | tf_op jit(solution)/shard_map/ppermute | solution.py:365
  69.1 0.1 pad_add_fusion.edge
  69.1 0.6 collective-permute-done.2.from_above
  69.7 4.1 %collective-permute-done.3.from_below = f32[5,2,8,128]{3,2,1,0:T(8,128)S(1)} collective-permute-done((f32[5,2,8,128]{3,2,1,0:T(8,128)}, f32[5,2,8,128]{3,2,1,0:T(8,128)S(1)}, u32[]{:S(2)}, u32[]{:S(2)}) %collective-permute-start.3) | collective-permute-done | bytes 40992 | tf_op jit(solution)/shard_map/ppermute | solution.py:365
  73.9 0.0 copy-done.8
  73.9 0.1 broadcast_in_dim.10.bias
  73.9 1.1 %copy-done = f32[5,2,136,128]{3,2,1,0:T(8,128)S(1)} copy-done((f32[5,2,136,128]{3,2,1,0:T(8,128)S(1)}, f32[5,2,136,128]{3,2,1,0:T(8,128)}, u32[]{:S(2)}) %copy-start) | copy-done | bytes 696344
  75.0 10.0 %convolve.1 = f32[2048,128]{1,0:T(8,128)} custom-call(s32[2]{0:T(128)S(1)} %pad_add_fusion.edge, f32[5,2,8,128]{3,2,1,0:T(8,128)S(1)} %collective-permute-done.2.from_above, f32[5,2,8,128]{3,2,1,0:T(8,128)S(1)} %collective-permute-done.3.from_below, f32[5,2,136,128]{3,2,1,0:T(8,128)S(1)} %copy-done, bf16[288,304]{1,0:T(8,128)(2,1)S(1)} %fusion.1.first, ...), custom_call_target="tpu_custom_call" | custom-call | tf_op jit(solution)/shard_map/convolve/pallas_call | solution.py:319
  (12 shorter events, 0.1 us)
Async XLA Ops:
  0.0 22.7 %copy-start.6 = (f32[4,3,9,1,1,1]{2,1,5,4,3,0:T(4,128)S(1)}, f32[4,3,9,1,1,1]{2,1,5,4,3,0:T(4,128)}, u32[]{:S(2)}) copy-start(f32[4,3,9,1,1,1]{2,1,5,4,3,0:T(4,128)} %constant.21) | copy-start | bytes 1300
  0.0 22.7 %slice-start = ((f32[32,16,3,3,3]{0,1,4,3,2:T(8,128)}), f32[32,16,2,3,3]{0,1,4,3,2:T(8,128)S(1)}, s32[]{:S(2)}) async-start(f32[32,16,3,3,3]{0,1,4,3,2:T(8,128)} %param.12), calls=%async_computation.2 | async-start | bytes 294912 | tf_op jit(solution)/shard_map/slice | solution.py:357
  20.0 28.9 %all-to-all-start.1 = ((f32[64,32,128]{2,1,0:T(8,128)}), f32[64,32,128]{2,1,0:T(8,128)S(1)}, u32[]{:S(2)}, u32[]{:S(2)}) async-start(f32[64,32,128]{2,1,0:T(8,128)} %get-tuple-element.14), calls=%async_computation.1 | async-start | bytes 2097152 | tf_op jit(solution)/shard_map/all_to_all | solution.py:373
  26.6 1.0 %copy-start.7 = (f32[16]{0:T(128)S(1)}, f32[16]{0:T(128)}, u32[]{:S(2)}) copy-start(f32[16]{0:T(128)} %param.11) | copy-start | bytes 196
  26.6 1.5 %copy-start.5 = (f32[16,1,3,3,3]{0,1,4,3,2:T(1,128)S(1)}, f32[16,1,3,3,3]{0,1,4,3,2:T(1,128)}, u32[]{:S(2)}) copy-start(f32[16,1,3,3,3]{0,1,4,3,2:T(1,128)} %param.10) | copy-start | bytes 5188
  26.6 1.5 %copy-start.2 = (f32[9,3,16,1,1,1]{2,1,0,5,4,3:T(4,128)S(1)}, f32[9,3,16,1,1,1]{2,1,0,5,4,3:T(4,128)}, u32[]{:S(2)}) copy-start(f32[9,3,16,1,1,1]{2,1,0,5,4,3:T(4,128)} %constant.20) | copy-start | bytes 5188
  29.6 44.3 %copy-start.8 = (f32[32]{0:T(128)S(1)}, f32[32]{0:T(128)}, u32[]{:S(2)}) copy-start(f32[32]{0:T(128)} %param.13) | copy-start | bytes 388
  54.2 0.7 copy-start.1
  55.0 2.8 %collective-permute-start = (f32[16,136]{1,0:T(8,128)S(1)}, f32[16,136]{1,0:T(8,128)S(1)}, u32[]{:S(2)}, u32[]{:S(2)}) collective-permute-start(f32[16,136]{1,0:T(8,128)S(1)} %get-tuple-element.16), channel_id=1, source_target_pairs={{0,1},{1,2},{2,3},{4,5},{5,6},{6,7},{8,9},{9,10},{10,11},{12,13},{... | collective-permute-start | bytes 26120 | tf_op jit(solution)/shard_map/ppermute | solution.py:365
  56.3 4.8 %collective-permute-start.1 = (f32[16,136]{1,0:T(8,128)S(1)}, f32[16,136]{1,0:T(8,128)S(1)}, u32[]{:S(2)}, u32[]{:S(2)}) collective-permute-start(f32[16,136]{1,0:T(8,128)S(1)} %get-tuple-element.17), channel_id=1, source_target_pairs={{1,0},{2,1},{3,2},{5,4},{6,5},{7,6},{9,8},{10,9},{11,10},{13,12},{... | collective-permute-start | bytes 26120 | tf_op jit(solution)/shard_map/ppermute | solution.py:365
  57.8 3.3 %copy-start.3 = (f32[16,136]{1,0:T(8,128)}, f32[16,136]{1,0:T(8,128)S(1)}, u32[]{:S(2)}) copy-start(f32[16,136]{1,0:T(8,128)S(1)} %collective-permute-done.from_left) | copy-start | bytes 26116
  61.1 0.6 copy-start.4
  64.4 5.4 %collective-permute-start.2 = (f32[5,2,8,128]{3,2,1,0:T(8,128)}, f32[5,2,8,128]{3,2,1,0:T(8,128)S(1)}, u32[]{:S(2)}, u32[]{:S(2)}) collective-permute-start(f32[5,2,8,128]{3,2,1,0:T(8,128)} %get-tuple-element.18), channel_id=1, source_target_pairs={{0,4},{4,8},{8,12},{12,16},{16,20},{20,24},{24,28},{1,5},{5,9},{9,... | collective-permute-start | bytes 122888 | tf_op jit(solution)/shard_map/ppermute | solution.py:365
  67.8 6.1 %collective-permute-start.3 = (f32[5,2,8,128]{3,2,1,0:T(8,128)}, f32[5,2,8,128]{3,2,1,0:T(8,128)S(1)}, u32[]{:S(2)}, u32[]{:S(2)}) collective-permute-start(f32[5,2,8,128]{3,2,1,0:T(8,128)} %get-tuple-element.19), channel_id=1, source_target_pairs={{4,0},{8,4},{12,8},{16,12},{20,16},{24,20},{28,24},{5,1},{9,5},{13... | collective-permute-start | bytes 122888 | tf_op jit(solution)/shard_map/ppermute | solution.py:365
  73.9 1.1 %copy-start = (f32[5,2,136,128]{3,2,1,0:T(8,128)S(1)}, f32[5,2,136,128]{3,2,1,0:T(8,128)}, u32[]{:S(2)}) copy-start(f32[5,2,136,128]{3,2,1,0:T(8,128)} %get-tuple-element.20.phases_in) | copy-start | bytes 2088964

commit v2 on v1

v2 whole, which is shorter than its diff:
```python
import jax
import jax.numpy as jnp
import numpy as np
from jax import lax
from jax.experimental import pallas as pl
from jax.experimental.pallas import tpu as pltpu
from jax.sharding import PartitionSpec as P

BZ = 2
BY = 128
BX = 128
BLK = 2
STRIPS = 64
SY = 16
SX = 128
C1 = 16
C2 = 32

COLS = BX * BLK
HALF = COLS // 2
TOP = 2
SROW = 136
OUT_ROWS = 4
HID_ROWS = 9
WIN = 16
BLOCKS = BY // (2 * OUT_ROWS)
PHASES = 5
K1 = 3 * BZ * WIN
HID = HID_ROWS * C1 * BZ
K2 = 3 * HID
OUTM = OUT_ROWS * C2

EXACT = lax.Precision.HIGHEST
F32 = jnp.float32
BF16 = jnp.bfloat16


def iota(shape, dim):
    return lax.broadcasted_iota(jnp.int32, shape, dim)


def split_kernel(x):
    hi = x.astype(BF16)
    return hi, (x - hi.astype(F32)).astype(BF16)


def split_host(x):
    hi = lax.reduce_precision(x, 8, 7)
    return hi.astype(BF16), (x - hi).astype(BF16)


def chunk_of(per_pair):
    return BZ * SY // 2 * per_pair + 1


def pack_body(per_pair, routes, route_rows, strips, payload, count, sems):
    pairs = BZ * SY // 2
    chunk = chunk_of(per_pair)
    held = route_rows.shape[1]
    senders = payload.shape[0] // chunk
    full = held == STRIPS

    def clear(i, carry):
        count[i] = 0
        return carry

    lax.fori_loop(0, senders, clear, 0, unroll=8)

    def copy(k, at):
        source = strips.at[pl.ds(k * pairs, pairs)]
        return pltpu.make_async_copy(source, payload.at[pl.ds(at, pairs)], sems.at[0 if full else k])

    def when_live(k, run):
        if full:
            run()
        else:
            pl.when(routes[1, k] == 1)(run)

    def place(k, carry):
        def run():
            dest = routes[0, k]
            rank = jnp.minimum(count[dest], per_pair - 1)
            count[dest] = rank + 1
            copy(k, dest * chunk + rank * pairs).start()

        when_live(k, run)
        return carry

    lax.fori_loop(0, held, place, 0, unroll=8)

    match = (route_rows[0:1, :] == iota((senders, held), 0)) & (route_rows[1:2, :] == 1)
    flags = jnp.where(match, 1.0, 0.0)
    before = jnp.where(iota((held, held), 0) < iota((held, held), 1), 1.0, 0.0)
    earlier = jnp.dot(flags.astype(BF16), before.astype(BF16), preferred_element_type=F32)
    fields = jnp.concatenate([route_rows[...].astype(F32), jnp.zeros((120, held), F32)], axis=0)
    fields = fields.astype(BF16)
    for r in range(per_pair):
        chosen = jnp.where(match & (earlier == float(r)), 1.0, 0.0).astype(BF16)
        sent = lax.dot_general(
            chosen, fields, (((1,), (1,)), ((), ())), preferred_element_type=F32
        )
        for dest in range(senders):
            payload[dest * chunk + chunk - 1, r : r + 1, :] = sent[dest : dest + 1, :]

    if full:
        everything = held * pairs
        pltpu.make_async_copy(strips, payload.at[pl.ds(0, everything)], sems.at[0]).wait()
    else:

        def finish(k, carry):
            when_live(k, lambda: copy(k, 0).wait())
            return carry

        lax.fori_loop(0, held, finish, 0)


def pack(strips, routes_t, senders, per_pair):
    held = strips.shape[0]
    pairs = BZ * SY // 2
    vmem = pl.BlockSpec(memory_space=pltpu.VMEM)
    return pl.pallas_call(
        lambda *refs: pack_body(per_pair, *refs),
        in_specs=[
            pl.BlockSpec(memory_space=pltpu.SMEM),
            vmem,
            pl.BlockSpec(memory_space=pl.ANY),
        ],
        out_specs=vmem,
        out_shape=jax.ShapeDtypeStruct((senders * chunk_of(per_pair), 2, SX), F32),
        scratch_shapes=[
            pltpu.SMEM((senders,), jnp.int32),
            pltpu.SemaphoreType.DMA((1 if held == STRIPS else held,)),
        ],
        name="pack",
    )(routes_t, routes_t, strips.reshape(held * pairs, 2, SX))


def join_body(per_pair, grid, edge, routes, strips, joined, messages, data, place_y, params, sem):
    senders = routes.shape[0]
    slots = senders * per_pair
    chunk = 2 * chunk_of(per_pair)
    fetch = pltpu.make_async_copy(routes.at[:, chunk_of(per_pair) - 1], params, sem)
    fetch.start()
    fetch.wait()
    lane = iota((SY, SX), 1)
    sub = iota((SY, SX), 0)
    row_lane = iota((SY, 256), 1)
    row_sub = iota((SY, 256), 0)

    def one(h, r):
        k = h * per_pair + r
        live = params[h, r, 1].astype(jnp.int32)
        top = params[h, r, 2].astype(jnp.int32)
        left = params[h, r, 3].astype(jnp.int32)
        frac_z = params[h, r, 4] * (1.0 / 16.0)
        frac_y = params[h, r, 5] * (1.0 / 16.0)
        frac_x = params[h, r, 6] * (1.0 / 16.0)
        ramp = params[h, r, 7].astype(jnp.int32)
        weight = jnp.minimum(jnp.minimum(lane + 1, SX - lane), ramp).astype(F32)
        here = weight * (1.0 - frac_x)
        there = jnp.where(lane < SX - 1, weight * frac_x, 0.0)
        stay_z = 1.0 - frac_z
        move_z = frac_z
        at = h * chunk + r * BZ * SY
        first = strips[pl.ds(at, SY), :]
        second = strips[pl.ds(at + SY, SY), :]
        if slots != STRIPS:
            first = jnp.where(live == 1, first, 0.0)
            second = jnp.where(live == 1, second, 0.0)
        plane0 = stay_z * first + move_z * second
        plane1 = stay_z * second
        shift = left & (SX - 1)
        for z, plane in enumerate((plane0, plane1)):
            piece = here * plane + there * pltpu.roll(plane, SX - 1, 1)
            turned = pltpu.roll(piece, shift, 1)
            low = jnp.where(lane >= left, turned, 0.0)
            high = jnp.where(lane < left, turned, 0.0)
            for side, part in enumerate((low, high)):
                coarse, fine = split_kernel(part)
                at = z * COLS + side * SX
                data[pl.ds(k * SY, SY), at : at + SX] = coarse
                data[pl.ds(k * SY, SY), BZ * COLS + at : BZ * COLS + at + SX] = fine
        y = row_lane - TOP - top
        weight_y = jnp.minimum(jnp.minimum(y + 1, SY - y), ramp).astype(F32)
        spread = jnp.where(row_sub == y, weight_y * (1.0 - frac_y), 0.0) + jnp.where(
            row_sub == y + 1, weight_y * frac_y, 0.0
        )
        place_y[pl.ds(k * SY, SY), :] = spread.astype(BF16)

    def holder(h, carry):
        for r in range(per_pair):
            one(h, r)
        return carry

    lax.fori_loop(0, senders, holder, 0, unroll=4 // per_pair)

    columns = jnp.concatenate(
        [strips[pl.ds(chunk - 2 + r, senders, stride=chunk), :] for r in range(per_pair)], axis=0
    ).astype(jnp.int32)

    def field(q):
        return columns[:, q : q + 1]

    live = field(1)
    top = field(2)
    left = field(3)
    ramp = field(7)
    y = iota((slots, 256), 1) - TOP - top
    weight_y = jnp.where((y >= 0) & (y < SY), jnp.minimum(jnp.minimum(y + 1, SY - y), ramp), 0)
    col = iota((slots, COLS), 1)
    x = jnp.where(col < HALF, 2 * col, 2 * (col - HALF) + 1) - left
    weight_x = jnp.where((x >= 0) & (x < SX), jnp.minimum(jnp.minimum(x + 1, SX - x), ramp), 0)
    weight_y = jnp.where(live == 1, weight_y, 0).astype(F32).astype(BF16)
    weight_x = weight_x.astype(F32).astype(BF16)
    over_rows = (((0,), (0,)), ((), ()))
    total = lax.dot_general(weight_y, weight_x, over_rows, preferred_element_type=F32)[:SROW]
    sums = lax.dot_general(place_y[...], data[...], over_rows, preferred_element_type=F32)[:SROW]
    sums = sums[:, : BZ * COLS] + sums[:, BZ * COLS :]

    src = iota((COLS, COLS), 0)
    dst = iota((COLS, COLS), 1)
    order = (src == jnp.where(dst < HALF, 2 * dst, 2 * (dst - HALF) + 1)).astype(F32).astype(BF16)
    row = iota((SROW, COLS), 0)
    inside = (row >= TOP) & (row < TOP + BY)
    pick_row = iota((8, COLS), 0)
    pick_col = iota((8, COLS), 1)
    pick = jnp.where(
        ((pick_row == 0) & (pick_col == HALF - 1))
        | ((pick_row == 1) & (pick_col == COLS - 1))
        | ((pick_row == 2) & (pick_col == 0)),
        1.0,
        0.0,
    )
    right_rows = []
    left_rows = []
    down_rows = []
    up_rows = []
    for z in range(BZ):
        coarse, fine = split_kernel(sums[:, z * COLS : (z + 1) * COLS])
        ordered = jnp.dot(coarse, order, preferred_element_type=F32) + jnp.dot(
            fine, order, preferred_element_type=F32
        )
        value = jnp.where(inside, ordered / jnp.where(inside, total, 1.0), 0.0)
        joined[z] = value
        columns_as_rows = lax.dot_general(
            pick, value, (((1,), (1,)), ((), ())), precision=EXACT, preferred_element_type=F32
        )[:, TOP : TOP + BY]
        right_rows.append(columns_as_rows[0:2])
        left_rows.append(columns_as_rows[2:3])
        for half in range(2):
            cut = value[:, half * HALF : (half + 1) * HALF]
            down_rows.append(cut[BY : BY + 2])
            up_rows.append(cut[TOP : TOP + 1])

    def tile(rows):
        have = sum(r.shape[0] for r in rows)
        if have < 8:
            rows = rows + [jnp.zeros((8 - have, HALF), F32)]
        return jnp.concatenate(rows, axis=0)

    right = tile(right_rows)
    left = tile(left_rows)
    down = tile(down_rows)
    up = tile(up_rows)
    at_row = edge[0]
    at_col = edge[1]
    rows, cols = grid

    def send(dy, dx, values):
        to_row = at_row + dy
        to_col = at_col + dx

        @pl.when((to_row >= 0) & (to_row < rows) & (to_col >= 0) & (to_col < cols))
        def _():
            messages[to_row * cols + to_col] = values

    for dy in (-1, 0, 1):
        send(dy, 1, right)
        send(dy, -1, left)
    send(1, 0, down)
    send(-1, 0, up)


def join(grid, edge, arrived, per_pair):
    senders = arrived.shape[0] // chunk_of(per_pair)
    slots = senders * per_pair
    vmem = pl.BlockSpec(memory_space=pltpu.VMEM)
    return pl.pallas_call(
        lambda *refs: join_body(per_pair, grid, *refs),
        in_specs=[pl.BlockSpec(memory_space=pltpu.SMEM), pl.BlockSpec(memory_space=pl.ANY), vmem],
        out_specs=[vmem, vmem],
        out_shape=[
            jax.ShapeDtypeStruct((BZ, SROW, COLS), F32),
            jax.ShapeDtypeStruct((senders, 8, HALF), F32),
        ],
        scratch_shapes=[
            pltpu.VMEM((slots * SY, 2 * BZ * COLS), BF16),
            pltpu.VMEM((slots * SY, 256), BF16),
            pltpu.SMEM((senders, 2, SX), F32),
            pltpu.SemaphoreType.DMA,
        ],
        compiler_params=pltpu.CompilerParams(vmem_limit_bytes=48 * 2**20),
        name="join",
    )(
        edge,
        arrived.reshape(senders, chunk_of(per_pair), 2, SX),
        arrived.reshape(arrived.shape[0] * 2, SX),
    )


def conv_body(grid, edge, joined, received, first, second, bias, out, phases, coarse_h, fine_h):
    at_row = edge[0]
    at_col = edge[1]
    rows, cols = grid
    halo = {}
    for dy in (-1, 0, 1):
        for dx in (-1, 0, 1):
            if (dy, dx) == (0, 0):
                continue
            row = at_row + dy
            col = at_col + dx
            there = (row >= 0) & (row < rows) & (col >= 0) & (col < cols)
            index = jnp.where(there, row * cols + col, 0)
            halo[dy, dx] = jnp.where(there, received[index], 0.0)
    wide_lane = iota((8, 256), 1)

    def along(above, here, below):
        zero = jnp.zeros((8, 128), F32)
        turned = [
            pltpu.roll(jnp.concatenate([part, zero], axis=1), by, 1)
            for part, by in ((above, 256 - (BY - TOP)), (here, TOP), (below, TOP + BY))
        ]
        low = jnp.where(wide_lane < TOP, turned[0], turned[1])
        return jnp.where(
            wide_lane < TOP + BY, low, jnp.where(wide_lane == TOP + BY, turned[2], 0.0)
        )

    from_left = along(halo[-1, -1], halo[0, -1], halo[1, -1])
    from_right = along(halo[-1, 1], halo[0, 1], halo[1, 1])
    from_above = halo[-1, 0]
    from_below = halo[1, 0]
    pick_row = iota((8, HALF), 0)
    pick_lane = iota((8, HALF), 1)
    tall_lane = iota((SROW, HALF), 1)
    row8 = iota((8, HALF), 0)

    def column(message, row, lane_at):
        chosen = jnp.where((pick_row == row) & (pick_lane == lane_at), 1.0, 0.0)
        return lax.dot_general(
            message, chosen, (((0,), (0,)), ((), ())), precision=EXACT, preferred_element_type=F32
        )[:SROW]

    for z in range(BZ):
        halves = []
        for half in range(2):
            own = joined[z, :, half * HALF : (half + 1) * HALF]
            at = 4 * z + 2 * half
            above = jnp.concatenate([from_above[at : at + 2], own[2:8]], axis=0)
            at = 2 * z + half
            below = jnp.concatenate(
                [own[SROW - 8 : SROW - 6], from_below[at : at + 1], jnp.zeros((5, HALF), F32)], axis=0
            )
            halves.append(jnp.concatenate([above, own[8 : SROW - 8], below], axis=0))
        even, odd = halves
        phases[0, z] = jnp.where(tall_lane == 0, column(from_left, 2 * z, 0), pltpu.roll(even, 1, 1))
        phases[1, z] = jnp.where(tall_lane == 0, column(from_left, 2 * z + 1, 0), pltpu.roll(odd, 1, 1))
        phases[2, z] = even
        phases[3, z] = odd
        phases[4, z] = jnp.where(
            tall_lane == HALF - 1, column(from_right, z, HALF - 1), pltpu.roll(even, HALF - 1, 1)
        )
    no_row = edge[0] == 0
    no_col = edge[1] == 0
    lane = iota((HID, 256), 1)
    hid_row = iota((HID, 256), 0)
    ones = jnp.ones((16, 256), BF16)

    def pair(step, carry):
        blocks = (step, step + BLOCKS // 2)
        wide = {}
        for j in range(PHASES):
            for z in range(BZ):
                cut = [
                    phases[j, z, pl.ds(pl.multiple_of(8 * b, 8), WIN), :] for b in blocks
                ]
                wide[j, z] = split_kernel(jnp.concatenate(cut, axis=1))
        for group in range(3):
            coarse = [wide[group + dx, z][0] for dx in range(3) for z in range(BZ)]
            fine = [wide[group + dx, z][1] for dx in range(3) for z in range(BZ)]
            stacked = jnp.concatenate(coarse + fine + coarse + [ones], axis=0)
            hidden = jnp.dot(first[...], stacked, preferred_element_type=F32)
            hidden = jnp.maximum(hidden, 0.0)
            outside = no_row & (step == 0) & (hid_row < C1 * BZ) & (lane < HALF)
            if group == 0:
                outside = outside | (no_col & ((lane & (HALF - 1)) == 0))
            hidden = jnp.where(outside, 0.0, hidden)
            coarse, fine = split_kernel(hidden)
            coarse_h[group * HID : (group + 1) * HID, :] = coarse
            fine_h[group * HID : (group + 1) * HID, :] = fine
        both = jnp.dot(second[...], coarse_h[...], preferred_element_type=F32)
        rest = jnp.dot(second[:OUTM, :], fine_h[...], preferred_element_type=F32)
        result = both[:OUTM] + both[OUTM:] + rest
        for side, b in enumerate(blocks):
            for r in range(OUT_ROWS):
                at = OUT_ROWS * b + r
                out[pl.ds(at, C2, stride=BY // 2), :] = (
                    result[r * C2 : (r + 1) * C2, side * HALF : (side + 1) * HALF] + bias[...]
                )
        return carry

    lax.fori_loop(0, BLOCKS // 2, pair, 0)


def convolve(grid, edge, joined, received, first, second, bias):
    vmem = pl.BlockSpec(memory_space=pltpu.VMEM)
    return pl.pallas_call(
        lambda *refs: conv_body(grid, *refs),
        in_specs=[pl.BlockSpec(memory_space=pltpu.SMEM)] + [vmem] * 5,
        out_specs=vmem,
        out_shape=jax.ShapeDtypeStruct((C2 * BY // 2, HALF), F32),
        scratch_shapes=[
            pltpu.VMEM((PHASES, BZ, SROW, HALF), F32),
            pltpu.VMEM((K2, 256), BF16),
            pltpu.VMEM((K2, 256), BF16),
        ],
        compiler_params=pltpu.CompilerParams(vmem_limit_bytes=48 * 2**20),
        name="convolve",
    )(edge, joined, received, first, second, bias)


def first_table(weight, bias):
    kernel = weight[:, 0]
    planes = jnp.stack([kernel[:, 1:3], kernel[:, 0:2]], axis=1)
    reach = np.zeros((HID_ROWS, 3, WIN), np.float32)
    for i in range(HID_ROWS):
        for dy in range(3):
            reach[i, dy, i + dy] = 1.0
    table = jnp.einsum("czpyx,iys->iczxps", planes, jnp.asarray(reach), precision=EXACT)
    coarse, fine = split_host(table.reshape(HID, K1))
    each = jnp.tile(jnp.repeat(bias, BZ), HID_ROWS)
    one = lax.reduce_precision(each, 8, 7)
    two = lax.reduce_precision(each - one, 8, 7)
    three = each - one - two
    tail = jnp.stack([one, two, three], axis=1).astype(BF16)
    tail = jnp.pad(tail, ((0, 0), (0, 16 - 3)))
    return jnp.concatenate([coarse, coarse, fine, tail], axis=1)


def second_table(weight):
    reach = np.zeros((OUT_ROWS, 3, HID_ROWS), np.float32)
    for i in range(OUT_ROWS):
        for dy in range(3):
            reach[i, dy, 2 * i + dy] = 1.0
    table = jnp.einsum("oczyx,iyh->ioxhcz", weight[:, :, 1:3], jnp.asarray(reach), precision=EXACT)
    coarse, fine = split_host(table.reshape(OUTM, K2))
    return jnp.concatenate([coarse, fine], axis=0)


def body(strips, routes, conv1_weight, conv1_bias, conv2_weight, conv2_bias):
    rows = lax.axis_size("gx")
    cols = lax.axis_size("gy")
    senders = rows * cols
    per_pair = max(1, STRIPS // senders)
    axes = ("gx", "gy")
    at_row = lax.axis_index("gx").astype(jnp.int32)
    at_col = lax.axis_index("gy").astype(jnp.int32)
    edge = jnp.stack([at_row, at_col])
    routes_t = routes.T
    outgoing = pack(strips, routes_t, senders, per_pair)
    arrived = lax.all_to_all(outgoing, axes, split_axis=0, concat_axis=0, tiled=True)
    first = first_table(conv1_weight, conv1_bias)
    second = second_table(conv2_weight)
    bias = jnp.broadcast_to(conv2_bias[:, None], (C2, HALF))
    joined, messages = join((rows, cols), edge, arrived, per_pair)
    received = lax.all_to_all(messages, axes, split_axis=0, concat_axis=0, tiled=True)
    features = convolve((rows, cols), edge, joined, received, first, second, bias)
    return features.reshape(C2, 1, BY // 2, HALF)


def solution(mesh):
    in_specs = (P(("gx", "gy"), None, None, None), P(("gx", "gy"), None), P(), P(), P(), P())
    out_specs = P(None, None, "gx", "gy")
    return jax.shard_map(body, mesh=mesh, in_specs=in_specs, out_specs=out_specs, check_vma=False)
```

time: 86 us -> 67.4 us (0.78)
  blocking collectives: 14.6 us -> 0 us
  local copies, waits for them, and re-layouts: 7.65 us -> 3.8 us
  Pallas kernels: 22 us -> 20.7 us
  starting transfers between devices: 9.9 us -> 11.1 us
    all_to_all x1 -> x0, blocking collectives: 14.6 us -> none  [body(): lax.all_to_all(outgoing_params, axes, split_axis=0, concat_axis=0, tiled=...]
    ppermute x4 -> x0, waiting for transfers between devices: 8.02 us -> none  [shift(): return lax.ppermute(values, axis, pairs)]
    all_to_all x0 -> x1, waiting for transfers between devices: none -> 7.83 us  [body(): lax.all_to_all(messages, axes, split_axis=0, concat_axis=0, tiled=True)]
    ppermute x4 -> x0, starting transfers between devices: 7.26 us -> none  [shift(): return lax.ppermute(values, axis, pairs)]
    all_to_all x1, starting transfers between devices: 2.65 us -> 7.3 us  [body(): lax.all_to_all(outgoing, axes, split_axis=0, concat_axis=0, tiled=True)]
    unnamed x20 -> x13, local copies, waits for them, and re-layouts: 3.89 us -> 0.04 us
    all_to_all x0 -> x1, starting transfers between devices: none -> 3.76 us  [body(): lax.all_to_all(messages, axes, split_axis=0, concat_axis=0, tiled=True)]
    pallas_call x4 -> x3, Pallas kernels: 22 us -> 20.7 us  [the longest x1 10.8 us: convolve(): pl.pallas_call(lambda *refs: conv_body(grid, *refs), in_specs=[pl.BlockSp...]
  transfers between devices with their start and end apart: 5 -> 2, of which waited for: 4 -> 2; matrix products, arithmetic and copies ran while one was open for 9% -> 13% of each run, Pallas kernels for 0% -> 0%
where the time goes in v2:
time: 67.4 us; the launch traced here: 67 us
  waiting for transfers between devices  26.3 us (39%)
  Pallas kernels  20.7 us (31%)
  starting transfers between devices  11.1 us (16%)
  local copies, waits for them, and re-layouts  3.8 us (6%)
  matrix products  3.73 us (6%)
  other arithmetic  1.2 us (2%)
    all_to_all x1, waiting for transfers between devices, body(): lax.all_to_all(outgoing, axes, split_axis=0, concat_axis=0, tiled=True)  18.5 us
    pallas_call x1, Pallas kernels, convolve(): pl.pallas_call(lambda *refs: conv_body(grid, *refs), in_specs=[pl.BlockSp...  10.8 us
    all_to_all x1, waiting for transfers between devices, body(): lax.all_to_all(messages, axes, split_axis=0, concat_axis=0, tiled=True)  7.83 us
    all_to_all x1, starting transfers between devices, body(): lax.all_to_all(outgoing, axes, split_axis=0, concat_axis=0, tiled=True)  7.3 us
    pallas_call x1, Pallas kernels, join(): pl.pallas_call(lambda *refs: join_body(per_pair, grid, *refs), in_specs=[...  6.7 us
    all_to_all x1, starting transfers between devices, body(): lax.all_to_all(messages, axes, split_axis=0, concat_axis=0, tiled=True)  3.76 us
    pallas_call x1, Pallas kernels, pack(): pl.pallas_call(lambda *refs: pack_body(per_pair, *refs), in_specs=[pl.Blo...  3.15 us
    dot_general x1, matrix products, second_table(): jnp.einsum('oczyx,iyh->ioxhcz', weight[:, :, 1:3], jnp.asarray(reach), pr...  2.71 us
  transfers between devices with their start and end apart: 2, of which 2 were waited for; matrix products, arithmetic and copies ran while one was open for 13% of the time, Pallas kernels for 0%

profile of v2, /device:TPU:0, one launch (start us, length us, event | category | flops | bytes accessed | tf_op | source)
XLA Modules:
  0.0 67.0 jit_solution(11709371675448460702)
XLA Ops:
  0.0 0.0 slice-start
  0.0 0.0 copy-start.3
  0.0 3.1 %pack.1 = f32[1056,2,128]{2,1,0:T(2,128)} custom-call(s32[8,64]{1,0:T(8,128)} %bitcast.42, s32[8,64]{1,0:T(8,128)} %bitcast.43, f32[1024,2,128]{2,1,0:T(2,128)} %bitcast.40), custom_call_target="tpu_custom_call" | custom-call | tf_op jit(solution)/shard_map/pack/pallas_call | solution.py:121
  3.2 7.3 %all-to-all-start = ((f32[1056,2,128]{2,1,0:T(2,128)}), f32[1056,2,128]{2,1,0:T(2,128)S(1)}, u32[]{:S(2)}, u32[]{:S(2)}) async-start(f32[1056,2,128]{2,1,0:T(2,128)} %pack.1), calls=%async_computation | async-start | bytes 2162688 | tf_op jit(solution)/shard_map/all_to_all | solution.py:470
  10.5 0.0 slice-done
  10.5 0.0 copy-done.3
  10.5 2.7 %convolution_bitcast_fusion = f32[4,32,3,9,16,2]{1,3,2,5,4,0:T(8,128)S(1)} fusion(f32[4,3,9,1,1,1]{2,1,5,4,3,0:T(4,128)S(1)} %copy-done.3, f32[32,16,2,3,3]{0,1,4,3,2:T(8,128)S(1)} %slice-done), kind=kOutput, calls=%fused_computation | convolution fusion | flops 3981312 | bytes 479664 | tf_op jit(solution)/shard_map/oczyx,iyh->ioxhcz/dot_general | solution.py:454
  13.2 1.1 %copy.35 = f32[4,32,3,9,16,2]{1,0,5,4,3,2:T(4,128)S(1)} copy(f32[4,32,3,9,16,2]{1,3,2,5,4,0:T(8,128)S(1)} %convolution_bitcast_fusion) | data formatting | bytes 884736 | tf_op jit(solution)/shard_map/oczyx,iyh->ioxhcz/transpose | solution.py:454
  14.4 0.0 copy-start.4
  14.4 0.0 copy-start.2
  14.4 0.0 copy-start.1
  14.4 0.7 %reshape.60 = f32[128,864]{0,1:T(8,128)S(1)} reshape(f32[4,32,3,9,16,2]{1,0,5,4,3,2:T(4,128)S(1)} %copy.35) | data formatting | bytes 884736 | tf_op jit(solution)/shard_map/reshape | solution.py:455
  15.1 0.8 %reduce_precision.41 = f32[128,864]{0,1:T(8,128)} reduce-precision(f32[128,864]{0,1:T(8,128)S(1)} %reshape.60), exponent_bits=8, mantissa_bits=7 | non-fusion elementwise | flops 110592 | bytes 884736 | tf_op jit(solution)/shard_map/reduce_precision | solution.py:48
  15.9 0.2 copy.37
  16.1 0.0 copy-done.4
  16.2 0.1 broadcast_in_dim.4
  16.2 0.1 tile.10
  16.3 0.1 tile.12
  16.4 0.0 copy-done.2
  16.4 0.0 copy-done.1
  16.4 0.0 copy-start
  16.4 1.0 %convolution_bitcast_fusion.1 = f32[9,16,2,3,2,16]{5,1,0,3,4,2:T(8,128)S(1)} fusion(f32[9,3,16,1,1,1]{2,1,0,5,4,3:T(4,128)S(1)} %copy-done.1, f32[16,1,2,3,3]{0,3,4,2,1:T(4,128)S(1)} %get-tuple-element.14, f32[16,1,2,3,3]{0,3,4,2,1:T(4,128)S(1)} %get-tuple-element.13), kind=kOutput, calls=%fused_computation.1 | convolution fusion | flops 995904 | bytes 114624 | tf_op jit(solution)/shard_map/czpyx,iys->iczxps/dot_general | solution.py:438
  17.5 0.5 copy.32
  17.9 0.6 reshape.59
  18.5 0.0 copy-done
  18.5 0.2 copy.36
  18.7 0.1 pad_add_fusion.refs_0_
  18.8 0.1 fusion.7
  18.9 18.5 %all-to-all-done = f32[1056,2,128]{2,1,0:T(2,128)S(1)} async-done(((f32[1056,2,128]{2,1,0:T(2,128)}), f32[1056,2,128]{2,1,0:T(2,128)S(1)}, u32[]{:S(2)}, u32[]{:S(2)}) %all-to-all-start) | async-done | bytes 1081376 | tf_op jit(solution)/shard_map/all_to_all | solution.py:470
  37.4 0.0 copy-start.5
  37.4 6.7 %join.1 = (f32[2,136,256]{2,1,0:T(8,128)S(1)}, f32[32,8,128]{2,1,0:T(8,128)}) custom-call(s32[2]{0:T(128)S(1)} %pad_add_fusion.refs_0_, f32[32,33,2,128]{3,2,1,0:T(2,128)S(1)} %bitcast.38, f32[2112,128]{1,0:T(8,128)S(1)} %bitcast.39), custom_call_target="tpu_custom_call" | custom-call | tf_op jit(solution)/shard_map/join/pallas_call | solution.py:288
  44.1 3.8 %all-to-all-start.1 = ((f32[32,8,128]{2,1,0:T(8,128)}), f32[32,8,128]{2,1,0:T(8,128)S(1)}, u32[]{:S(2)}, u32[]{:S(2)}) async-start(f32[32,8,128]{2,1,0:T(8,128)} %get-tuple-element.8), calls=%async_computation.1 | async-start | bytes 262144 | tf_op jit(solution)/shard_map/all_to_all | solution.py:475
  47.9 0.1 copy.33
  48.1 0.2 fusion.1.refs_3_
  48.3 7.8 %all-to-all-done.1.refs_2_ = f32[32,8,128]{2,1,0:T(8,128)S(1)} async-done(((f32[32,8,128]{2,1,0:T(8,128)}), f32[32,8,128]{2,1,0:T(8,128)S(1)}, u32[]{:S(2)}, u32[]{:S(2)}) %all-to-all-start.1) | async-done | bytes 131104 | tf_op jit(solution)/shard_map/all_to_all | solution.py:475
  56.1 0.0 copy-done.5
  56.1 0.1 broadcast_in_dim.10.refs_5_
  56.2 10.8 %convolve.1 = f32[2048,128]{1,0:T(8,128)} custom-call(s32[2]{0:T(128)S(1)} %pad_add_fusion.refs_0_, f32[2,136,256]{2,1,0:T(8,128)S(1)} %get-tuple-element.7.refs_1_, f32[32,8,128]{2,1,0:T(8,128)S(1)} %all-to-all-done.1.refs_2_, bf16[288,304]{1,0:T(8,128)(2,1)S(1)} %fusion.1.refs_3_, bf16[256,864]{1,0:T(8,128)(2,1)S(1)} %pad_maximum_fusion.refs_4_, ...), custom_call_target="tpu_custom_call" | custom-call | tf_op jit(solution)/shard_map/convolve/pallas_call | solution.py:416
  (7 shorter events, 0.1 us)
Async XLA Ops:
  0.0 10.5 %slice-start = ((f32[32,16,3,3,3]{0,1,4,3,2:T(8,128)}), f32[32,16,2,3,3]{0,1,4,3,2:T(8,128)S(1)}, s32[]{:S(2)}) async-start(f32[32,16,3,3,3]{0,1,4,3,2:T(8,128)} %param.12), calls=%async_computation.2 | async-start | bytes 294912 | tf_op jit(solution)/shard_map/slice | solution.py:454
  0.0 10.5 %copy-start.3 = (f32[4,3,9,1,1,1]{2,1,5,4,3,0:T(4,128)S(1)}, f32[4,3,9,1,1,1]{2,1,5,4,3,0:T(4,128)}, u32[]{:S(2)}) copy-start(f32[4,3,9,1,1,1]{2,1,5,4,3,0:T(4,128)} %constant.21) | copy-start | bytes 1300
  3.2 34.2 %all-to-all-start = ((f32[1056,2,128]{2,1,0:T(2,128)}), f32[1056,2,128]{2,1,0:T(2,128)S(1)}, u32[]{:S(2)}, u32[]{:S(2)}) async-start(f32[1056,2,128]{2,1,0:T(2,128)} %pack.1), calls=%async_computation | async-start | bytes 2162688 | tf_op jit(solution)/shard_map/all_to_all | solution.py:470
  14.4 1.8 %copy-start.4 = (f32[16]{0:T(128)S(1)}, f32[16]{0:T(128)}, u32[]{:S(2)}) copy-start(f32[16]{0:T(128)} %param.11) | copy-start | bytes 196
  14.4 2.0 %copy-start.2 = (f32[16,1,3,3,3]{0,1,4,3,2:T(1,128)S(1)}, f32[16,1,3,3,3]{0,1,4,3,2:T(1,128)}, u32[]{:S(2)}) copy-start(f32[16,1,3,3,3]{0,1,4,3,2:T(1,128)} %param.10) | copy-start | bytes 5188
  14.4 2.0 %copy-start.1 = (f32[9,3,16,1,1,1]{2,1,0,5,4,3:T(4,128)S(1)}, f32[9,3,16,1,1,1]{2,1,0,5,4,3:T(4,128)}, u32[]{:S(2)}) copy-start(f32[9,3,16,1,1,1]{2,1,0,5,4,3:T(4,128)} %constant.20) | copy-start | bytes 5188
  16.4 2.1 %copy-start = (f32[128,864]{0,1:T(8,128)S(1)}, f32[128,864]{0,1:T(8,128)}, u32[]{:S(2)}) copy-start(f32[128,864]{0,1:T(8,128)} %reduce_precision.41) | copy-start | bytes 1327108
  37.4 18.7 %copy-start.5 = (f32[32]{0:T(128)S(1)}, f32[32]{0:T(128)}, u32[]{:S(2)}) copy-start(f32[32]{0:T(128)} %param.13) | copy-start | bytes 388
  44.1 12.0 %all-to-all-start.1 = ((f32[32,8,128]{2,1,0:T(8,128)}), f32[32,8,128]{2,1,0:T(8,128)S(1)}, u32[]{:S(2)}, u32[]{:S(2)}) async-start(f32[32,8,128]{2,1,0:T(8,128)} %get-tuple-element.8), calls=%async_computation.1 | async-start | bytes 262144 | tf_op jit(solution)/shard_map/all_to_all | solution.py:475

commit v3 on v2

--- a/solution.py
+++ b/solution.py
@@ -25,6 +25,8 @@
 WIN = 16
 BLOCKS = BY // (2 * OUT_ROWS)
 PHASES = 5
+UNROLL = 8
+JOIN_UNROLL = 8
 K1 = 3 * BZ * WIN
 HID = HID_ROWS * C1 * BZ
 K2 = 3 * HID
@@ -141,9 +143,28 @@
     chunk = 2 * chunk_of(per_pair)
     fetch = pltpu.make_async_copy(routes.at[:, chunk_of(per_pair) - 1], params, sem)
     fetch.start()
+    columns = jnp.concatenate(
+        [strips[pl.ds(chunk - 2 + r, senders, stride=chunk), :] for r in range(per_pair)], axis=0
+    ).astype(jnp.int32)
+
+    def field(q):
+        return columns[:, q : q + 1]
+
+    live = field(1)
+    top = field(2)
+    left = field(3)
+    ramp = field(7)
+    y = iota((slots, 256), 1) - TOP - top
+    weight_y = jnp.where((y >= 0) & (y < SY), jnp.minimum(jnp.minimum(y + 1, SY - y), ramp), 0)
+    col = iota((slots, COLS), 1)
+    x = jnp.where(col < HALF, 2 * col, 2 * (col - HALF) + 1) - left
+    weight_x = jnp.where((x >= 0) & (x < SX), jnp.minimum(jnp.minimum(x + 1, SX - x), ramp), 0)
+    weight_y = jnp.where(live == 1, weight_y, 0).astype(F32).astype(BF16)
+    weight_x = weight_x.astype(F32).astype(BF16)
+    over_rows = (((0,), (0,)), ((), ()))
+    total = lax.dot_general(weight_y, weight_x, over_rows, preferred_element_type=F32)[:SROW]
     fetch.wait()
     lane = iota((SY, SX), 1)
-    sub = iota((SY, SX), 0)
     row_lane = iota((SY, 256), 1)
     row_sub = iota((SY, 256), 0)
 
@@ -192,28 +213,8 @@
             one(h, r)
         return carry
 
-    lax.fori_loop(0, senders, holder, 0, unroll=4 // per_pair)
-
-    columns = jnp.concatenate(
-        [strips[pl.ds(chunk - 2 + r, senders, stride=chunk), :] for r in range(per_pair)], axis=0
-    ).astype(jnp.int32)
-
-    def field(q):
-        return columns[:, q : q + 1]
-
-    live = field(1)
-    top = field(2)
-    left = field(3)
-    ramp = field(7)
-    y = iota((slots, 256), 1) - TOP - top
-    weight_y = jnp.where((y >= 0) & (y < SY), jnp.minimum(jnp.minimum(y + 1, SY - y), ramp), 0)
-    col = iota((slots, COLS), 1)
-    x = jnp.where(col < HALF, 2 * col, 2 * (col - HALF) + 1) - left
-    weight_x = jnp.where((x >= 0) & (x < SX), jnp.minimum(jnp.minimum(x + 1, SX - x), ramp), 0)
-    weight_y = jnp.where(live == 1, weight_y, 0).astype(F32).astype(BF16)
-    weight_x = weight_x.astype(F32).astype(BF16)
-    over_rows = (((0,), (0,)), ((), ()))
-    total = lax.dot_general(weight_y, weight_x, over_rows, preferred_element_type=F32)[:SROW]
+    lax.fori_loop(0, senders, holder, 0, unroll=JOIN_UNROLL)
+
     sums = lax.dot_general(place_y[...], data[...], over_rows, preferred_element_type=F32)[:SROW]
     sums = sums[:, : BZ * COLS] + sums[:, BZ * COLS :]
 
@@ -371,11 +372,11 @@
         )
     no_row = edge[0] == 0
     no_col = edge[1] == 0
-    lane = iota((HID, 256), 1)
-    hid_row = iota((HID, 256), 0)
+    keep = jnp.where(no_col & ((iota((1, 256), 1) & (HALF - 1)) == 0), 0.0, 1.0)
     ones = jnp.ones((16, 256), BF16)
 
-    def pair(step, carry):
+    def pair(step, part):
+        slot = part % 2
         blocks = (step, step + BLOCKS // 2)
         wide = {}
         for j in range(PHASES):
@@ -390,15 +391,23 @@
             stacked = jnp.concatenate(coarse + fine + coarse + [ones], axis=0)
             hidden = jnp.dot(first[...], stacked, preferred_element_type=F32)
             hidden = jnp.maximum(hidden, 0.0)
-            outside = no_row & (step == 0) & (hid_row < C1 * BZ) & (lane < HALF)
             if group == 0:
-                outside = outside | (no_col & ((lane & (HALF - 1)) == 0))
-            hidden = jnp.where(outside, 0.0, hidden)
+                hidden = hidden * keep
             coarse, fine = split_kernel(hidden)
-            coarse_h[group * HID : (group + 1) * HID, :] = coarse
-            fine_h[group * HID : (group + 1) * HID, :] = fine
-        both = jnp.dot(second[...], coarse_h[...], preferred_element_type=F32)
-        rest = jnp.dot(second[:OUTM, :], fine_h[...], preferred_element_type=F32)
+            coarse_h[slot, group * HID : (group + 1) * HID, :] = coarse
+            fine_h[slot, group * HID : (group + 1) * HID, :] = fine
+
+        if part == 0:
+
+            @pl.when(no_row & (step == 0))
+            def _():
+                for group in range(3):
+                    for scratch in (coarse_h, fine_h):
+                        nothing = jnp.zeros((C1 * BZ, HALF), BF16)
+                        scratch[slot, group * HID : group * HID + C1 * BZ, :HALF] = nothing
+
+        both = jnp.dot(second[...], coarse_h[slot], preferred_element_type=F32)
+        rest = jnp.dot(second[:OUTM, :], fine_h[slot], preferred_element_type=F32)
         result = both[:OUTM] + both[OUTM:] + rest
         for side, b in enumerate(blocks):
             for r in range(OUT_ROWS):
@@ -406,9 +415,13 @@
                 out[pl.ds(at, C2, stride=BY // 2), :] = (
                     result[r * C2 : (r + 1) * C2, side * HALF : (side + 1) * HALF] + bias[...]
                 )
+
+    def steps(i, carry):
+        for part in range(UNROLL):
+            pair(UNROLL * i + part, part)
         return carry
 
-    lax.fori_loop(0, BLOCKS // 2, pair, 0)
+    lax.fori_loop(0, BLOCKS // 2 // UNROLL, steps, 0)
 
 
 def convolve(grid, edge, joined, received, first, second, bias):
@@ -420,8 +433,8 @@
         out_shape=jax.ShapeDtypeStruct((C2 * BY // 2, HALF), F32),
         scratch_shapes=[
             pltpu.VMEM((PHASES, BZ, SROW, HALF), F32),
-            pltpu.VMEM((K2, 256), BF16),
-            pltpu.VMEM((K2, 256), BF16),
+            pltpu.VMEM((2, K2, 256), BF16),
+            pltpu.VMEM((2, K2, 256), BF16),
         ],
         compiler_params=pltpu.CompilerParams(vmem_limit_bytes=48 * 2**20),
         name="convolve",

time: 67.4 us -> 62.9 us (0.933)
  Pallas kernels: 20.7 us -> 16.2 us
    pallas_call x1, Pallas kernels: 10.8 us -> 8.12 us  [convolve(): pl.pallas_call(lambda *refs: conv_body(grid, *refs), in_specs=[pl.BlockSp...]
    pallas_call x1, Pallas kernels: 6.7 us -> 4.95 us  [join(): pl.pallas_call(lambda *refs: join_body(per_pair, grid, *refs), in_specs=[...]
  transfers between devices with their start and end apart: 2 -> 2, of which waited for: 2 -> 2; matrix products, arithmetic and copies ran while one was open for 13% -> 14% of each run, Pallas kernels for 0% -> 0%
where the time goes in v3:
time: 62.9 us; the launch traced here: 62.6 us
  waiting for transfers between devices  26.3 us (42%)
  Pallas kernels  16.2 us (26%)
  starting transfers between devices  11.1 us (18%)
  local copies, waits for them, and re-layouts  3.8 us (6%)
  matrix products  3.73 us (6%)
  other arithmetic  1.2 us (2%)
    all_to_all x1, waiting for transfers between devices, body(): lax.all_to_all(outgoing, axes, split_axis=0, concat_axis=0, tiled=True)  18.5 us
    pallas_call x1, Pallas kernels, convolve(): pl.pallas_call(lambda *refs: conv_body(grid, *refs), in_specs=[pl.BlockSp...  8.12 us
    all_to_all x1, waiting for transfers between devices, body(): lax.all_to_all(messages, axes, split_axis=0, concat_axis=0, tiled=True)  7.83 us
    all_to_all x1, starting transfers between devices, body(): lax.all_to_all(outgoing, axes, split_axis=0, concat_axis=0, tiled=True)  7.3 us
    pallas_call x1, Pallas kernels, join(): pl.pallas_call(lambda *refs: join_body(per_pair, grid, *refs), in_specs=[...  4.95 us
    all_to_all x1, starting transfers between devices, body(): lax.all_to_all(messages, axes, split_axis=0, concat_axis=0, tiled=True)  3.77 us
    pallas_call x1, Pallas kernels, pack(): pl.pallas_call(lambda *refs: pack_body(per_pair, *refs), in_specs=[pl.Blo...  3.15 us
    dot_general x1, matrix products, second_table(): jnp.einsum('oczyx,iyh->ioxhcz', weight[:, :, 1:3], jnp.asarray(reach), pr...  2.71 us
  transfers between devices with their start and end apart: 2, of which 2 were waited for; matrix products, arithmetic and copies ran while one was open for 14% of the time, Pallas kernels for 0%

profile of v3, /device:TPU:0, one launch (start us, length us, event | category | flops | bytes accessed | tf_op | source)
XLA Modules:
  0.0 62.6 jit_solution(10175639816785847060)
XLA Ops:
  0.0 0.0 slice-start
  0.0 0.0 copy-start.3
  0.0 3.1 %pack.1 = f32[1056,2,128]{2,1,0:T(2,128)} custom-call(s32[8,64]{1,0:T(8,128)} %bitcast.42, s32[8,64]{1,0:T(8,128)} %bitcast.43, f32[1024,2,128]{2,1,0:T(2,128)} %bitcast.40), custom_call_target="tpu_custom_call" | custom-call | tf_op jit(solution)/shard_map/pack/pallas_call | solution.py:123
  3.2 7.3 %all-to-all-start = ((f32[1056,2,128]{2,1,0:T(2,128)}), f32[1056,2,128]{2,1,0:T(2,128)S(1)}, u32[]{:S(2)}, u32[]{:S(2)}) async-start(f32[1056,2,128]{2,1,0:T(2,128)} %pack.1), calls=%async_computation | async-start | bytes 2162688 | tf_op jit(solution)/shard_map/all_to_all | solution.py:483
  10.5 0.0 slice-done
  10.5 0.0 copy-done.3
  10.5 2.7 %convolution_bitcast_fusion = f32[4,32,3,9,16,2]{1,3,2,5,4,0:T(8,128)S(1)} fusion(f32[4,3,9,1,1,1]{2,1,5,4,3,0:T(4,128)S(1)} %copy-done.3, f32[32,16,2,3,3]{0,1,4,3,2:T(8,128)S(1)} %slice-done), kind=kOutput, calls=%fused_computation | convolution fusion | flops 3981312 | bytes 479664 | tf_op jit(solution)/shard_map/oczyx,iyh->ioxhcz/dot_general | solution.py:467
  13.2 1.1 %copy.35 = f32[4,32,3,9,16,2]{1,0,5,4,3,2:T(4,128)S(1)} copy(f32[4,32,3,9,16,2]{1,3,2,5,4,0:T(8,128)S(1)} %convolution_bitcast_fusion) | data formatting | bytes 884736 | tf_op jit(solution)/shard_map/oczyx,iyh->ioxhcz/transpose | solution.py:467
  14.4 0.0 copy-start.4
  14.4 0.0 copy-start.2
  14.4 0.0 copy-start.1
  14.4 0.7 %reshape.60 = f32[128,864]{0,1:T(8,128)S(1)} reshape(f32[4,32,3,9,16,2]{1,0,5,4,3,2:T(4,128)S(1)} %copy.35) | data formatting | bytes 884736 | tf_op jit(solution)/shard_map/reshape | solution.py:468
  15.2 0.8 %reduce_precision.41 = f32[128,864]{0,1:T(8,128)} reduce-precision(f32[128,864]{0,1:T(8,128)S(1)} %reshape.60), exponent_bits=8, mantissa_bits=7 | non-fusion elementwise | flops 110592 | bytes 884736 | tf_op jit(solution)/shard_map/reduce_precision | solution.py:50
  15.9 0.2 copy.37
  16.1 0.0 copy-done.4
  16.2 0.1 broadcast_in_dim.4
  16.2 0.1 tile.10
  16.3 0.1 tile.12
  16.4 0.0 copy-done.2
  16.4 0.0 copy-done.1
  16.4 0.0 copy-start
  16.4 1.0 %convolution_bitcast_fusion.1 = f32[9,16,2,3,2,16]{5,1,0,3,4,2:T(8,128)S(1)} fusion(f32[9,3,16,1,1,1]{2,1,0,5,4,3:T(4,128)S(1)} %copy-done.1, f32[16,1,2,3,3]{0,3,4,2,1:T(4,128)S(1)} %get-tuple-element.14, f32[16,1,2,3,3]{0,3,4,2,1:T(4,128)S(1)} %get-tuple-element.13), kind=kOutput, calls=%fused_computation.1 | convolution fusion | flops 995904 | bytes 114624 | tf_op jit(solution)/shard_map/czpyx,iys->iczxps/dot_general | solution.py:451
  17.5 0.5 copy.32
  17.9 0.6 reshape.59
  18.5 0.0 copy-done
  18.5 0.2 copy.36
  18.7 0.1 pad_add_fusion.refs_0_
  18.8 0.1 fusion.7
  18.9 18.5 %all-to-all-done = f32[1056,2,128]{2,1,0:T(2,128)S(1)} async-done(((f32[1056,2,128]{2,1,0:T(2,128)}), f32[1056,2,128]{2,1,0:T(2,128)S(1)}, u32[]{:S(2)}, u32[]{:S(2)}) %all-to-all-start) | async-done | bytes 1081376 | tf_op jit(solution)/shard_map/all_to_all | solution.py:483
  37.4 0.0 copy-start.5
  37.4 5.0 %join.1 = (f32[2,136,256]{2,1,0:T(8,128)S(1)}, f32[32,8,128]{2,1,0:T(8,128)}) custom-call(s32[2]{0:T(128)S(1)} %pad_add_fusion.refs_0_, f32[32,33,2,128]{3,2,1,0:T(2,128)S(1)} %bitcast.38, f32[2112,128]{1,0:T(8,128)S(1)} %bitcast.39), custom_call_target="tpu_custom_call" | custom-call | tf_op jit(solution)/shard_map/join/pallas_call | solution.py:289
  42.4 3.8 %all-to-all-start.1 = ((f32[32,8,128]{2,1,0:T(8,128)}), f32[32,8,128]{2,1,0:T(8,128)S(1)}, u32[]{:S(2)}, u32[]{:S(2)}) async-start(f32[32,8,128]{2,1,0:T(8,128)} %get-tuple-element.8), calls=%async_computation.1 | async-start | bytes 262144 | tf_op jit(solution)/shard_map/all_to_all | solution.py:488
  46.2 0.1 copy.33
  46.3 0.2 fusion.1.refs_3_
  46.6 7.8 %all-to-all-done.1.refs_2_ = f32[32,8,128]{2,1,0:T(8,128)S(1)} async-done(((f32[32,8,128]{2,1,0:T(8,128)}), f32[32,8,128]{2,1,0:T(8,128)S(1)}, u32[]{:S(2)}, u32[]{:S(2)}) %all-to-all-start.1) | async-done | bytes 131104 | tf_op jit(solution)/shard_map/all_to_all | solution.py:488
  54.4 0.0 copy-done.5
  54.4 0.1 broadcast_in_dim.10.refs_5_
  54.5 8.1 %convolve.1 = f32[2048,128]{1,0:T(8,128)} custom-call(s32[2]{0:T(128)S(1)} %pad_add_fusion.refs_0_, f32[2,136,256]{2,1,0:T(8,128)S(1)} %get-tuple-element.7.refs_1_, f32[32,8,128]{2,1,0:T(8,128)S(1)} %all-to-all-done.1.refs_2_, bf16[288,304]{1,0:T(8,128)(2,1)S(1)} %fusion.1.refs_3_, bf16[256,864]{1,0:T(8,128)(2,1)S(1)} %pad_maximum_fusion.refs_4_, ...), custom_call_target="tpu_custom_call" | custom-call | tf_op jit(solution)/shard_map/convolve/pallas_call | solution.py:429
  (7 shorter events, 0.1 us)
Async XLA Ops:
  0.0 10.5 %slice-start = ((f32[32,16,3,3,3]{0,1,4,3,2:T(8,128)}), f32[32,16,2,3,3]{0,1,4,3,2:T(8,128)S(1)}, s32[]{:S(2)}) async-start(f32[32,16,3,3,3]{0,1,4,3,2:T(8,128)} %param.12), calls=%async_computation.2 | async-start | bytes 294912 | tf_op jit(solution)/shard_map/slice | solution.py:467
  0.0 10.5 %copy-start.3 = (f32[4,3,9,1,1,1]{2,1,5,4,3,0:T(4,128)S(1)}, f32[4,3,9,1,1,1]{2,1,5,4,3,0:T(4,128)}, u32[]{:S(2)}) copy-start(f32[4,3,9,1,1,1]{2,1,5,4,3,0:T(4,128)} %constant.21) | copy-start | bytes 1300
  3.2 34.2 %all-to-all-start = ((f32[1056,2,128]{2,1,0:T(2,128)}), f32[1056,2,128]{2,1,0:T(2,128)S(1)}, u32[]{:S(2)}, u32[]{:S(2)}) async-start(f32[1056,2,128]{2,1,0:T(2,128)} %pack.1), calls=%async_computation | async-start | bytes 2162688 | tf_op jit(solution)/shard_map/all_to_all | solution.py:483
  14.4 1.8 %copy-start.4 = (f32[16]{0:T(128)S(1)}, f32[16]{0:T(128)}, u32[]{:S(2)}) copy-start(f32[16]{0:T(128)} %param.11) | copy-start | bytes 196
  14.4 2.0 %copy-start.2 = (f32[16,1,3,3,3]{0,1,4,3,2:T(1,128)S(1)}, f32[16,1,3,3,3]{0,1,4,3,2:T(1,128)}, u32[]{:S(2)}) copy-start(f32[16,1,3,3,3]{0,1,4,3,2:T(1,128)} %param.10) | copy-start | bytes 5188
  14.4 2.0 %copy-start.1 = (f32[9,3,16,1,1,1]{2,1,0,5,4,3:T(4,128)S(1)}, f32[9,3,16,1,1,1]{2,1,0,5,4,3:T(4,128)}, u32[]{:S(2)}) copy-start(f32[9,3,16,1,1,1]{2,1,0,5,4,3:T(4,128)} %constant.20) | copy-start | bytes 5188
  16.4 2.1 %copy-start = (f32[128,864]{0,1:T(8,128)S(1)}, f32[128,864]{0,1:T(8,128)}, u32[]{:S(2)}) copy-start(f32[128,864]{0,1:T(8,128)} %reduce_precision.41) | copy-start | bytes 1327108
  37.4 17.0 %copy-start.5 = (f32[32]{0:T(128)S(1)}, f32[32]{0:T(128)}, u32[]{:S(2)}) copy-start(f32[32]{0:T(128)} %param.13) | copy-start | bytes 388
  42.4 12.0 %all-to-all-start.1 = ((f32[32,8,128]{2,1,0:T(8,128)}), f32[32,8,128]{2,1,0:T(8,128)S(1)}, u32[]{:S(2)}, u32[]{:S(2)}) async-start(f32[32,8,128]{2,1,0:T(8,128)} %get-tuple-element.8), calls=%async_computation.1 | async-start | bytes 262144 | tf_op jit(solution)/shard_map/all_to_all | solution.py:488

commit v4 on v3

--- a/solution.py
+++ b/solution.py
@@ -25,7 +25,6 @@
 WIN = 16
 BLOCKS = BY // (2 * OUT_ROWS)
 PHASES = 5
-UNROLL = 8
 JOIN_UNROLL = 8
 K1 = 3 * BZ * WIN
 HID = HID_ROWS * C1 * BZ
@@ -137,7 +136,20 @@
     )(routes_t, routes_t, strips.reshape(held * pairs, 2, SX))
 
 
-def join_body(per_pair, grid, edge, routes, strips, joined, messages, data, place_y, params, sem):
+EDGE_COLUMNS = (COLS - 4, COLS - 3, COLS - 2, COLS - 1, 0, 1, 2)
+
+
+def pick_columns():
+    row = iota((8, COLS), 0)
+    col = iota((8, COLS), 1)
+    chosen = None
+    for i, x in enumerate(EDGE_COLUMNS):
+        here = (row == i) & (col == x // 2 + (x % 2) * HALF)
+        chosen = here if chosen is None else chosen | here
+    return jnp.where(chosen, 1.0, 0.0)
+
+
+def join_body(per_pair, grid, edge, routes, strips, joined, messages, own_columns, data, place_y, params, sem):
     senders = routes.shape[0]
     slots = senders * per_pair
     chunk = 2 * chunk_of(per_pair)
@@ -154,7 +166,7 @@
     top = field(2)
     left = field(3)
     ramp = field(7)
-    y = iota((slots, 256), 1) - TOP - top
+    y = iota((slots, BY), 1) - top
     weight_y = jnp.where((y >= 0) & (y < SY), jnp.minimum(jnp.minimum(y + 1, SY - y), ramp), 0)
     col = iota((slots, COLS), 1)
     x = jnp.where(col < HALF, 2 * col, 2 * (col - HALF) + 1) - left
@@ -162,11 +174,11 @@
     weight_y = jnp.where(live == 1, weight_y, 0).astype(F32).astype(BF16)
     weight_x = weight_x.astype(F32).astype(BF16)
     over_rows = (((0,), (0,)), ((), ()))
-    total = lax.dot_general(weight_y, weight_x, over_rows, preferred_element_type=F32)[:SROW]
+    total = lax.dot_general(weight_y, weight_x, over_rows, preferred_element_type=F32)
     fetch.wait()
     lane = iota((SY, SX), 1)
-    row_lane = iota((SY, 256), 1)
-    row_sub = iota((SY, 256), 0)
+    row_lane = iota((SY, BY), 1)
+    row_sub = iota((SY, BY), 0)
 
     def one(h, r):
         k = h * per_pair + r
@@ -201,7 +213,7 @@
                 at = z * COLS + side * SX
                 data[pl.ds(k * SY, SY), at : at + SX] = coarse
                 data[pl.ds(k * SY, SY), BZ * COLS + at : BZ * COLS + at + SX] = fine
-        y = row_lane - TOP - top
+        y = row_lane - top
         weight_y = jnp.minimum(jnp.minimum(y + 1, SY - y), ramp).astype(F32)
         spread = jnp.where(row_sub == y, weight_y * (1.0 - frac_y), 0.0) + jnp.where(
             row_sub == y + 1, weight_y * frac_y, 0.0
@@ -215,23 +227,13 @@
 
     lax.fori_loop(0, senders, holder, 0, unroll=JOIN_UNROLL)
 
-    sums = lax.dot_general(place_y[...], data[...], over_rows, preferred_element_type=F32)[:SROW]
+    sums = lax.dot_general(place_y[...], data[...], over_rows, preferred_element_type=F32)
     sums = sums[:, : BZ * COLS] + sums[:, BZ * COLS :]
 
     src = iota((COLS, COLS), 0)
     dst = iota((COLS, COLS), 1)
     order = (src == jnp.where(dst < HALF, 2 * dst, 2 * (dst - HALF) + 1)).astype(F32).astype(BF16)
-    row = iota((SROW, COLS), 0)
-    inside = (row >= TOP) & (row < TOP + BY)
-    pick_row = iota((8, COLS), 0)
-    pick_col = iota((8, COLS), 1)
-    pick = jnp.where(
-        ((pick_row == 0) & (pick_col == HALF - 1))
-        | ((pick_row == 1) & (pick_col == COLS - 1))
-        | ((pick_row == 2) & (pick_col == 0)),
-        1.0,
-        0.0,
-    )
+    pick = pick_columns()
     right_rows = []
     left_rows = []
     down_rows = []
@@ -241,17 +243,18 @@
         ordered = jnp.dot(coarse, order, preferred_element_type=F32) + jnp.dot(
             fine, order, preferred_element_type=F32
         )
-        value = jnp.where(inside, ordered / jnp.where(inside, total, 1.0), 0.0)
+        value = ordered / total
         joined[z] = value
         columns_as_rows = lax.dot_general(
             pick, value, (((1,), (1,)), ((), ())), precision=EXACT, preferred_element_type=F32
-        )[:, TOP : TOP + BY]
-        right_rows.append(columns_as_rows[0:2])
-        left_rows.append(columns_as_rows[2:3])
+        )
+        own_columns[8 * z : 8 * z + 8, :] = columns_as_rows
+        right_rows.append(columns_as_rows[2:4])
+        left_rows.append(columns_as_rows[4:5])
         for half in range(2):
             cut = value[:, half * HALF : (half + 1) * HALF]
-            down_rows.append(cut[BY : BY + 2])
-            up_rows.append(cut[TOP : TOP + 1])
+            down_rows.append(cut[BY - 2 : BY])
+            up_rows.append(cut[0:1])
 
     def tile(rows):
         have = sum(r.shape[0] for r in rows)
@@ -289,14 +292,15 @@
     return pl.pallas_call(
         lambda *refs: join_body(per_pair, grid, *refs),
         in_specs=[pl.BlockSpec(memory_space=pltpu.SMEM), pl.BlockSpec(memory_space=pl.ANY), vmem],
-        out_specs=[vmem, vmem],
+        out_specs=[vmem, vmem, vmem],
         out_shape=[
-            jax.ShapeDtypeStruct((BZ, SROW, COLS), F32),
+            jax.ShapeDtypeStruct((BZ, BY, COLS), F32),
             jax.ShapeDtypeStruct((senders, 8, HALF), F32),
+            jax.ShapeDtypeStruct((8 * BZ, BY), F32),
         ],
         scratch_shapes=[
             pltpu.VMEM((slots * SY, 2 * BZ * COLS), BF16),
-            pltpu.VMEM((slots * SY, 256), BF16),
+            pltpu.VMEM((slots * SY, BY), BF16),
             pltpu.SMEM((senders, 2, SX), F32),
             pltpu.SemaphoreType.DMA,
         ],
@@ -309,7 +313,80 @@
     )
 
 
-def conv_body(grid, edge, joined, received, first, second, bias, out, phases, coarse_h, fine_h):
+def two_blocks(wide, blocks, keep, first, second, bias, out, coarse_h, fine_h, top_outside=None):
+    ones = jnp.ones((16, 256), BF16)
+    for group in range(3):
+        coarse = [wide[group + dx, z][0] for dx in range(3) for z in range(BZ)]
+        fine = [wide[group + dx, z][1] for dx in range(3) for z in range(BZ)]
+        stacked = jnp.concatenate(coarse + fine + coarse + [ones], axis=0)
+        hidden = jnp.dot(first[...], stacked, preferred_element_type=F32)
+        hidden = jnp.maximum(hidden, 0.0)
+        if group == 0 and keep is not None:
+            hidden = hidden * keep
+        coarse, fine = split_kernel(hidden)
+        coarse_h[group * HID : (group + 1) * HID, :] = coarse
+        fine_h[group * HID : (group + 1) * HID, :] = fine
+    if top_outside is not None:
+
+        @pl.when(top_outside)
+        def _():
+            for group in range(3):
+                for scratch in (coarse_h, fine_h):
+                    nothing = jnp.zeros((C1 * BZ, HALF), BF16)
+                    scratch[group * HID : group * HID + C1 * BZ, :HALF] = nothing
+
+    both = jnp.dot(second[...], coarse_h[...], preferred_element_type=F32)
+    rest = jnp.dot(second[:OUTM, :], fine_h[...], preferred_element_type=F32)
+    result = both[:OUTM] + both[OUTM:] + rest
+    for side, b in enumerate(blocks):
+        for r in range(OUT_ROWS):
+            out[pl.ds(OUT_ROWS * b + r, C2, stride=BY // 2), :] = (
+                result[r * C2 : (r + 1) * C2, side * HALF : (side + 1) * HALF] + bias[...]
+            )
+
+
+def inner_body(joined, first, second, bias, out, phases, coarse_h, fine_h):
+    for z in range(BZ):
+        even = joined[z, :, :HALF]
+        odd = joined[z, :, HALF:]
+        parts = (pltpu.roll(even, 1, 1), pltpu.roll(odd, 1, 1), even, odd, pltpu.roll(even, HALF - 1, 1))
+        for j, part in enumerate(parts):
+            phases[j, z, TOP : TOP + BY, :] = part
+    half = (BLOCKS - 2) // 2
+    for step in range(half):
+        blocks = (1 + step, 1 + step + half)
+        wide = {}
+        for j in range(PHASES):
+            for z in range(BZ):
+                cut = [phases[j, z, 8 * b : 8 * b + WIN, :] for b in blocks]
+                wide[j, z] = split_kernel(jnp.concatenate(cut, axis=1))
+        slot = step % 2
+        two_blocks(
+            wide, blocks, None, first, second, bias, out, coarse_h.at[slot], fine_h.at[slot]
+        )
+
+
+def inner(joined, first, second, bias):
+    vmem = pl.BlockSpec(memory_space=pltpu.VMEM)
+    return pl.pallas_call(
+        inner_body,
+        in_specs=[vmem] * 4,
+        out_specs=vmem,
+        out_shape=jax.ShapeDtypeStruct((C2 * BY // 2, HALF), F32),
+        scratch_shapes=[
+            pltpu.VMEM((PHASES, BZ, SROW, HALF), F32),
+            pltpu.VMEM((2, K2, 256), BF16),
+            pltpu.VMEM((2, K2, 256), BF16),
+        ],
+        compiler_params=pltpu.CompilerParams(vmem_limit_bytes=48 * 2**20),
+        name="inner",
+    )(joined, first, second, bias)
+
+
+def rim_body(
+    grid, edge, joined, received, own_columns, inner_out, first, second, bias, first_rim, second_rim,
+    out, coarse_h, fine_h,
+):
     at_row = edge[0]
     at_col = edge[1]
     rows, cols = grid
@@ -323,9 +400,11 @@
             there = (row >= 0) & (row < rows) & (col >= 0) & (col < cols)
             index = jnp.where(there, row * cols + col, 0)
             halo[dy, dx] = jnp.where(there, received[index], 0.0)
+    no_row = at_row == 0
+    no_col = at_col == 0
     wide_lane = iota((8, 256), 1)
 
-    def along(above, here, below):
+    def stored(above, here, below):
         zero = jnp.zeros((8, 128), F32)
         turned = [
             pltpu.roll(jnp.concatenate([part, zero], axis=1), by, 1)
@@ -336,109 +415,148 @@
             wide_lane < TOP + BY, low, jnp.where(wide_lane == TOP + BY, turned[2], 0.0)
         )
 
-    from_left = along(halo[-1, -1], halo[0, -1], halo[1, -1])
-    from_right = along(halo[-1, 1], halo[0, 1], halo[1, 1])
+    from_left = stored(halo[-1, -1], halo[0, -1], halo[1, -1])
+    from_right = stored(halo[-1, 1], halo[0, 1], halo[1, 1])
     from_above = halo[-1, 0]
     from_below = halo[1, 0]
+
     pick_row = iota((8, HALF), 0)
     pick_lane = iota((8, HALF), 1)
-    tall_lane = iota((SROW, HALF), 1)
-    row8 = iota((8, HALF), 0)
+    tall_lane = iota((2 * WIN, HALF), 1)
 
     def column(message, row, lane_at):
         chosen = jnp.where((pick_row == row) & (pick_lane == lane_at), 1.0, 0.0)
+        ends = jnp.concatenate([message[:, :WIN], message[:, SROW - WIN : SROW]], axis=1)
         return lax.dot_general(
-            message, chosen, (((0,), (0,)), ((), ())), precision=EXACT, preferred_element_type=F32
-        )[:SROW]
-
+            ends, chosen, (((0,), (0,)), ((), ())), precision=EXACT, preferred_element_type=F32
+        )
+
+    wide = {}
     for z in range(BZ):
         halves = []
         for half in range(2):
             own = joined[z, :, half * HALF : (half + 1) * HALF]
             at = 4 * z + 2 * half
-            above = jnp.concatenate([from_above[at : at + 2], own[2:8]], axis=0)
-            at = 2 * z + half
-            below = jnp.concatenate(
-                [own[SROW - 8 : SROW - 6], from_below[at : at + 1], jnp.zeros((5, HALF), F32)], axis=0
-            )
-            halves.append(jnp.concatenate([above, own[8 : SROW - 8], below], axis=0))
+            bottom = 2 * z + half
+            ends = [
+                from_above[at : at + 2],
+                own[: WIN - TOP],
+                own[SROW - WIN - TOP :],
+                from_below[bottom : bottom + 1],
+                jnp.zeros((SROW - BY - TOP - 1, HALF), F32),
+            ]
+            halves.append(jnp.concatenate(ends, axis=0))
         even, odd = halves
-        phases[0, z] = jnp.where(tall_lane == 0, column(from_left, 2 * z, 0), pltpu.roll(even, 1, 1))
-        phases[1, z] = jnp.where(tall_lane == 0, column(from_left, 2 * z + 1, 0), pltpu.roll(odd, 1, 1))
-        phases[2, z] = even
-        phases[3, z] = odd
-        phases[4, z] = jnp.where(
-            tall_lane == HALF - 1, column(from_right, z, HALF - 1), pltpu.roll(even, HALF - 1, 1)
-        )
-    no_row = edge[0] == 0
-    no_col = edge[1] == 0
+        parts = (
+            jnp.where(tall_lane == 0, column(from_left, 2 * z, 0), pltpu.roll(even, 1, 1)),
+            jnp.where(tall_lane == 0, column(from_left, 2 * z + 1, 0), pltpu.roll(odd, 1, 1)),
+            even,
+            odd,
+            jnp.where(
+                tall_lane == HALF - 1, column(from_right, z, HALF - 1), pltpu.roll(even, HALF - 1, 1)
+            ),
+        )
+        for j, part in enumerate(parts):
+            wide[j, z] = split_kernel(jnp.concatenate([part[:WIN], part[WIN:]], axis=1))
+
+    pick = pick_columns()
+    left_rows = []
+    right_rows = []
+    for z in range(BZ):
+        cut = [
+            jnp.concatenate([from_above[4 * z + c : 4 * z + c + 1], from_above[4 * z + 2 + c : 4 * z + 3 + c]], axis=1)
+            for c in range(2)
+        ]
+        cut.append(jnp.concatenate([from_below[2 * z : 2 * z + 1], from_below[2 * z + 1 : 2 * z + 2]], axis=1))
+        cut.append(jnp.zeros((5, COLS), F32))
+        outer = lax.dot_general(
+            pick,
+            jnp.concatenate(cut, axis=0),
+            (((1,), (1,)), ((), ())),
+            precision=EXACT,
+            preferred_element_type=F32,
+        )
+        outer = jnp.concatenate([outer, jnp.zeros((8, 256 - 8), F32)], axis=1)
+        here = jnp.concatenate([own_columns[8 * z : 8 * z + 8, :], jnp.zeros((8, BY), F32)], axis=1)
+        own = jnp.where(
+            wide_lane < TOP,
+            outer,
+            jnp.where(
+                wide_lane < TOP + BY,
+                pltpu.roll(here, TOP, 1),
+                jnp.where(wide_lane == TOP + BY, pltpu.roll(outer, BY, 1), 0.0),
+            ),
+        )
+        one = jnp.ones((1, 256), F32)
+        rest = jnp.zeros((2, 256), F32)
+        left_rows += [from_left[2 * z : 2 * z + 2], own[4:7], one, rest]
+        right_rows += [own[0:4], from_right[z : z + 1], one, rest]
+    both = jnp.concatenate(
+        [jnp.concatenate(left_rows, axis=0), jnp.concatenate(right_rows, axis=0)], axis=1
+    )
+
+    def reach(values):
+        return jnp.concatenate([values] + [pltpu.roll(values, 512 - dy, 1) for dy in (1, 2)], axis=0)
+
+    hidden = jnp.dot(first_rim[...], reach(both), precision=EXACT, preferred_element_type=F32)
+    hidden = jnp.maximum(hidden, 0.0)
+    lane = iota((3 * C1 * BZ, 512), 1)
+    depth = iota((3 * C1 * BZ, 512), 0)
+    outside = no_row & ((lane & 255) == 0)
+    outside = outside | (no_col & (lane < 256) & (depth < C1 * BZ))
+    hidden = jnp.where(outside, 0.0, hidden)
+    found = jnp.dot(second_rim[...], reach(hidden), precision=EXACT, preferred_element_type=F32)
+    every = jnp.where(iota((BY // 2, 256), 1) == 2 * iota((BY // 2, 256), 0), 1.0, 0.0)
+    columns = [
+        lax.dot_general(
+            every,
+            found[:, side * 256 : (side + 1) * 256] + bias[:, :1],
+            (((1,), (1,)), ((), ())),
+            precision=EXACT,
+            preferred_element_type=F32,
+        )
+        for side in range(2)
+    ]
+    out_lane = iota((BY // 2, HALF), 1)
+    for o in range(C2):
+        at = o * (BY // 2)
+        values = inner_out[at : at + BY // 2, :]
+        values = jnp.where(out_lane == 0, columns[0][:, o : o + 1], values)
+        out[at : at + BY // 2, :] = jnp.where(out_lane == HALF - 1, columns[1][:, o : o + 1], values)
+
     keep = jnp.where(no_col & ((iota((1, 256), 1) & (HALF - 1)) == 0), 0.0, 1.0)
-    ones = jnp.ones((16, 256), BF16)
-
-    def pair(step, part):
-        slot = part % 2
-        blocks = (step, step + BLOCKS // 2)
-        wide = {}
-        for j in range(PHASES):
-            for z in range(BZ):
-                cut = [
-                    phases[j, z, pl.ds(pl.multiple_of(8 * b, 8), WIN), :] for b in blocks
-                ]
-                wide[j, z] = split_kernel(jnp.concatenate(cut, axis=1))
-        for group in range(3):
-            coarse = [wide[group + dx, z][0] for dx in range(3) for z in range(BZ)]
-            fine = [wide[group + dx, z][1] for dx in range(3) for z in range(BZ)]
-            stacked = jnp.concatenate(coarse + fine + coarse + [ones], axis=0)
-            hidden = jnp.dot(first[...], stacked, preferred_element_type=F32)
-            hidden = jnp.maximum(hidden, 0.0)
-            if group == 0:
-                hidden = hidden * keep
-            coarse, fine = split_kernel(hidden)
-            coarse_h[slot, group * HID : (group + 1) * HID, :] = coarse
-            fine_h[slot, group * HID : (group + 1) * HID, :] = fine
-
-        if part == 0:
-
-            @pl.when(no_row & (step == 0))
-            def _():
-                for group in range(3):
-                    for scratch in (coarse_h, fine_h):
-                        nothing = jnp.zeros((C1 * BZ, HALF), BF16)
-                        scratch[slot, group * HID : group * HID + C1 * BZ, :HALF] = nothing
-
-        both = jnp.dot(second[...], coarse_h[slot], preferred_element_type=F32)
-        rest = jnp.dot(second[:OUTM, :], fine_h[slot], preferred_element_type=F32)
-        result = both[:OUTM] + both[OUTM:] + rest
-        for side, b in enumerate(blocks):
-            for r in range(OUT_ROWS):
-                at = OUT_ROWS * b + r
-                out[pl.ds(at, C2, stride=BY // 2), :] = (
-                    result[r * C2 : (r + 1) * C2, side * HALF : (side + 1) * HALF] + bias[...]
-                )
-
-    def steps(i, carry):
-        for part in range(UNROLL):
-            pair(UNROLL * i + part, part)
-        return carry
-
-    lax.fori_loop(0, BLOCKS // 2 // UNROLL, steps, 0)
-
-
-def convolve(grid, edge, joined, received, first, second, bias):
+    two_blocks(
+        wide, (0, BLOCKS - 1), keep, first, second, bias, out, coarse_h, fine_h, top_outside=no_row
+    )
+
+
+def rim(grid, edge, joined, received, own_columns, inner_out, first, second, bias, first_rim, second_rim):
     vmem = pl.BlockSpec(memory_space=pltpu.VMEM)
     return pl.pallas_call(
-        lambda *refs: conv_body(grid, *refs),
-        in_specs=[pl.BlockSpec(memory_space=pltpu.SMEM)] + [vmem] * 5,
+        lambda *refs: rim_body(grid, *refs),
+        in_specs=[pl.BlockSpec(memory_space=pltpu.SMEM)] + [vmem] * 9,
         out_specs=vmem,
         out_shape=jax.ShapeDtypeStruct((C2 * BY // 2, HALF), F32),
-        scratch_shapes=[
-            pltpu.VMEM((PHASES, BZ, SROW, HALF), F32),
-            pltpu.VMEM((2, K2, 256), BF16),
-            pltpu.VMEM((2, K2, 256), BF16),
-        ],
+        scratch_shapes=[pltpu.VMEM((K2, 256), BF16), pltpu.VMEM((K2, 256), BF16)],
         compiler_params=pltpu.CompilerParams(vmem_limit_bytes=48 * 2**20),
-        name="convolve",
-    )(edge, joined, received, first, second, bias)
+        name="rim",
+    )(edge, joined, received, own_columns, inner_out, first, second, bias, first_rim, second_rim)
+
+
+def rim_tables(weight1, bias1, weight2):
+    kernel = weight1[:, 0]
+    planes = jnp.stack([kernel[:, 1:3], kernel[:, 0:2]], axis=1)
+    reach = np.zeros((3, 3, 8), np.float32)
+    for i in range(3):
+        for dx in range(3):
+            reach[i, dx, i + dx] = 1.0
+    table = jnp.einsum("czpyx,kxq->kczypq", planes, jnp.asarray(reach), precision=EXACT)
+    ones = np.zeros((3, BZ, 8), np.float32)
+    ones[0, 0, PHASES] = 1.0
+    table = table + bias1[None, :, None, None, None, None] * jnp.asarray(ones)
+    first = table.reshape(3 * C1 * BZ, 3 * BZ * 8)
+    second = jnp.transpose(weight2[:, :, 1:3], (0, 3, 4, 1, 2)).reshape(C2, 9 * C1 * BZ)
+    return first, second
 
 
 def first_table(weight, bias):
@@ -484,9 +602,13 @@
     first = first_table(conv1_weight, conv1_bias)
     second = second_table(conv2_weight)
     bias = jnp.broadcast_to(conv2_bias[:, None], (C2, HALF))
-    joined, messages = join((rows, cols), edge, arrived, per_pair)
+    first_rim, second_rim = rim_tables(conv1_weight, conv1_bias, conv2_weight)
+    joined, messages, own_columns = join((rows, cols), edge, arrived, per_pair)
     received = lax.all_to_all(messages, axes, split_axis=0, concat_axis=0, tiled=True)
-    features = convolve((rows, cols), edge, joined, received, first, second, bias)
+    inner_out = inner(joined, first, second, bias)
+    features = rim(
+        (rows, cols), edge, joined, received, own_columns, inner_out, first, second, bias, first_rim, second_rim
+    )
     return features.reshape(C2, 1, BY // 2, HALF)
 
 

time: 62.9 us -> 58.6 us (0.932)
  waiting for transfers between devices: 26.3 us -> 20.3 us
  local copies, waits for them, and re-layouts: 3.8 us -> 4.51 us
    all_to_all x1, waiting for transfers between devices: 7.83 us -> 2.27 us  [body(): lax.all_to_all(messages, axes, split_axis=0, concat_axis=0, tiled=True)]
    pallas_call x1 -> x2, Pallas kernels: 8.12 us -> 9.05 us  [the longest x1 4.58 us: inner(): pl.pallas_call(inner_body, in_specs=[vmem] * 4, out_specs=vmem, out_shape...]
  transfers between devices with their start and end apart: 2 -> 2, of which waited for: 2 -> 2; matrix products, arithmetic and copies ran while one was open for 14% -> 17% of each run, Pallas kernels for 0% -> 8%
where the time goes in v4:
time: 58.6 us; the launch traced here: 58.3 us
  waiting for transfers between devices  20.3 us (35%)
  Pallas kernels  16.7 us (28%)
  starting transfers between devices  11.1 us (19%)
  local copies, waits for them, and re-layouts  4.51 us (8%)
  matrix products  4.05 us (7%)
  other arithmetic  1.29 us (2%)
    all_to_all x1, waiting for transfers between devices, body(): lax.all_to_all(outgoing, axes, split_axis=0, concat_axis=0, tiled=True)  18 us
    all_to_all x1, starting transfers between devices, body(): lax.all_to_all(outgoing, axes, split_axis=0, concat_axis=0, tiled=True)  7.3 us
    pallas_call x1, Pallas kernels, inner(): pl.pallas_call(inner_body, in_specs=[vmem] * 4, out_specs=vmem, out_shape...  4.58 us
    pallas_call x1, Pallas kernels, join(): pl.pallas_call(lambda *refs: join_body(per_pair, grid, *refs), in_specs=[...  4.52 us
    pallas_call x1, Pallas kernels, rim(): pl.pallas_call(lambda *refs: rim_body(grid, *refs), in_specs=[pl.BlockSpe...  4.47 us
    all_to_all x1, starting transfers between devices, body(): lax.all_to_all(messages, axes, split_axis=0, concat_axis=0, tiled=True)  3.81 us
    pallas_call x1, Pallas kernels, pack(): pl.pallas_call(lambda *refs: pack_body(per_pair, *refs), in_specs=[pl.Blo...  3.15 us
    dot_general x1, matrix products, second_table(): jnp.einsum('oczyx,iyh->ioxhcz', weight[:, :, 1:3], jnp.asarray(reach), pr...  2.71 us
  transfers between devices with their start and end apart: 2, of which 2 were waited for; matrix products, arithmetic and copies ran while one was open for 17% of the time, Pallas kernels for 8%

profile of v4, /device:TPU:0, one launch (start us, length us, event | category | flops | bytes accessed | tf_op | source)
XLA Modules:
  0.0 58.3 jit_solution(11605892326765189528)
XLA Ops:
  0.0 3.1 %pack.1 = f32[1056,2,128]{2,1,0:T(2,128)} custom-call(s32[8,64]{1,0:T(8,128)} %bitcast.58, s32[8,64]{1,0:T(8,128)} %bitcast.59, f32[1024,2,128]{2,1,0:T(2,128)} %bitcast.54), custom_call_target="tpu_custom_call" | custom-call | tf_op jit(solution)/shard_map/pack/pallas_call | solution.py:122
  3.2 7.3 %all-to-all-start = ((f32[1056,2,128]{2,1,0:T(2,128)}), f32[1056,2,128]{2,1,0:T(2,128)S(1)}, u32[]{:S(2)}, u32[]{:S(2)}) async-start(f32[1056,2,128]{2,1,0:T(2,128)} %pack.1), calls=%async_computation | async-start | bytes 2162688 | tf_op jit(solution)/shard_map/all_to_all | solution.py:601
  10.5 0.0 copy-done.1
  10.5 0.0 copy-done.4
  10.5 2.7 %convolution_bitcast_fusion = f32[4,32,3,9,16,2]{1,3,2,5,4,0:T(8,128)S(1)} fusion(f32[4,3,9,1,1,1]{2,1,5,4,3,0:T(4,128)S(1)} %copy-done.4, f32[32,16,2,3,3]{0,1,4,3,2:T(8,128)S(1)} %slice.14), kind=kOutput, calls=%fused_computation | convolution fusion | flops 3981312 | bytes 479664 | tf_op jit(solution)/shard_map/oczyx,iyh->ioxhcz/dot_general | solution.py:585
  13.2 1.1 %copy.48 = f32[4,32,3,9,16,2]{1,0,5,4,3,2:T(4,128)S(1)} copy(f32[4,32,3,9,16,2]{1,3,2,5,4,0:T(8,128)S(1)} %convolution_bitcast_fusion) | data formatting | bytes 884736 | tf_op jit(solution)/shard_map/oczyx,iyh->ioxhcz/transpose | solution.py:585
  14.4 0.0 copy-start.7
  14.4 0.0 copy-start.3
  14.4 0.0 copy-start.2
  14.4 0.7 %reshape.74 = f32[128,864]{0,1:T(8,128)S(1)} reshape(f32[4,32,3,9,16,2]{1,0,5,4,3,2:T(4,128)S(1)} %copy.48) | data formatting | bytes 884736 | tf_op jit(solution)/shard_map/reshape | solution.py:586
  15.2 0.8 %reduce_precision.41 = f32[128,864]{0,1:T(8,128)} reduce-precision(f32[128,864]{0,1:T(8,128)S(1)} %reshape.74), exponent_bits=8, mantissa_bits=7 | non-fusion elementwise | flops 110592 | bytes 884736 | tf_op jit(solution)/shard_map/reduce_precision | solution.py:49
  16.0 0.2 copy.50
  16.2 0.0 copy-done.7
  16.2 0.1 broadcast_in_dim.4
  16.2 0.1 tile.10
  16.3 0.1 tile.12
  16.4 0.0 copy-done.3
  16.4 0.0 copy-done.2
  16.5 0.0 copy-start
  16.5 1.0 %convolution_bitcast_fusion.1 = f32[9,16,2,3,2,16]{5,1,0,3,4,2:T(8,128)S(1)} fusion(f32[9,3,16,1,1,1]{2,1,0,5,4,3:T(4,128)S(1)} %copy-done.2, f32[16,1,2,3,3]{0,3,4,2,1:T(4,128)S(1)} %get-tuple-element.16, f32[16,1,2,3,3]{0,3,4,2,1:T(4,128)S(1)} %get-tuple-element.15), kind=kOutput, calls=%fused_computation.1 | convolution fusion | flops 995904 | bytes 114624 | tf_op jit(solution)/shard_map/czpyx,iys->iczxps/dot_general | solution.py:569
  17.5 0.0 copy-start.6
  17.5 0.0 copy-start.5
  17.5 0.5 copy.45
  18.0 0.6 reshape.73
  18.5 0.0 copy-done
  18.6 0.2 copy.49
  18.8 0.1 pad_add_fusion.refs_0_
  18.9 0.0 copy-done.6
  18.9 0.1 broadcast_multiply_fusion
  18.9 0.0 copy-done.5
  18.9 0.3 fusion
  19.3 0.1 fusion.9
  19.4 18.0 %all-to-all-done = f32[1056,2,128]{2,1,0:T(2,128)S(1)} async-done(((f32[1056,2,128]{2,1,0:T(2,128)}), f32[1056,2,128]{2,1,0:T(2,128)S(1)}, u32[]{:S(2)}, u32[]{:S(2)}) %all-to-all-start) | async-done | bytes 1081376 | tf_op jit(solution)/shard_map/all_to_all | solution.py:601
  37.4 4.5 %join.1 = (f32[2,128,256]{2,1,0:T(8,128)S(1)}, f32[32,8,128]{2,1,0:T(8,128)}, f32[16,128]{1,0:T(8,128)S(1)}) custom-call(s32[2]{0:T(128)S(1)} %pad_add_fusion.refs_0_, f32[32,33,2,128]{3,2,1,0:T(2,128)S(1)} %bitcast.52, f32[2112,128]{1,0:T(8,128)S(1)} %bitcast.53), custom_call_target="tpu_custom_call" | custom-call | tf_op jit(solution)/shard_map/join/pallas_call | solution.py:292
  41.9 0.0 copy-start.8
  41.9 3.8 %all-to-all-start.1 = ((f32[32,8,128]{2,1,0:T(8,128)}), f32[32,8,128]{2,1,0:T(8,128)S(1)}, u32[]{:S(2)}, u32[]{:S(2)}) async-start(f32[32,8,128]{2,1,0:T(8,128)} %get-tuple-element.9), calls=%async_computation.1 | async-start | bytes 262144 | tf_op jit(solution)/shard_map/all_to_all | solution.py:607
  45.8 0.1 copy.71
  45.9 0.1 copy.46
  46.0 0.2 copy.53
  46.2 0.2 reshape.75.refs_8_
  46.5 0.1 copy.54
  46.5 0.1 copy.55.refs_9_
  46.6 0.2 fusion.2.first.refs_5_
  46.9 0.0 copy-done.8
  46.9 0.1 broadcast_in_dim.5.bias.refs_7_
  47.0 4.6 %inner.1.refs_4_ = f32[2048,128]{1,0:T(8,128)S(1)} custom-call(f32[2,128,256]{2,1,0:T(8,128)S(1)} %get-tuple-element.8.joined.refs_1_, bf16[288,304]{1,0:T(8,128)(2,1)S(1)} %fusion.2.first.refs_5_, bf16[256,864]{1,0:T(8,128)(2,1)S(1)} %pad_maximum_fusion.second.refs_6_, f32[32,128]{1,0:T(8,128)S(1)} %broadcast_in_dim.5.bias.refs_7_), custom_call_target="tpu_custom_call" | custom-call | tf_op jit(solution)/shard_map/inner/pallas_call | solution.py:371
  51.5 2.3 %all-to-all-done.1.refs_2_ = f32[32,8,128]{2,1,0:T(8,128)S(1)} async-done(((f32[32,8,128]{2,1,0:T(8,128)}), f32[32,8,128]{2,1,0:T(8,128)S(1)}, u32[]{:S(2)}, u32[]{:S(2)}) %all-to-all-start.1) | async-done | bytes 131104 | tf_op jit(solution)/shard_map/all_to_all | solution.py:607
  53.8 4.5 %rim.1 = f32[2048,128]{1,0:T(8,128)} custom-call(s32[2]{0:T(128)S(1)} %pad_add_fusion.refs_0_, f32[2,128,256]{2,1,0:T(8,128)S(1)} %get-tuple-element.8.joined.refs_1_, f32[32,8,128]{2,1,0:T(8,128)S(1)} %all-to-all-done.1.refs_2_, f32[16,128]{1,0:T(8,128)S(1)} %get-tuple-element.10.refs_3_, f32[2048,128]{1,0:T(8,128)S(1)} %inner.1.refs_4_, ...), custom_call_target="tpu_custom_call" | custom-call | tf_op jit(solution)/shard_map/rim/pallas_call | solution.py:535
  (11 shorter events, 0.1 us)
Async XLA Ops:
  0.0 10.5 %copy-start.1 = (f32[32,16,3,3,3]{0,1,4,3,2:T(8,128)S(1)}, f32[32,16,3,3,3]{0,1,4,3,2:T(8,128)}, u32[]{:S(2)}) copy-start(f32[32,16,3,3,3]{0,1,4,3,2:T(8,128)} %param.14) | copy-start | bytes 165892
  0.0 10.5 %copy-start.4 = (f32[4,3,9,1,1,1]{2,1,5,4,3,0:T(4,128)S(1)}, f32[4,3,9,1,1,1]{2,1,5,4,3,0:T(4,128)}, u32[]{:S(2)}) copy-start(f32[4,3,9,1,1,1]{2,1,5,4,3,0:T(4,128)} %constant.27) | copy-start | bytes 1300
  3.2 34.2 %all-to-all-start = ((f32[1056,2,128]{2,1,0:T(2,128)}), f32[1056,2,128]{2,1,0:T(2,128)S(1)}, u32[]{:S(2)}, u32[]{:S(2)}) async-start(f32[1056,2,128]{2,1,0:T(2,128)} %pack.1), calls=%async_computation | async-start | bytes 2162688 | tf_op jit(solution)/shard_map/all_to_all | solution.py:601
  14.4 1.8 %copy-start.7 = (f32[16]{0:T(128)S(1)}, f32[16]{0:T(128)}, u32[]{:S(2)}) copy-start(f32[16]{0:T(128)} %param.13) | copy-start | bytes 196
  14.4 2.0 %copy-start.3 = (f32[16,1,3,3,3]{0,1,4,3,2:T(1,128)S(1)}, f32[16,1,3,3,3]{0,1,4,3,2:T(1,128)}, u32[]{:S(2)}) copy-start(f32[16,1,3,3,3]{0,1,4,3,2:T(1,128)} %param.12) | copy-start | bytes 5188
  14.4 2.0 %copy-start.2 = (f32[9,3,16,1,1,1]{2,1,0,5,4,3:T(4,128)S(1)}, f32[9,3,16,1,1,1]{2,1,0,5,4,3:T(4,128)}, u32[]{:S(2)}) copy-start(f32[9,3,16,1,1,1]{2,1,0,5,4,3:T(4,128)} %constant.26) | copy-start | bytes 5188
  16.5 2.1 %copy-start = (f32[128,864]{0,1:T(8,128)S(1)}, f32[128,864]{0,1:T(8,128)}, u32[]{:S(2)}) copy-start(f32[128,864]{0,1:T(8,128)} %reduce_precision.41) | copy-start | bytes 1327108
  17.5 1.4 %copy-start.6 = (f32[3,2,8]{2,0,1:T(4,128)S(1)}, f32[3,2,8]{2,0,1:T(4,128)}, u32[]{:S(2)}) copy-start(f32[3,2,8]{2,0,1:T(4,128)} %constant.23.clone) | copy-start | bytes 580
  17.5 1.4 %copy-start.5 = (f32[3,3,8,1,1,1]{2,1,0,5,4,3:T(4,128)S(1)}, f32[3,3,8,1,1,1]{2,1,0,5,4,3:T(4,128)}, u32[]{:S(2)}) copy-start(f32[3,3,8,1,1,1]{2,1,0,5,4,3:T(4,128)} %constant.28) | copy-start | bytes 868
  41.9 4.9 %copy-start.8 = (f32[32]{0:T(128)S(1)}, f32[32]{0:T(128)}, u32[]{:S(2)}) copy-start(f32[32]{0:T(128)} %param.15) | copy-start | bytes 388
  41.9 11.9 %all-to-all-start.1 = ((f32[32,8,128]{2,1,0:T(8,128)}), f32[32,8,128]{2,1,0:T(8,128)S(1)}, u32[]{:S(2)}, u32[]{:S(2)}) async-start(f32[32,8,128]{2,1,0:T(8,128)} %get-tuple-element.9), calls=%async_computation.1 | async-start | bytes 262144 | tf_op jit(solution)/shard_map/all_to_all | solution.py:607

commit v5 on v4

--- a/solution.py
+++ b/solution.py
@@ -137,6 +137,10 @@
 
 
 EDGE_COLUMNS = (COLS - 4, COLS - 3, COLS - 2, COLS - 1, 0, 1, 2)
+
+
+def edge_column(i):
+    return jnp.where(i < 4, COLS - 4 + i, i - 4)
 
 
 def pick_columns():
@@ -233,7 +237,13 @@
     src = iota((COLS, COLS), 0)
     dst = iota((COLS, COLS), 1)
     order = (src == jnp.where(dst < HALF, 2 * dst, 2 * (dst - HALF) + 1)).astype(F32).astype(BF16)
-    pick = pick_columns()
+    along = iota((8, COLS), 1)
+    natural = edge_column(iota((8, COLS), 0))
+    pick = jnp.where(along == natural, 1.0, 0.0).astype(BF16)
+    x = edge_column(iota((slots, 8), 1)) - left
+    rim_weight = jnp.where((x >= 0) & (x < SX), jnp.minimum(jnp.minimum(x + 1, SX - x), ramp), 0)
+    rim_weight = rim_weight.astype(F32).astype(BF16)
+    rim_total = lax.dot_general(rim_weight, weight_y, over_rows, preferred_element_type=F32)
     right_rows = []
     left_rows = []
     down_rows = []
@@ -245,9 +255,11 @@
         )
         value = ordered / total
         joined[z] = value
+        over_lanes = (((1,), (1,)), ((), ()))
         columns_as_rows = lax.dot_general(
-            pick, value, (((1,), (1,)), ((), ())), precision=EXACT, preferred_element_type=F32
-        )
+            pick, coarse, over_lanes, preferred_element_type=F32
+        ) + lax.dot_general(pick, fine, over_lanes, preferred_element_type=F32)
+        columns_as_rows = columns_as_rows / rim_total
         own_columns[8 * z : 8 * z + 8, :] = columns_as_rows
         right_rows.append(columns_as_rows[2:4])
         left_rows.append(columns_as_rows[4:5])
@@ -313,7 +325,7 @@
     )
 
 
-def two_blocks(wide, blocks, keep, first, second, bias, out, coarse_h, fine_h, top_outside=None):
+def two_blocks(wide, blocks, keep, first, second, bias, out, coarse_h, fine_h, keep_top=None):
     ones = jnp.ones((16, 256), BF16)
     for group in range(3):
         coarse = [wide[group + dx, z][0] for dx in range(3) for z in range(BZ)]
@@ -323,18 +335,12 @@
         hidden = jnp.maximum(hidden, 0.0)
         if group == 0 and keep is not None:
             hidden = hidden * keep
+        if keep_top is not None:
+            top = C1 * BZ
+            hidden = jnp.concatenate([hidden[:top] * keep_top, hidden[top:]], axis=0)
         coarse, fine = split_kernel(hidden)
         coarse_h[group * HID : (group + 1) * HID, :] = coarse
         fine_h[group * HID : (group + 1) * HID, :] = fine
-    if top_outside is not None:
-
-        @pl.when(top_outside)
-        def _():
-            for group in range(3):
-                for scratch in (coarse_h, fine_h):
-                    nothing = jnp.zeros((C1 * BZ, HALF), BF16)
-                    scratch[group * HID : group * HID + C1 * BZ, :HALF] = nothing
-
     both = jnp.dot(second[...], coarse_h[...], preferred_element_type=F32)
     rest = jnp.dot(second[:OUTM, :], fine_h[...], preferred_element_type=F32)
     result = both[:OUTM] + both[OUTM:] + rest
@@ -420,16 +426,15 @@
     from_above = halo[-1, 0]
     from_below = halo[1, 0]
 
-    pick_row = iota((8, HALF), 0)
-    pick_lane = iota((8, HALF), 1)
     tall_lane = iota((2 * WIN, HALF), 1)
-
-    def column(message, row, lane_at):
-        chosen = jnp.where((pick_row == row) & (pick_lane == lane_at), 1.0, 0.0)
-        ends = jnp.concatenate([message[:, :WIN], message[:, SROW - WIN : SROW]], axis=1)
-        return lax.dot_general(
-            ends, chosen, (((0,), (0,)), ((), ())), precision=EXACT, preferred_element_type=F32
-        )
+    sides = jnp.concatenate([from_left[:4], from_right[:4]], axis=0)
+    ends = jnp.concatenate(
+        [sides[:, :WIN], sides[:, SROW - WIN : SROW], jnp.zeros((8, 128 - 2 * WIN), F32)], axis=1
+    )
+    side_columns = jnp.transpose(ends)[: 2 * WIN]
+
+    def column(row):
+        return side_columns[:, row : row + 1]
 
     wide = {}
     for z in range(BZ):
@@ -448,35 +453,36 @@
             halves.append(jnp.concatenate(ends, axis=0))
         even, odd = halves
         parts = (
-            jnp.where(tall_lane == 0, column(from_left, 2 * z, 0), pltpu.roll(even, 1, 1)),
-            jnp.where(tall_lane == 0, column(from_left, 2 * z + 1, 0), pltpu.roll(odd, 1, 1)),
+            jnp.where(tall_lane == 0, column(2 * z), pltpu.roll(even, 1, 1)),
+            jnp.where(tall_lane == 0, column(2 * z + 1), pltpu.roll(odd, 1, 1)),
             even,
             odd,
             jnp.where(
-                tall_lane == HALF - 1, column(from_right, z, HALF - 1), pltpu.roll(even, HALF - 1, 1)
+                tall_lane == HALF - 1, column(4 + z), pltpu.roll(even, HALF - 1, 1)
             ),
         )
         for j, part in enumerate(parts):
             wide[j, z] = split_kernel(jnp.concatenate([part[:WIN], part[WIN:]], axis=1))
 
-    pick = pick_columns()
     left_rows = []
     right_rows = []
+    cut = []
     for z in range(BZ):
-        cut = [
-            jnp.concatenate([from_above[4 * z + c : 4 * z + c + 1], from_above[4 * z + 2 + c : 4 * z + 3 + c]], axis=1)
-            for c in range(2)
-        ]
+        for c in range(2):
+            at = 4 * z + c
+            cut.append(jnp.concatenate([from_above[at : at + 1], from_above[at + 2 : at + 3]], axis=1))
         cut.append(jnp.concatenate([from_below[2 * z : 2 * z + 1], from_below[2 * z + 1 : 2 * z + 2]], axis=1))
         cut.append(jnp.zeros((5, COLS), F32))
-        outer = lax.dot_general(
-            pick,
-            jnp.concatenate(cut, axis=0),
-            (((1,), (1,)), ((), ())),
-            precision=EXACT,
-            preferred_element_type=F32,
-        )
-        outer = jnp.concatenate([outer, jnp.zeros((8, 256 - 8), F32)], axis=1)
+    outer_all = lax.dot_general(
+        pick_columns(),
+        jnp.concatenate(cut, axis=0),
+        (((1,), (1,)), ((), ())),
+        precision=EXACT,
+        preferred_element_type=F32,
+    )
+    outer_all = jnp.concatenate([outer_all, jnp.zeros((8, 256 - 8 * BZ), F32)], axis=1)
+    for z in range(BZ):
+        outer = pltpu.roll(outer_all, 256 - 8 * z, 1) if z else outer_all
         here = jnp.concatenate([own_columns[8 * z : 8 * z + 8, :], jnp.zeros((8, BY), F32)], axis=1)
         own = jnp.where(
             wide_lane < TOP,
@@ -498,23 +504,31 @@
     def reach(values):
         return jnp.concatenate([values] + [pltpu.roll(values, 512 - dy, 1) for dy in (1, 2)], axis=0)
 
-    hidden = jnp.dot(first_rim[...], reach(both), precision=EXACT, preferred_element_type=F32)
+    def product(table, values):
+        coarse, fine = split_kernel(reach(values))
+        stacked = jnp.concatenate([coarse, fine, coarse], axis=0)
+        return jnp.dot(table[...], stacked, preferred_element_type=F32)
+
+    hidden = product(first_rim, both)
     hidden = jnp.maximum(hidden, 0.0)
     lane = iota((3 * C1 * BZ, 512), 1)
     depth = iota((3 * C1 * BZ, 512), 0)
     outside = no_row & ((lane & 255) == 0)
     outside = outside | (no_col & (lane < 256) & (depth < C1 * BZ))
     hidden = jnp.where(outside, 0.0, hidden)
-    found = jnp.dot(second_rim[...], reach(hidden), precision=EXACT, preferred_element_type=F32)
-    every = jnp.where(iota((BY // 2, 256), 1) == 2 * iota((BY // 2, 256), 0), 1.0, 0.0)
+    found = product(second_rim, hidden)
+    every = jnp.where(iota((BY // 2, 256), 1) == 2 * iota((BY // 2, 256), 0), 1.0, 0.0).astype(BF16)
+    parts = []
+    for side in range(2):
+        parts += split_kernel(found[:, side * 256 : (side + 1) * 256] + bias[:, :1])
+    turned = lax.dot_general(
+        every,
+        jnp.concatenate(parts, axis=0),
+        (((1,), (1,)), ((), ())),
+        preferred_element_type=F32,
+    )
     columns = [
-        lax.dot_general(
-            every,
-            found[:, side * 256 : (side + 1) * 256] + bias[:, :1],
-            (((1,), (1,)), ((), ())),
-            precision=EXACT,
-            preferred_element_type=F32,
-        )
+        turned[:, 2 * side * C2 : (2 * side + 1) * C2] + turned[:, (2 * side + 1) * C2 : (2 * side + 2) * C2]
         for side in range(2)
     ]
     out_lane = iota((BY // 2, HALF), 1)
@@ -525,8 +539,9 @@
         out[at : at + BY // 2, :] = jnp.where(out_lane == HALF - 1, columns[1][:, o : o + 1], values)
 
     keep = jnp.where(no_col & ((iota((1, 256), 1) & (HALF - 1)) == 0), 0.0, 1.0)
+    keep_top = jnp.where(no_row & (iota((1, 256), 1) < HALF), 0.0, 1.0)
     two_blocks(
-        wide, (0, BLOCKS - 1), keep, first, second, bias, out, coarse_h, fine_h, top_outside=no_row
+        wide, (0, BLOCKS - 1), keep, first, second, bias, out, coarse_h, fine_h, keep_top=keep_top
     )
 
 
@@ -556,7 +571,12 @@
     table = table + bias1[None, :, None, None, None, None] * jnp.asarray(ones)
     first = table.reshape(3 * C1 * BZ, 3 * BZ * 8)
     second = jnp.transpose(weight2[:, :, 1:3], (0, 3, 4, 1, 2)).reshape(C2, 9 * C1 * BZ)
-    return first, second
+
+    def stacked(values):
+        coarse, fine = split_host(values)
+        return jnp.concatenate([coarse, coarse, fine], axis=1)
+
+    return stacked(first), stacked(second)
 
 
 def first_table(weight, bias):

time: 58.6 us -> 57.5 us (0.981)
  waiting for transfers between devices: 20.3 us -> 17 us
  local copies, waits for them, and re-layouts: 4.51 us -> 6.61 us
  Pallas kernels: 16.7 us -> 15.6 us
  matrix products: 4.05 us -> 4.96 us
    all_to_all x1, waiting for transfers between devices: 18 us -> 14.1 us  [body(): lax.all_to_all(outgoing, axes, split_axis=0, concat_axis=0, tiled=True)]
    pallas_call x1, Pallas kernels: 4.47 us -> 3.53 us  [rim(): pl.pallas_call(lambda *refs: rim_body(grid, *refs), in_specs=[pl.BlockSpe...]
    dot_general x1, matrix products: 1.02 us -> 1.93 us  [first_table(): jnp.einsum('czpyx,iys->iczxps', planes, jnp.asarray(reach), precision=EXACT)]
    reshape x2, local copies, waits for them, and re-layouts: 0.94 us -> 1.71 us  [second_table(): coarse, fine = split_host(table.reshape(OUTM, K2))]
    all_to_all x1, waiting for transfers between devices: 2.27 us -> 2.98 us  [body(): lax.all_to_all(messages, axes, split_axis=0, concat_axis=0, tiled=True)]
    unnamed x20 -> x28, local copies, waits for them, and re-layouts: 0.14 us -> 0.81 us
    reshape x1, local copies, waits for them, and re-layouts: 0.56 us -> 1.22 us  [first_table(): coarse, fine = split_host(table.reshape(HID, K1))]
  transfers between devices with their start and end apart: 2 -> 2, of which waited for: 2 -> 2; matrix products, arithmetic and copies ran while one was open for 17% -> 23% of each run, Pallas kernels for 8% -> 8%
where the time goes in v5:
time: 57.5 us; the launch traced here: 57.1 us
  waiting for transfers between devices  17 us (30%)
  Pallas kernels  15.6 us (27%)
  starting transfers between devices  11.1 us (19%)
  local copies, waits for them, and re-layouts  6.61 us (11%)
  matrix products  4.96 us (9%)
  other arithmetic  1.53 us (3%)
    all_to_all x1, waiting for transfers between devices, body(): lax.all_to_all(outgoing, axes, split_axis=0, concat_axis=0, tiled=True)  14.1 us
    all_to_all x1, starting transfers between devices, body(): lax.all_to_all(outgoing, axes, split_axis=0, concat_axis=0, tiled=True)  7.3 us
    pallas_call x1, Pallas kernels, inner(): pl.pallas_call(inner_body, in_specs=[vmem] * 4, out_specs=vmem, out_shape...  4.58 us
    pallas_call x1, Pallas kernels, join(): pl.pallas_call(lambda *refs: join_body(per_pair, grid, *refs), in_specs=[...  4.29 us
    all_to_all x1, starting transfers between devices, body(): lax.all_to_all(messages, axes, split_axis=0, concat_axis=0, tiled=True)  3.81 us
    pallas_call x1, Pallas kernels, rim(): pl.pallas_call(lambda *refs: rim_body(grid, *refs), in_specs=[pl.BlockSpe...  3.53 us
    pallas_call x1, Pallas kernels, pack(): pl.pallas_call(lambda *refs: pack_body(per_pair, *refs), in_specs=[pl.Blo...  3.17 us
    all_to_all x1, waiting for transfers between devices, body(): lax.all_to_all(messages, axes, split_axis=0, concat_axis=0, tiled=True)  2.98 us
  transfers between devices with their start and end apart: 2, of which 2 were waited for; matrix products, arithmetic and copies ran while one was open for 23% of the time, Pallas kernels for 8%

profile of v5, /device:TPU:0, one launch (start us, length us, event | category | flops | bytes accessed | tf_op | source)
XLA Modules:
  0.0 57.1 jit_solution(13478723662133866973)
XLA Ops:
  0.0 3.2 %pack.1 = f32[1056,2,128]{2,1,0:T(2,128)} custom-call(s32[8,64]{1,0:T(8,128)} %bitcast.58, s32[8,64]{1,0:T(8,128)} %bitcast.59, f32[1024,2,128]{2,1,0:T(2,128)} %bitcast.54), custom_call_target="tpu_custom_call" | custom-call | tf_op jit(solution)/shard_map/pack/pallas_call | solution.py:122
  3.2 0.0 copy-start.8
  3.2 7.3 %all-to-all-start = ((f32[1056,2,128]{2,1,0:T(2,128)}), f32[1056,2,128]{2,1,0:T(2,128)S(1)}, u32[]{:S(2)}, u32[]{:S(2)}) async-start(f32[1056,2,128]{2,1,0:T(2,128)} %pack.1), calls=%async_computation | async-start | bytes 2162688 | tf_op jit(solution)/shard_map/all_to_all | solution.py:621
  10.5 0.0 copy-done.7
  10.5 0.0 copy-done.5
  10.6 0.0 copy-start.6
  10.6 0.0 copy-done.8
  10.6 2.7 %convolution_bitcast_fusion = f32[4,32,3,9,16,2]{1,3,2,5,4,0:T(8,128)S(1)} fusion(f32[4,3,9,1,1,1]{2,1,5,4,3,0:T(4,128)S(1)} %copy-done.8, f32[32,16,2,3,3]{0,1,4,3,2:T(8,128)S(1)} %slice.14), kind=kOutput, calls=%fused_computation | convolution fusion | flops 3981312 | bytes 479664 | tf_op jit(solution)/shard_map/oczyx,iyh->ioxhcz/dot_general | solution.py:605
  13.3 0.0 copy-done.6
  13.3 1.9 %convolution_bitcast_fusion.1 = f32[9,16,2,3,2,16]{5,1,0,3,4,2:T(8,128)} fusion(f32[9,3,16,1,1,1]{2,1,0,5,4,3:T(4,128)S(1)} %copy-done.6, f32[16,1,2,3,3]{0,3,4,2,1:T(4,128)S(1)} %get-tuple-element.20, f32[16,1,2,3,3]{0,3,4,2,1:T(4,128)S(1)} %get-tuple-element.19), kind=kOutput, calls=%fused_computation.1 | convolution fusion | flops 995904 | bytes 114624 | tf_op jit(solution)/shard_map/czpyx,iys->iczxps/dot_general | solution.py:589
  15.3 1.1 %copy.50 = f32[4,32,3,9,16,2]{1,0,5,4,3,2:T(4,128)S(1)} copy(f32[4,32,3,9,16,2]{1,3,2,5,4,0:T(8,128)S(1)} %convolution_bitcast_fusion) | data formatting | bytes 884736 | tf_op jit(solution)/shard_map/oczyx,iyh->ioxhcz/transpose | solution.py:605
  16.4 0.0 copy-start.11
  16.4 0.7 %reshape.74 = f32[128,864]{0,1:T(8,128)S(1)} reshape(f32[4,32,3,9,16,2]{1,0,5,4,3,2:T(4,128)S(1)} %copy.50) | data formatting | bytes 884736 | tf_op jit(solution)/shard_map/reshape | solution.py:606
  17.2 0.0 copy-start
  17.2 0.8 %reduce_precision.47 = f32[128,864]{0,1:T(8,128)} reduce-precision(f32[128,864]{0,1:T(8,128)S(1)} %reshape.74), exponent_bits=8, mantissa_bits=7 | non-fusion elementwise | flops 110592 | bytes 884736 | tf_op jit(solution)/shard_map/reduce_precision | solution.py:49
  18.0 1.0 %copy.52 = f32[128,864]{1,0:T(8,128)} copy(f32[128,864]{0,1:T(8,128)S(1)} %reshape.74) | data formatting | bytes 884736 | tf_op jit(solution)/shard_map/reshape | solution.py:606
  19.0 0.7 %copy.74 = f32[32,16,2,3,3]{0,3,4,2,1:T(4,128)} copy(f32[32,16,2,3,3]{0,1,4,3,2:T(8,128)S(1)} %slice.14) | data formatting | bytes 73728
  19.7 0.0 copy-done.11
  19.7 0.1 broadcast_in_dim.4
  19.8 0.1 tile.10
  19.9 0.1 tile.12
  20.0 0.0 copy-done
  20.0 0.5 copy.47
  20.5 0.0 copy-start.3
  20.5 1.2 %reshape.73 = f32[288,96]{1,0:T(8,128)} reshape(f32[9,16,2,3,2,16]{5,4,3,2,1,0:T(2,128)S(1)} %copy.47) | data formatting | bytes 221184 | tf_op jit(solution)/shard_map/reshape | solution.py:590
  21.7 0.0 copy-done.2
  21.7 0.2 copy.51
  21.9 0.1 broadcast_multiply_fusion
  22.0 0.3 fusion
  22.3 0.2 copy.55
  22.5 0.2 reshape.75
  22.8 0.1 copy.56
  22.8 0.1 copy.57
  22.9 0.1 pad_add_fusion.refs_0_
  23.0 0.1 pad_maximum_fusion.2.refs_8_
  23.2 0.1 pad_maximum_fusion.1.refs_9_
  23.3 0.0 copy-done.4
  23.3 0.0 copy-done.1
  23.3 0.1 fusion.11
  23.4 14.1 %all-to-all-done = f32[1056,2,128]{2,1,0:T(2,128)S(1)} async-done(((f32[1056,2,128]{2,1,0:T(2,128)}), f32[1056,2,128]{2,1,0:T(2,128)S(1)}, u32[]{:S(2)}, u32[]{:S(2)}) %all-to-all-start) | async-done | bytes 1081376 | tf_op jit(solution)/shard_map/all_to_all | solution.py:621
  37.4 4.3 %join.1 = (f32[2,128,256]{2,1,0:T(8,128)S(1)}, f32[32,8,128]{2,1,0:T(8,128)}, f32[16,128]{1,0:T(8,128)S(1)}) custom-call(s32[2]{0:T(128)S(1)} %pad_add_fusion.refs_0_, f32[32,33,2,128]{3,2,1,0:T(2,128)S(1)} %bitcast.52, f32[2112,128]{1,0:T(8,128)S(1)} %bitcast.53), custom_call_target="tpu_custom_call" | custom-call | tf_op jit(solution)/shard_map/join/pallas_call | solution.py:304
  41.7 3.8 %all-to-all-start.1 = ((f32[32,8,128]{2,1,0:T(8,128)}), f32[32,8,128]{2,1,0:T(8,128)S(1)}, u32[]{:S(2)}, u32[]{:S(2)}) async-start(f32[32,8,128]{2,1,0:T(8,128)} %get-tuple-element.9), calls=%async_computation.1 | async-start | bytes 262144 | tf_op jit(solution)/shard_map/all_to_all | solution.py:627
  45.6 0.1 copy.48
  45.7 0.2 fusion.2.first.refs_5_
  46.0 0.1 broadcast_in_dim.5.bias.refs_7_
  46.0 4.6 %inner.1.refs_4_ = f32[2048,128]{1,0:T(8,128)S(1)} custom-call(f32[2,128,256]{2,1,0:T(8,128)S(1)} %get-tuple-element.8.joined.refs_1_, bf16[288,304]{1,0:T(8,128)(2,1)S(1)} %fusion.2.first.refs_5_, bf16[256,864]{1,0:T(8,128)(2,1)S(1)} %pad_maximum_fusion.second.refs_6_, f32[32,128]{1,0:T(8,128)S(1)} %broadcast_in_dim.5.bias.refs_7_), custom_call_target="tpu_custom_call" | custom-call | tf_op jit(solution)/shard_map/inner/pallas_call | solution.py:377
  50.6 3.0 %all-to-all-done.1.refs_2_ = f32[32,8,128]{2,1,0:T(8,128)S(1)} async-done(((f32[32,8,128]{2,1,0:T(8,128)}), f32[32,8,128]{2,1,0:T(8,128)S(1)}, u32[]{:S(2)}, u32[]{:S(2)}) %all-to-all-start.1) | async-done | bytes 131104 | tf_op jit(solution)/shard_map/all_to_all | solution.py:627
  53.6 3.5 %rim.1 = f32[2048,128]{1,0:T(8,128)} custom-call(s32[2]{0:T(128)S(1)} %pad_add_fusion.refs_0_, f32[2,128,256]{2,1,0:T(8,128)S(1)} %get-tuple-element.8.joined.refs_1_, f32[32,8,128]{2,1,0:T(8,128)S(1)} %all-to-all-done.1.refs_2_, f32[16,128]{1,0:T(8,128)S(1)} %get-tuple-element.10.refs_3_, f32[2048,128]{1,0:T(8,128)S(1)} %inner.1.refs_4_, ...), custom_call_target="tpu_custom_call" | custom-call | tf_op jit(solution)/shard_map/rim/pallas_call | solution.py:550
  (23 shorter events, 0.2 us)
Async XLA Ops:
  0.0 10.5 %copy-start.7 = (f32[16,1,3,3,3]{0,1,4,3,2:T(1,128)S(1)}, f32[16,1,3,3,3]{0,1,4,3,2:T(1,128)}, u32[]{:S(2)}) copy-start(f32[16,1,3,3,3]{0,1,4,3,2:T(1,128)} %param.12) | copy-start | bytes 5188
  0.0 10.5 %copy-start.5 = (f32[32,16,3,3,3]{0,1,4,3,2:T(8,128)S(1)}, f32[32,16,3,3,3]{0,1,4,3,2:T(8,128)}, u32[]{:S(2)}) copy-start(f32[32,16,3,3,3]{0,1,4,3,2:T(8,128)} %param.14) | copy-start | bytes 165892
  3.2 7.4 %copy-start.8 = (f32[4,3,9,1,1,1]{2,1,5,4,3,0:T(4,128)S(1)}, f32[4,3,9,1,1,1]{2,1,5,4,3,0:T(4,128)}, u32[]{:S(2)}) copy-start(f32[4,3,9,1,1,1]{2,1,5,4,3,0:T(4,128)} %constant.27) | copy-start | bytes 1300
  3.2 34.2 %all-to-all-start = ((f32[1056,2,128]{2,1,0:T(2,128)}), f32[1056,2,128]{2,1,0:T(2,128)S(1)}, u32[]{:S(2)}, u32[]{:S(2)}) async-start(f32[1056,2,128]{2,1,0:T(2,128)} %pack.1), calls=%async_computation | async-start | bytes 2162688 | tf_op jit(solution)/shard_map/all_to_all | solution.py:621
  10.6 2.8 %copy-start.6 = (f32[9,3,16,1,1,1]{2,1,0,5,4,3:T(4,128)S(1)}, f32[9,3,16,1,1,1]{2,1,0,5,4,3:T(4,128)}, u32[]{:S(2)}) copy-start(f32[9,3,16,1,1,1]{2,1,0,5,4,3:T(4,128)} %constant.26) | copy-start | bytes 5188
  16.4 3.3 %copy-start.11 = (f32[16]{0:T(128)S(1)}, f32[16]{0:T(128)}, u32[]{:S(2)}) copy-start(f32[16]{0:T(128)} %param.13) | copy-start | bytes 196
  17.2 2.8 %copy-start = (f32[9,16,2,3,2,16]{5,1,0,3,4,2:T(8,128)S(1)}, f32[9,16,2,3,2,16]{5,1,0,3,4,2:T(8,128)}, u32[]{:S(2)}) copy-start(f32[9,16,2,3,2,16]{5,1,0,3,4,2:T(8,128)} %convolution_bitcast_fusion.1) | copy-start | bytes 331780
  19.0 2.7 %copy-start.2 = (f32[128,864]{0,1:T(8,128)S(1)}, f32[128,864]{0,1:T(8,128)}, u32[]{:S(2)}) copy-start(f32[128,864]{0,1:T(8,128)} %reduce_precision.47) | copy-start | bytes 1327108
  20.0 1.9 %copy-start.10 = (f32[3,2,8]{2,0,1:T(4,128)S(1)}, f32[3,2,8]{2,0,1:T(4,128)}, u32[]{:S(2)}) copy-start(f32[3,2,8]{2,0,1:T(4,128)} %constant.23.clone) | copy-start | bytes 580
  20.0 2.0 %copy-start.9 = (f32[3,3,8,1,1,1]{2,1,0,5,4,3:T(4,128)S(1)}, f32[3,3,8,1,1,1]{2,1,0,5,4,3:T(4,128)}, u32[]{:S(2)}) copy-start(f32[3,3,8,1,1,1]{2,1,0,5,4,3:T(4,128)} %constant.28) | copy-start | bytes 868
  20.5 2.3 %copy-start.3 = (f32[32,16,2,3,3]{0,3,4,2,1:T(4,128)S(1)}, f32[32,16,2,3,3]{0,3,4,2,1:T(4,128)}, u32[]{:S(2)}) copy-start(f32[32,16,2,3,3]{0,3,4,2,1:T(4,128)} %copy.74) | copy-start | bytes 110596
  21.7 1.6 %copy-start.4 = (f32[288,96]{1,0:T(8,128)S(1)}, f32[288,96]{1,0:T(8,128)}, u32[]{:S(2)}) copy-start(f32[288,96]{1,0:T(8,128)} %reshape.73) | copy-start | bytes 331780
  21.7 1.6 %copy-start.1 = (f32[128,864]{1,0:T(8,128)S(1)}, f32[128,864]{1,0:T(8,128)}, u32[]{:S(2)}) copy-start(f32[128,864]{1,0:T(8,128)} %copy.52) | copy-start | bytes 1327108
  37.4 8.5 %copy-start.12 = (f32[32]{0:T(128)S(1)}, f32[32]{0:T(128)}, u32[]{:S(2)}) copy-start(f32[32]{0:T(128)} %param.15) | copy-start | bytes 388
  41.7 11.9 %all-to-all-start.1 = ((f32[32,8,128]{2,1,0:T(8,128)}), f32[32,8,128]{2,1,0:T(8,128)S(1)}, u32[]{:S(2)}, u32[]{:S(2)}) async-start(f32[32,8,128]{2,1,0:T(8,128)} %get-tuple-element.9), calls=%async_computation.1 | async-start | bytes 262144 | tf_op jit(solution)/shard_map/all_to_all | solution.py:627

commit v6 on v5

--- a/solution.py
+++ b/solution.py
@@ -54,6 +54,25 @@
     return BZ * SY // 2 * per_pair + 1
 
 
+def sent_routes(per_pair, senders, route_rows):
+    held = route_rows.shape[1]
+    match = (route_rows[0:1, :] == iota((senders, held), 0)) & (route_rows[1:2, :] == 1)
+    flags = jnp.where(match, 1.0, 0.0)
+    before = jnp.where(iota((held, held), 0) < iota((held, held), 1), 1.0, 0.0)
+    earlier = jnp.dot(flags.astype(BF16), before.astype(BF16), preferred_element_type=F32)
+    fields = jnp.concatenate([route_rows[...].astype(F32), jnp.zeros((120, held), F32)], axis=0)
+    fields = fields.astype(BF16)
+    return [
+        lax.dot_general(
+            jnp.where(match & (earlier == float(r)), 1.0, 0.0).astype(BF16),
+            fields,
+            (((1,), (1,)), ((), ())),
+            preferred_element_type=F32,
+        )
+        for r in range(per_pair)
+    ]
+
+
 def pack_body(per_pair, routes, route_rows, strips, payload, count, sems):
     pairs = BZ * SY // 2
     chunk = chunk_of(per_pair)
@@ -89,19 +108,9 @@
 
     lax.fori_loop(0, held, place, 0, unroll=8)
 
-    match = (route_rows[0:1, :] == iota((senders, held), 0)) & (route_rows[1:2, :] == 1)
-    flags = jnp.where(match, 1.0, 0.0)
-    before = jnp.where(iota((held, held), 0) < iota((held, held), 1), 1.0, 0.0)
-    earlier = jnp.dot(flags.astype(BF16), before.astype(BF16), preferred_element_type=F32)
-    fields = jnp.concatenate([route_rows[...].astype(F32), jnp.zeros((120, held), F32)], axis=0)
-    fields = fields.astype(BF16)
-    for r in range(per_pair):
-        chosen = jnp.where(match & (earlier == float(r)), 1.0, 0.0).astype(BF16)
-        sent = lax.dot_general(
-            chosen, fields, (((1,), (1,)), ((), ())), preferred_element_type=F32
-        )
+    for r, rows in enumerate(sent_routes(per_pair, senders, route_rows)):
         for dest in range(senders):
-            payload[dest * chunk + chunk - 1, r : r + 1, :] = sent[dest : dest + 1, :]
+            payload[dest * chunk + chunk - 1, r : r + 1, :] = rows[dest : dest + 1, :]
 
     if full:
         everything = held * pairs
@@ -115,8 +124,78 @@
         lax.fori_loop(0, held, finish, 0)
 
 
+def pack_full_body(per_pair, routes, route_rows, strips, payload, buffer, sent, count, sems_in, sems_out):
+    pairs = BZ * SY // 2
+    senders = payload.shape[0]
+    held = senders * per_pair
+    groups = sems_in.shape[0]
+    per_group = senders // groups
+
+    def fetch(g):
+        at = pl.ds(g * per_group, per_group)
+        return pltpu.make_async_copy(strips.at[at], buffer.at[at], sems_in.at[g])
+
+    for g in range(groups):
+        fetch(g).start()
+
+    def clear(i, carry):
+        count[i] = 0
+        return carry
+
+    lax.fori_loop(0, senders, clear, 0, unroll=8)
+    for r, rows in enumerate(sent_routes(per_pair, senders, route_rows)):
+        for dest in range(senders):
+            sent[dest, r : r + 1, :] = rows[dest : dest + 1, :]
+    tail = pltpu.make_async_copy(sent, payload.at[:, per_pair * pairs], sems_out.at[0])
+    tail.start()
+
+    def place(row, carry):
+        for r in range(per_pair):
+            dest = routes[0, row * per_pair + r]
+            rank = jnp.minimum(count[dest], per_pair - 1)
+            count[dest] = rank + 1
+            pltpu.make_async_copy(
+                buffer.at[row, pl.ds(r * pairs, pairs)],
+                payload.at[dest, pl.ds(rank * pairs, pairs)],
+                sems_out.at[1],
+            ).start()
+        return carry
+
+    for g in range(groups):
+        fetch(g).wait()
+        lax.fori_loop(g * per_group, (g + 1) * per_group, place, 0, unroll=4)
+    tail.wait()
+    pltpu.make_async_copy(buffer, payload.at[:, pl.ds(0, per_pair * pairs)], sems_out.at[1]).wait()
+
+
+def pack_full(strips, routes_t, senders, per_pair):
+    pairs = BZ * SY // 2
+    strips = strips.reshape(senders, per_pair * pairs, 2, SX)
+    payload = pl.pallas_call(
+        lambda *refs: pack_full_body(per_pair, *refs),
+        in_specs=[
+            pl.BlockSpec(memory_space=pltpu.SMEM),
+            pl.BlockSpec(memory_space=pltpu.VMEM),
+            pl.BlockSpec(memory_space=pl.ANY),
+        ],
+        out_specs=pl.BlockSpec(memory_space=pl.ANY),
+        out_shape=jax.ShapeDtypeStruct((senders, chunk_of(per_pair), 2, SX), F32),
+        scratch_shapes=[
+            pltpu.VMEM(strips.shape, F32),
+            pltpu.VMEM((senders, 2, SX), F32),
+            pltpu.SMEM((senders,), jnp.int32),
+            pltpu.SemaphoreType.DMA((4,)),
+            pltpu.SemaphoreType.DMA((2,)),
+        ],
+        name="pack",
+    )(routes_t, routes_t, strips)
+    return payload.reshape(senders * chunk_of(per_pair), 2, SX)
+
+
 def pack(strips, routes_t, senders, per_pair):
     held = strips.shape[0]
+    if held == STRIPS and held == senders * per_pair and per_pair == 2 and senders % 16 == 0:
+        return pack_full(strips, routes_t, senders, per_pair)
     pairs = BZ * SY // 2
     vmem = pl.BlockSpec(memory_space=pltpu.VMEM)
     return pl.pallas_call(
@@ -153,7 +232,7 @@
     return jnp.where(chosen, 1.0, 0.0)
 
 
-def join_body(per_pair, grid, edge, routes, strips, joined, messages, own_columns, data, place_y, params, sem):
+def join_body(per_pair, grid, edge, routes, strips, joined, messages, own_columns, data, place_y, pieces, route_rows, params, sem):
     senders = routes.shape[0]
     slots = senders * per_pair
     chunk = 2 * chunk_of(per_pair)
@@ -161,7 +240,9 @@
     fetch.start()
     columns = jnp.concatenate(
         [strips[pl.ds(chunk - 2 + r, senders, stride=chunk), :] for r in range(per_pair)], axis=0
-    ).astype(jnp.int32)
+    )
+    route_rows[...] = columns
+    columns = columns.astype(jnp.int32)
 
     def field(q):
         return columns[:, q : q + 1]
@@ -179,57 +260,74 @@
     weight_x = weight_x.astype(F32).astype(BF16)
     over_rows = (((0,), (0,)), ((), ()))
     total = lax.dot_general(weight_y, weight_x, over_rows, preferred_element_type=F32)
+    lane = iota((8, SX), 1)
+    row_lane = iota((8, BY), 1)
+    row_sub = iota((SY, BY), 0)
+    to_edge = jnp.minimum(lane + 1, SX - lane).astype(F32)
+
+    def twice(values):
+        return jnp.concatenate([values, values], axis=0)
+
+    def prepare(group, carry):
+        blocks = [
+            route_rows[pl.ds(pl.multiple_of(r * senders + 8 * group, 8), 8), :] for r in range(per_pair)
+        ]
+        for inside, r in [(i, r) for i in range(8) for r in range(per_pair)]:
+            h = 8 * group + inside
+            k = h * per_pair + r
+            route = blocks[r][inside : inside + 1, :]
+
+            def value(q):
+                return jnp.broadcast_to(route[:, q : q + 1], (8, SX))
+
+            frac_z = twice(value(4) * (1.0 / 16.0))
+            frac_y = value(5) * (1.0 / 16.0)
+            frac_x = value(6) * (1.0 / 16.0)
+            ramp = value(7)
+            weight = jnp.minimum(to_edge, ramp)
+            here = twice(weight * (1.0 - frac_x))
+            there = twice(jnp.where(lane < SX - 1, weight * frac_x, 0.0))
+            at = h * chunk + r * BZ * SY
+            first = strips[pl.ds(at, SY), :]
+            second = strips[pl.ds(at + SY, SY), :]
+            if slots != STRIPS:
+                live = twice(value(1)) == 1.0
+                first = jnp.where(live, first, 0.0)
+                second = jnp.where(live, second, 0.0)
+            plane0 = (1.0 - frac_z) * first + frac_z * second
+            plane1 = (1.0 - frac_z) * second
+            for z, plane in enumerate((plane0, plane1)):
+                pieces[k, z * SY : (z + 1) * SY, :] = here * plane + there * pltpu.roll(plane, SX - 1, 1)
+            y = row_lane - value(2).astype(jnp.int32)
+            weight_y = jnp.minimum(jnp.minimum(y + 1, SY - y).astype(F32), ramp)
+            stay_y = twice(weight_y * (1.0 - frac_y))
+            move_y = twice(weight_y * frac_y)
+            ahead = row_sub - twice(y)
+            spread = jnp.where(ahead == 0, stay_y, jnp.where(ahead == 1, move_y, 0.0))
+            place_y[pl.ds(k * SY, SY), :] = spread.astype(BF16)
+        return carry
+
+    lax.fori_loop(0, senders // 8, prepare, 0)
     fetch.wait()
-    lane = iota((SY, SX), 1)
-    row_lane = iota((SY, BY), 1)
-    row_sub = iota((SY, BY), 0)
-
-    def one(h, r):
-        k = h * per_pair + r
-        live = params[h, r, 1].astype(jnp.int32)
-        top = params[h, r, 2].astype(jnp.int32)
-        left = params[h, r, 3].astype(jnp.int32)
-        frac_z = params[h, r, 4] * (1.0 / 16.0)
-        frac_y = params[h, r, 5] * (1.0 / 16.0)
-        frac_x = params[h, r, 6] * (1.0 / 16.0)
-        ramp = params[h, r, 7].astype(jnp.int32)
-        weight = jnp.minimum(jnp.minimum(lane + 1, SX - lane), ramp).astype(F32)
-        here = weight * (1.0 - frac_x)
-        there = jnp.where(lane < SX - 1, weight * frac_x, 0.0)
-        stay_z = 1.0 - frac_z
-        move_z = frac_z
-        at = h * chunk + r * BZ * SY
-        first = strips[pl.ds(at, SY), :]
-        second = strips[pl.ds(at + SY, SY), :]
-        if slots != STRIPS:
-            first = jnp.where(live == 1, first, 0.0)
-            second = jnp.where(live == 1, second, 0.0)
-        plane0 = stay_z * first + move_z * second
-        plane1 = stay_z * second
-        shift = left & (SX - 1)
-        for z, plane in enumerate((plane0, plane1)):
-            piece = here * plane + there * pltpu.roll(plane, SX - 1, 1)
-            turned = pltpu.roll(piece, shift, 1)
-            low = jnp.where(lane >= left, turned, 0.0)
-            high = jnp.where(lane < left, turned, 0.0)
-            for side, part in enumerate((low, high)):
-                coarse, fine = split_kernel(part)
-                at = z * COLS + side * SX
-                data[pl.ds(k * SY, SY), at : at + SX] = coarse
-                data[pl.ds(k * SY, SY), BZ * COLS + at : BZ * COLS + at + SX] = fine
-        y = row_lane - top
-        weight_y = jnp.minimum(jnp.minimum(y + 1, SY - y), ramp).astype(F32)
-        spread = jnp.where(row_sub == y, weight_y * (1.0 - frac_y), 0.0) + jnp.where(
-            row_sub == y + 1, weight_y * frac_y, 0.0
-        )
-        place_y[pl.ds(k * SY, SY), :] = spread.astype(BF16)
-
-    def holder(h, carry):
+    wide_lane = iota((SY, SX), 1)
+
+    def shift(h, carry):
         for r in range(per_pair):
-            one(h, r)
+            k = h * per_pair + r
+            left = params[h, r, 3].astype(jnp.int32)
+            low_side = wide_lane >= left
+            for z in range(BZ):
+                turned = pltpu.roll(pieces[k, z * SY : (z + 1) * SY, :], left & (SX - 1), 1)
+                low = jnp.where(low_side, turned, 0.0)
+                high = jnp.where(low_side, 0.0, turned)
+                for side, part in enumerate((low, high)):
+                    coarse, fine = split_kernel(part)
+                    at = z * COLS + side * SX
+                    data[pl.ds(k * SY, SY), at : at + SX] = coarse
+                    data[pl.ds(k * SY, SY), BZ * COLS + at : BZ * COLS + at + SX] = fine
         return carry
 
-    lax.fori_loop(0, senders, holder, 0, unroll=JOIN_UNROLL)
+    lax.fori_loop(0, senders, shift, 0, unroll=JOIN_UNROLL)
 
     sums = lax.dot_general(place_y[...], data[...], over_rows, preferred_element_type=F32)
     sums = sums[:, : BZ * COLS] + sums[:, BZ * COLS :]
@@ -313,6 +411,8 @@
         scratch_shapes=[
             pltpu.VMEM((slots * SY, 2 * BZ * COLS), BF16),
             pltpu.VMEM((slots * SY, BY), BF16),
+            pltpu.VMEM((slots, BZ * SY, SX), F32),
+            pltpu.VMEM((slots, SX), F32),
             pltpu.SMEM((senders, 2, SX), F32),
             pltpu.SemaphoreType.DMA,
         ],

time: 57.5 us -> 56.9 us (0.990)
  no operation moved by 1% of the time
where the time goes in v6:
time: 56.9 us; the launch traced here: 56.6 us
  waiting for transfers between devices  17 us (30%)
  Pallas kernels  15.1 us (27%)
  starting transfers between devices  11.1 us (20%)
  local copies, waits for them, and re-layouts  6.61 us (12%)
  matrix products  4.96 us (9%)
  other arithmetic  1.53 us (3%)
    all_to_all x1, waiting for transfers between devices, body(): lax.all_to_all(outgoing, axes, split_axis=0, concat_axis=0, tiled=True)  14.1 us
    all_to_all x1, starting transfers between devices, body(): lax.all_to_all(outgoing, axes, split_axis=0, concat_axis=0, tiled=True)  7.3 us
    pallas_call x1, Pallas kernels, inner(): pl.pallas_call(inner_body, in_specs=[vmem] * 4, out_specs=vmem, out_shape...  4.58 us
    pallas_call x1, Pallas kernels, join(): pl.pallas_call(lambda *refs: join_body(per_pair, grid, *refs), in_specs=[...  4.09 us
    all_to_all x1, starting transfers between devices, body(): lax.all_to_all(messages, axes, split_axis=0, concat_axis=0, tiled=True)  3.82 us
    pallas_call x1, Pallas kernels, rim(): pl.pallas_call(lambda *refs: rim_body(grid, *refs), in_specs=[pl.BlockSpe...  3.53 us
    all_to_all x1, waiting for transfers between devices, body(): lax.all_to_all(messages, axes, split_axis=0, concat_axis=0, tiled=True)  2.98 us
    pallas_call x1, Pallas kernels, pack_full(): pl.pallas_call(lambda *refs: pack_full_body(per_pair, *refs), in_specs=[p...  2.85 us
  transfers between devices with their start and end apart: 2, of which 2 were waited for; matrix products, arithmetic and copies ran while one was open for 23% of the time, Pallas kernels for 8%

profile of v6, /device:TPU:0, one launch (start us, length us, event | category | flops | bytes accessed | tf_op | source)
XLA Modules:
  0.0 56.6 jit_solution(266195780836474703)
XLA Ops:
  0.0 2.8 %pack.1 = f32[32,33,2,128]{3,2,1,0:T(2,128)} custom-call(s32[8,64]{1,0:T(8,128)} %bitcast.60, s32[8,64]{1,0:T(8,128)} %bitcast.61, f32[32,32,2,128]{3,2,1,0:T(2,128)} %bitcast.56), custom_call_target="tpu_custom_call" | custom-call | tf_op jit(solution)/shard_map/pack/pallas_call | solution.py:174
  2.9 0.0 copy-start.8
  2.9 7.3 %all-to-all-start = ((f32[1056,2,128]{2,1,0:T(2,128)}), f32[1056,2,128]{2,1,0:T(2,128)S(1)}, u32[]{:S(2)}, u32[]{:S(2)}) async-start(f32[1056,2,128]{2,1,0:T(2,128)} %bitcast.55), calls=%async_computation | async-start | bytes 2162688 | tf_op jit(solution)/shard_map/all_to_all | solution.py:721
  10.2 0.0 copy-done.7
  10.2 0.0 copy-done.5
  10.2 0.0 copy-start.6
  10.3 0.0 copy-done.8
  10.3 2.7 %convolution_bitcast_fusion = f32[4,32,3,9,16,2]{1,3,2,5,4,0:T(8,128)S(1)} fusion(f32[4,3,9,1,1,1]{2,1,5,4,3,0:T(4,128)S(1)} %copy-done.8, f32[32,16,2,3,3]{0,1,4,3,2:T(8,128)S(1)} %slice.14), kind=kOutput, calls=%fused_computation | convolution fusion | flops 3981312 | bytes 479664 | tf_op jit(solution)/shard_map/oczyx,iyh->ioxhcz/dot_general | solution.py:705
  13.0 0.0 copy-done.6
  13.0 1.9 %convolution_bitcast_fusion.1 = f32[9,16,2,3,2,16]{5,1,0,3,4,2:T(8,128)} fusion(f32[9,3,16,1,1,1]{2,1,0,5,4,3:T(4,128)S(1)} %copy-done.6, f32[16,1,2,3,3]{0,3,4,2,1:T(4,128)S(1)} %get-tuple-element.20, f32[16,1,2,3,3]{0,3,4,2,1:T(4,128)S(1)} %get-tuple-element.19), kind=kOutput, calls=%fused_computation.1 | convolution fusion | flops 995904 | bytes 114624 | tf_op jit(solution)/shard_map/czpyx,iys->iczxps/dot_general | solution.py:689
  14.9 1.1 %copy.50 = f32[4,32,3,9,16,2]{1,0,5,4,3,2:T(4,128)S(1)} copy(f32[4,32,3,9,16,2]{1,3,2,5,4,0:T(8,128)S(1)} %convolution_bitcast_fusion) | data formatting | bytes 884736 | tf_op jit(solution)/shard_map/oczyx,iyh->ioxhcz/transpose | solution.py:705
  16.1 0.0 copy-start.11
  16.1 0.7 %reshape.78 = f32[128,864]{0,1:T(8,128)S(1)} reshape(f32[4,32,3,9,16,2]{1,0,5,4,3,2:T(4,128)S(1)} %copy.50) | data formatting | bytes 884736 | tf_op jit(solution)/shard_map/reshape | solution.py:706
  16.8 0.0 copy-start
  16.9 0.8 %reduce_precision.47 = f32[128,864]{0,1:T(8,128)} reduce-precision(f32[128,864]{0,1:T(8,128)S(1)} %reshape.78), exponent_bits=8, mantissa_bits=7 | non-fusion elementwise | flops 110592 | bytes 884736 | tf_op jit(solution)/shard_map/reduce_precision | solution.py:49
  17.7 1.0 %copy.52 = f32[128,864]{1,0:T(8,128)} copy(f32[128,864]{0,1:T(8,128)S(1)} %reshape.78) | data formatting | bytes 884736 | tf_op jit(solution)/shard_map/reshape | solution.py:706
  18.7 0.7 %copy.74 = f32[32,16,2,3,3]{0,3,4,2,1:T(4,128)} copy(f32[32,16,2,3,3]{0,1,4,3,2:T(8,128)S(1)} %slice.14) | data formatting | bytes 73728
  19.4 0.0 copy-done.11
  19.4 0.1 broadcast_in_dim.4
  19.5 0.1 tile.10
  19.6 0.1 tile.12
  19.7 0.0 copy-done
  19.7 0.5 copy.47
  20.1 0.0 copy-start.3
  20.1 1.2 %reshape.77 = f32[288,96]{1,0:T(8,128)} reshape(f32[9,16,2,3,2,16]{5,4,3,2,1,0:T(2,128)S(1)} %copy.47) | data formatting | bytes 221184 | tf_op jit(solution)/shard_map/reshape | solution.py:690
  21.4 0.2 copy.51
  21.6 0.0 copy-done.10
  21.6 0.1 broadcast_multiply_fusion
  21.7 0.3 fusion
  22.0 0.2 copy.55
  22.2 0.2 reshape.79
  22.4 0.1 copy.56
  22.5 0.1 copy.57
  22.6 0.1 pad_add_fusion.refs_0_
  22.7 0.1 pad_maximum_fusion.2.refs_8_
  22.8 0.1 pad_maximum_fusion.1.refs_9_
  23.0 0.0 copy-done.4
  23.0 0.0 copy-done.1
  23.0 0.1 fusion.11
  23.1 14.1 %all-to-all-done = f32[1056,2,128]{2,1,0:T(2,128)S(1)} async-done(((f32[1056,2,128]{2,1,0:T(2,128)}), f32[1056,2,128]{2,1,0:T(2,128)S(1)}, u32[]{:S(2)}, u32[]{:S(2)}) %all-to-all-start) | async-done | bytes 1081376 | tf_op jit(solution)/shard_map/all_to_all | solution.py:721
  37.1 4.1 %join.1 = (f32[2,128,256]{2,1,0:T(8,128)S(1)}, f32[32,8,128]{2,1,0:T(8,128)}, f32[16,128]{1,0:T(8,128)S(1)}) custom-call(s32[2]{0:T(128)S(1)} %pad_add_fusion.refs_0_, f32[32,33,2,128]{3,2,1,0:T(2,128)S(1)} %bitcast.53, f32[2112,128]{1,0:T(8,128)S(1)} %bitcast.54), custom_call_target="tpu_custom_call" | custom-call | tf_op jit(solution)/shard_map/join/pallas_call | solution.py:402
  41.2 3.8 %all-to-all-start.1 = ((f32[32,8,128]{2,1,0:T(8,128)}), f32[32,8,128]{2,1,0:T(8,128)S(1)}, u32[]{:S(2)}, u32[]{:S(2)}) async-start(f32[32,8,128]{2,1,0:T(8,128)} %get-tuple-element.9), calls=%async_computation.1 | async-start | bytes 262144 | tf_op jit(solution)/shard_map/all_to_all | solution.py:727
  45.1 0.1 copy.48
  45.2 0.2 fusion.2.first.refs_5_
  45.5 0.1 broadcast_in_dim.5.bias.refs_7_
  45.5 4.6 %inner.1.refs_4_ = f32[2048,128]{1,0:T(8,128)S(1)} custom-call(f32[2,128,256]{2,1,0:T(8,128)S(1)} %get-tuple-element.8.joined.refs_1_, bf16[288,304]{1,0:T(8,128)(2,1)S(1)} %fusion.2.first.refs_5_, bf16[256,864]{1,0:T(8,128)(2,1)S(1)} %pad_maximum_fusion.second.refs_6_, f32[32,128]{1,0:T(8,128)S(1)} %broadcast_in_dim.5.bias.refs_7_), custom_call_target="tpu_custom_call" | custom-call | tf_op jit(solution)/shard_map/inner/pallas_call | solution.py:477
  50.1 3.0 %all-to-all-done.1.refs_2_ = f32[32,8,128]{2,1,0:T(8,128)S(1)} async-done(((f32[32,8,128]{2,1,0:T(8,128)}), f32[32,8,128]{2,1,0:T(8,128)S(1)}, u32[]{:S(2)}, u32[]{:S(2)}) %all-to-all-start.1) | async-done | bytes 131104 | tf_op jit(solution)/shard_map/all_to_all | solution.py:727
  53.1 3.5 %rim.1 = f32[2048,128]{1,0:T(8,128)} custom-call(s32[2]{0:T(128)S(1)} %pad_add_fusion.refs_0_, f32[2,128,256]{2,1,0:T(8,128)S(1)} %get-tuple-element.8.joined.refs_1_, f32[32,8,128]{2,1,0:T(8,128)S(1)} %all-to-all-done.1.refs_2_, f32[16,128]{1,0:T(8,128)S(1)} %get-tuple-element.10.refs_3_, f32[2048,128]{1,0:T(8,128)S(1)} %inner.1.refs_4_, ...), custom_call_target="tpu_custom_call" | custom-call | tf_op jit(solution)/shard_map/rim/pallas_call | solution.py:650
  (23 shorter events, 0.2 us)
Async XLA Ops:
  0.0 10.2 %copy-start.7 = (f32[16,1,3,3,3]{0,1,4,3,2:T(1,128)S(1)}, f32[16,1,3,3,3]{0,1,4,3,2:T(1,128)}, u32[]{:S(2)}) copy-start(f32[16,1,3,3,3]{0,1,4,3,2:T(1,128)} %param.12) | copy-start | bytes 5188
  0.0 10.2 %copy-start.5 = (f32[32,16,3,3,3]{0,1,4,3,2:T(8,128)S(1)}, f32[32,16,3,3,3]{0,1,4,3,2:T(8,128)}, u32[]{:S(2)}) copy-start(f32[32,16,3,3,3]{0,1,4,3,2:T(8,128)} %param.14) | copy-start | bytes 165892
  2.9 7.4 %copy-start.8 = (f32[4,3,9,1,1,1]{2,1,5,4,3,0:T(4,128)S(1)}, f32[4,3,9,1,1,1]{2,1,5,4,3,0:T(4,128)}, u32[]{:S(2)}) copy-start(f32[4,3,9,1,1,1]{2,1,5,4,3,0:T(4,128)} %constant.27) | copy-start | bytes 1300
  2.9 34.2 %all-to-all-start = ((f32[1056,2,128]{2,1,0:T(2,128)}), f32[1056,2,128]{2,1,0:T(2,128)S(1)}, u32[]{:S(2)}, u32[]{:S(2)}) async-start(f32[1056,2,128]{2,1,0:T(2,128)} %bitcast.55), calls=%async_computation | async-start | bytes 2162688 | tf_op jit(solution)/shard_map/all_to_all | solution.py:721
  10.2 2.8 %copy-start.6 = (f32[9,3,16,1,1,1]{2,1,0,5,4,3:T(4,128)S(1)}, f32[9,3,16,1,1,1]{2,1,0,5,4,3:T(4,128)}, u32[]{:S(2)}) copy-start(f32[9,3,16,1,1,1]{2,1,0,5,4,3:T(4,128)} %constant.26) | copy-start | bytes 5188
  16.1 3.3 %copy-start.11 = (f32[16]{0:T(128)S(1)}, f32[16]{0:T(128)}, u32[]{:S(2)}) copy-start(f32[16]{0:T(128)} %param.13) | copy-start | bytes 196
  16.8 2.8 %copy-start = (f32[9,16,2,3,2,16]{5,1,0,3,4,2:T(8,128)S(1)}, f32[9,16,2,3,2,16]{5,1,0,3,4,2:T(8,128)}, u32[]{:S(2)}) copy-start(f32[9,16,2,3,2,16]{5,1,0,3,4,2:T(8,128)} %convolution_bitcast_fusion.1) | copy-start | bytes 331780
  18.7 2.7 %copy-start.2 = (f32[128,864]{0,1:T(8,128)S(1)}, f32[128,864]{0,1:T(8,128)}, u32[]{:S(2)}) copy-start(f32[128,864]{0,1:T(8,128)} %reduce_precision.47) | copy-start | bytes 1327108
  19.7 1.9 %copy-start.10 = (f32[3,2,8]{2,0,1:T(4,128)S(1)}, f32[3,2,8]{2,0,1:T(4,128)}, u32[]{:S(2)}) copy-start(f32[3,2,8]{2,0,1:T(4,128)} %constant.23.clone) | copy-start | bytes 580
  19.7 2.0 %copy-start.9 = (f32[3,3,8,1,1,1]{2,1,0,5,4,3:T(4,128)S(1)}, f32[3,3,8,1,1,1]{2,1,0,5,4,3:T(4,128)}, u32[]{:S(2)}) copy-start(f32[3,3,8,1,1,1]{2,1,0,5,4,3:T(4,128)} %constant.28) | copy-start | bytes 868
  20.1 2.3 %copy-start.3 = (f32[32,16,2,3,3]{0,3,4,2,1:T(4,128)S(1)}, f32[32,16,2,3,3]{0,3,4,2,1:T(4,128)}, u32[]{:S(2)}) copy-start(f32[32,16,2,3,3]{0,3,4,2,1:T(4,128)} %copy.74) | copy-start | bytes 110596
  21.4 1.6 %copy-start.4 = (f32[288,96]{1,0:T(8,128)S(1)}, f32[288,96]{1,0:T(8,128)}, u32[]{:S(2)}) copy-start(f32[288,96]{1,0:T(8,128)} %reshape.77) | copy-start | bytes 331780
  21.4 1.6 %copy-start.1 = (f32[128,864]{1,0:T(8,128)S(1)}, f32[128,864]{1,0:T(8,128)}, u32[]{:S(2)}) copy-start(f32[128,864]{1,0:T(8,128)} %copy.52) | copy-start | bytes 1327108
  37.1 8.3 %copy-start.12 = (f32[32]{0:T(128)S(1)}, f32[32]{0:T(128)}, u32[]{:S(2)}) copy-start(f32[32]{0:T(128)} %param.15) | copy-start | bytes 388
  41.2 11.9 %all-to-all-start.1 = ((f32[32,8,128]{2,1,0:T(8,128)}), f32[32,8,128]{2,1,0:T(8,128)S(1)}, u32[]{:S(2)}, u32[]{:S(2)}) async-start(f32[32,8,128]{2,1,0:T(8,128)} %get-tuple-element.9), calls=%async_computation.1 | async-start | bytes 262144 | tf_op jit(solution)/shard_map/all_to_all | solution.py:727

commit v7 on v6

--- a/solution.py
+++ b/solution.py
@@ -30,6 +30,8 @@
 HID = HID_ROWS * C1 * BZ
 K2 = 3 * HID
 OUTM = OUT_ROWS * C2
+LAST = BY - 2
+ROW_HID = 3 * C1 * BZ
 
 EXACT = lax.Precision.HIGHEST
 F32 = jnp.float32
@@ -425,13 +427,13 @@
     )
 
 
-def two_blocks(wide, blocks, keep, first, second, bias, out, coarse_h, fine_h, keep_top=None):
+def hidden_parts(wide, table, count, coarse_h, fine_h, keep=None, keep_top=None):
     ones = jnp.ones((16, 256), BF16)
     for group in range(3):
         coarse = [wide[group + dx, z][0] for dx in range(3) for z in range(BZ)]
         fine = [wide[group + dx, z][1] for dx in range(3) for z in range(BZ)]
         stacked = jnp.concatenate(coarse + fine + coarse + [ones], axis=0)
-        hidden = jnp.dot(first[...], stacked, preferred_element_type=F32)
+        hidden = jnp.dot(table, stacked, preferred_element_type=F32)
         hidden = jnp.maximum(hidden, 0.0)
         if group == 0 and keep is not None:
             hidden = hidden * keep
@@ -439,16 +441,14 @@
             top = C1 * BZ
             hidden = jnp.concatenate([hidden[:top] * keep_top, hidden[top:]], axis=0)
         coarse, fine = split_kernel(hidden)
-        coarse_h[group * HID : (group + 1) * HID, :] = coarse
-        fine_h[group * HID : (group + 1) * HID, :] = fine
+        coarse_h[group * count : (group + 1) * count, :] = coarse
+        fine_h[group * count : (group + 1) * count, :] = fine
+
+
+def results(second, count, coarse_h, fine_h):
     both = jnp.dot(second[...], coarse_h[...], preferred_element_type=F32)
-    rest = jnp.dot(second[:OUTM, :], fine_h[...], preferred_element_type=F32)
-    result = both[:OUTM] + both[OUTM:] + rest
-    for side, b in enumerate(blocks):
-        for r in range(OUT_ROWS):
-            out[pl.ds(OUT_ROWS * b + r, C2, stride=BY // 2), :] = (
-                result[r * C2 : (r + 1) * C2, side * HALF : (side + 1) * HALF] + bias[...]
-            )
+    rest = jnp.dot(second[:count, :], fine_h[...], preferred_element_type=F32)
+    return both[:count] + both[count:] + rest
 
 
 def inner_body(joined, first, second, bias, out, phases, coarse_h, fine_h):
@@ -457,19 +457,25 @@
         odd = joined[z, :, HALF:]
         parts = (pltpu.roll(even, 1, 1), pltpu.roll(odd, 1, 1), even, odd, pltpu.roll(even, HALF - 1, 1))
         for j, part in enumerate(parts):
+            phases[j, z, 0:8, :] = jnp.zeros((8, HALF), F32)
+            phases[j, z, SROW - 8 : SROW, :] = jnp.zeros((8, HALF), F32)
             phases[j, z, TOP : TOP + BY, :] = part
-    half = (BLOCKS - 2) // 2
+    half = BLOCKS // 2
     for step in range(half):
-        blocks = (1 + step, 1 + step + half)
+        blocks = (step, step + half)
         wide = {}
         for j in range(PHASES):
             for z in range(BZ):
                 cut = [phases[j, z, 8 * b : 8 * b + WIN, :] for b in blocks]
                 wide[j, z] = split_kernel(jnp.concatenate(cut, axis=1))
-        slot = step % 2
-        two_blocks(
-            wide, blocks, None, first, second, bias, out, coarse_h.at[slot], fine_h.at[slot]
-        )
+        scratch = (coarse_h.at[step % 2], fine_h.at[step % 2])
+        hidden_parts(wide, first[...], HID, *scratch)
+        result = results(second, OUTM, *scratch)
+        for side, b in enumerate(blocks):
+            for r in range(OUT_ROWS):
+                out[pl.ds(OUT_ROWS * b + r, C2, stride=BY // 2), :] = (
+                    result[r * C2 : (r + 1) * C2, side * HALF : (side + 1) * HALF] + bias[...]
+                )
 
 
 def inner(joined, first, second, bias):
@@ -529,7 +535,7 @@
     tall_lane = iota((2 * WIN, HALF), 1)
     sides = jnp.concatenate([from_left[:4], from_right[:4]], axis=0)
     ends = jnp.concatenate(
-        [sides[:, :WIN], sides[:, SROW - WIN : SROW], jnp.zeros((8, 128 - 2 * WIN), F32)], axis=1
+        [sides[:, :WIN], sides[:, LAST : LAST + WIN], jnp.zeros((8, 128 - 2 * WIN), F32)], axis=1
     )
     side_columns = jnp.transpose(ends)[: 2 * WIN]
 
@@ -546,9 +552,9 @@
             ends = [
                 from_above[at : at + 2],
                 own[: WIN - TOP],
-                own[SROW - WIN - TOP :],
+                own[LAST - TOP :],
                 from_below[bottom : bottom + 1],
-                jnp.zeros((SROW - BY - TOP - 1, HALF), F32),
+                jnp.zeros((LAST + WIN - BY - TOP - 1, HALF), F32),
             ]
             halves.append(jnp.concatenate(ends, axis=0))
         even, odd = halves
@@ -597,40 +603,42 @@
         rest = jnp.zeros((2, 256), F32)
         left_rows += [from_left[2 * z : 2 * z + 2], own[4:7], one, rest]
         right_rows += [own[0:4], from_right[z : z + 1], one, rest]
-    both = jnp.concatenate(
-        [jnp.concatenate(left_rows, axis=0), jnp.concatenate(right_rows, axis=0)], axis=1
-    )
-
-    def reach(values):
-        return jnp.concatenate([values] + [pltpu.roll(values, 512 - dy, 1) for dy in (1, 2)], axis=0)
+    coarse, fine = split_kernel(jnp.concatenate(left_rows + right_rows, axis=0))
+    src = iota((256, 256), 0)
+    dst = iota((256, 256), 1)
+    apart = src == jnp.where(dst < 128, 2 * dst, 2 * (dst - 128) + 1)
+    apart = jnp.where(apart, 1.0, 0.0).astype(BF16)
+    lines = jnp.dot(jnp.concatenate([coarse, fine], axis=0), apart, preferred_element_type=F32)
+    lines = lines[:32] + lines[32:]
+    out_rows = BY // 2
+    line_lane = iota((16, 128), 1)
+
+    def stored_rows(t):
+        cut = lines[:, (t % 2) * 128 : (t % 2) * 128 + 128]
+        return jnp.where(
+            line_lane < out_rows,
+            pltpu.roll(cut[:16], (128 - t // 2) % 128, 1) if t // 2 else cut[:16],
+            pltpu.roll(cut[16:], out_rows - t // 2, 1),
+        )
+
+    taken = [stored_rows(t) for t in range(5)]
 
     def product(table, values):
-        coarse, fine = split_kernel(reach(values))
+        coarse, fine = split_kernel(values)
         stacked = jnp.concatenate([coarse, fine, coarse], axis=0)
         return jnp.dot(table[...], stacked, preferred_element_type=F32)
 
-    hidden = product(first_rim, both)
-    hidden = jnp.maximum(hidden, 0.0)
-    lane = iota((3 * C1 * BZ, 512), 1)
-    depth = iota((3 * C1 * BZ, 512), 0)
-    outside = no_row & ((lane & 255) == 0)
-    outside = outside | (no_col & (lane < 256) & (depth < C1 * BZ))
+    reach = [jnp.concatenate([taken[row + dy] for row in range(3)], axis=1) for dy in range(3)]
+    hidden = jnp.maximum(product(first_rim, jnp.concatenate(reach, axis=0)), 0.0)
+    lane = iota((3 * C1 * BZ, 384), 1)
+    depth = iota((3 * C1 * BZ, 384), 0)
+    outside = no_row & ((lane == 0) | (lane == out_rows))
+    outside = outside | (no_col & ((lane & 127) < out_rows) & (depth < C1 * BZ))
     hidden = jnp.where(outside, 0.0, hidden)
-    found = product(second_rim, hidden)
-    every = jnp.where(iota((BY // 2, 256), 1) == 2 * iota((BY // 2, 256), 0), 1.0, 0.0).astype(BF16)
-    parts = []
-    for side in range(2):
-        parts += split_kernel(found[:, side * 256 : (side + 1) * 256] + bias[:, :1])
-    turned = lax.dot_general(
-        every,
-        jnp.concatenate(parts, axis=0),
-        (((1,), (1,)), ((), ())),
-        preferred_element_type=F32,
-    )
-    columns = [
-        turned[:, 2 * side * C2 : (2 * side + 1) * C2] + turned[:, (2 * side + 1) * C2 : (2 * side + 2) * C2]
-        for side in range(2)
-    ]
+    reach = [hidden[:, row * 128 : (row + 1) * 128] for row in range(3)]
+    found = product(second_rim, jnp.concatenate(reach, axis=0)) + bias[...]
+    turned = jnp.transpose(found)
+    columns = [turned[:out_rows], turned[out_rows:]]
     out_lane = iota((BY // 2, HALF), 1)
     for o in range(C2):
         at = o * (BY // 2)
@@ -640,9 +648,12 @@
 
     keep = jnp.where(no_col & ((iota((1, 256), 1) & (HALF - 1)) == 0), 0.0, 1.0)
     keep_top = jnp.where(no_row & (iota((1, 256), 1) < HALF), 0.0, 1.0)
-    two_blocks(
-        wide, (0, BLOCKS - 1), keep, first, second, bias, out, coarse_h, fine_h, keep_top=keep_top
-    )
+    hidden_parts(wide, first[:ROW_HID, :], ROW_HID, coarse_h, fine_h, keep, keep_top)
+    result = results(second, C2, coarse_h, fine_h)
+    for side, at in enumerate((0, BY // 2 - 1)):
+        out[pl.ds(at, C2, stride=BY // 2), :] = (
+            result[:, side * HALF : (side + 1) * HALF] + bias[...]
+        )
 
 
 def rim(grid, edge, joined, received, own_columns, inner_out, first, second, bias, first_rim, second_rim):
@@ -652,7 +663,7 @@
         in_specs=[pl.BlockSpec(memory_space=pltpu.SMEM)] + [vmem] * 9,
         out_specs=vmem,
         out_shape=jax.ShapeDtypeStruct((C2 * BY // 2, HALF), F32),
-        scratch_shapes=[pltpu.VMEM((K2, 256), BF16), pltpu.VMEM((K2, 256), BF16)],
+        scratch_shapes=[pltpu.VMEM((3 * ROW_HID, 256), BF16), pltpu.VMEM((3 * ROW_HID, 256), BF16)],
         compiler_params=pltpu.CompilerParams(vmem_limit_bytes=48 * 2**20),
         name="rim",
     )(edge, joined, received, own_columns, inner_out, first, second, bias, first_rim, second_rim)
@@ -676,7 +687,8 @@
         coarse, fine = split_host(values)
         return jnp.concatenate([coarse, coarse, fine], axis=1)
 
-    return stacked(first), stacked(second)
+    row = jnp.transpose(weight2[:, :, 1:3], (0, 4, 3, 1, 2)).reshape(C2, 3 * ROW_HID)
+    return stacked(first), stacked(second), jnp.concatenate(split_host(row), axis=0)
 
 
 def first_table(weight, bias):
@@ -722,12 +734,12 @@
     first = first_table(conv1_weight, conv1_bias)
     second = second_table(conv2_weight)
     bias = jnp.broadcast_to(conv2_bias[:, None], (C2, HALF))
-    first_rim, second_rim = rim_tables(conv1_weight, conv1_bias, conv2_weight)
+    first_rim, second_rim, second_row = rim_tables(conv1_weight, conv1_bias, conv2_weight)
     joined, messages, own_columns = join((rows, cols), edge, arrived, per_pair)
     received = lax.all_to_all(messages, axes, split_axis=0, concat_axis=0, tiled=True)
     inner_out = inner(joined, first, second, bias)
     features = rim(
-        (rows, cols), edge, joined, received, own_columns, inner_out, first, second, bias, first_rim, second_rim
+        (rows, cols), edge, joined, received, own_columns, inner_out, first, second_row, bias, first_rim, second_rim
     )
     return features.reshape(C2, 1, BY // 2, HALF)
 

time: 56.9 us -> 56.6 us (level)
  Pallas kernels: 15.1 us -> 15.8 us
    pallas_call x1, Pallas kernels: 4.58 us -> 5.56 us  [inner(): pl.pallas_call(inner_body, in_specs=[vmem] * 4, out_specs=vmem, out_shape...]
    all_to_all x1, waiting for transfers between devices: 2.98 us -> 2 us  [body(): lax.all_to_all(messages, axes, split_axis=0, concat_axis=0, tiled=True)]
    unnamed x28 -> x30, local copies, waits for them, and re-layouts: 0.81 us -> 0.15 us
  transfers between devices with their start and end apart: 2 -> 2, of which waited for: 2 -> 2; matrix products, arithmetic and copies ran while one was open for 23% -> 22% of each run, Pallas kernels for 8% -> 10%
where the time goes in v7:
time: 56.6 us; the launch traced here: 56.3 us
  waiting for transfers between devices  16.5 us (29%)
  Pallas kernels  15.8 us (28%)
  starting transfers between devices  11.1 us (20%)
  local copies, waits for them, and re-layouts  6.14 us (11%)
  matrix products  4.96 us (9%)
  other arithmetic  1.54 us (3%)
    all_to_all x1, waiting for transfers between devices, body(): lax.all_to_all(outgoing, axes, split_axis=0, concat_axis=0, tiled=True)  14.5 us
    all_to_all x1, starting transfers between devices, body(): lax.all_to_all(outgoing, axes, split_axis=0, concat_axis=0, tiled=True)  7.3 us
    pallas_call x1, Pallas kernels, inner(): pl.pallas_call(inner_body, in_specs=[vmem] * 4, out_specs=vmem, out_shape...  5.56 us
    pallas_call x1, Pallas kernels, join(): pl.pallas_call(lambda *refs: join_body(per_pair, grid, *refs), in_specs=[...  4.11 us
    all_to_all x1, starting transfers between devices, body(): lax.all_to_all(messages, axes, split_axis=0, concat_axis=0, tiled=True)  3.8 us
    pallas_call x1, Pallas kernels, rim(): pl.pallas_call(lambda *refs: rim_body(grid, *refs), in_specs=[pl.BlockSpe...  3.23 us
    pallas_call x1, Pallas kernels, pack_full(): pl.pallas_call(lambda *refs: pack_full_body(per_pair, *refs), in_specs=[p...  2.86 us
    dot_general x1, matrix products, second_table(): jnp.einsum('oczyx,iyh->ioxhcz', weight[:, :, 1:3], jnp.asarray(reach), pr...  2.71 us
  transfers between devices with their start and end apart: 2, of which 2 were waited for; matrix products, arithmetic and copies ran while one was open for 22% of the time, Pallas kernels for 10%

profile of v7, /device:TPU:0, one launch (start us, length us, event | category | flops | bytes accessed | tf_op | source)
XLA Modules:
  0.0 56.3 jit_solution(11140276329284978655)
XLA Ops:
  0.0 2.9 %pack.1 = f32[32,33,2,128]{3,2,1,0:T(2,128)} custom-call(s32[8,64]{1,0:T(8,128)} %bitcast.65, s32[8,64]{1,0:T(8,128)} %bitcast.66, f32[32,32,2,128]{3,2,1,0:T(2,128)} %bitcast.61), custom_call_target="tpu_custom_call" | custom-call | tf_op jit(solution)/shard_map/pack/pallas_call | solution.py:176
  2.9 0.0 copy-start.9
  2.9 7.3 %all-to-all-start = ((f32[1056,2,128]{2,1,0:T(2,128)}), f32[1056,2,128]{2,1,0:T(2,128)S(1)}, u32[]{:S(2)}, u32[]{:S(2)}) async-start(f32[1056,2,128]{2,1,0:T(2,128)} %bitcast.58), calls=%async_computation | async-start | bytes 2162688 | tf_op jit(solution)/shard_map/all_to_all | solution.py:733
  10.2 0.0 copy-done.8
  10.2 0.0 copy-done.6
  10.2 0.0 copy-start.11
  10.3 0.0 copy-start.12
  10.3 0.0 copy-start.7
  10.3 0.0 copy-done.9
  10.3 0.0 copy-start.3
  10.3 2.7 %convolution_bitcast_fusion = f32[4,32,3,9,16,2]{1,3,2,5,4,0:T(8,128)S(1)} fusion(f32[4,3,9,1,1,1]{2,1,5,4,3,0:T(4,128)S(1)} %copy-done.9, f32[32,16,2,3,3]{0,1,4,3,2:T(8,128)S(1)} %slice.15), kind=kOutput, calls=%fused_computation | convolution fusion | flops 3981312 | bytes 479664 | tf_op jit(solution)/shard_map/oczyx,iyh->ioxhcz/dot_general | solution.py:717
  13.0 0.0 copy-done.11
  13.0 0.0 copy-done.12
  13.1 0.1 broadcast_multiply_fusion
  13.1 1.9 %convolution_bitcast_fusion.1 = f32[9,16,2,3,2,16]{5,1,0,3,4,2:T(8,128)} fusion(f32[9,3,16,1,1,1]{2,1,0,5,4,3:T(4,128)S(1)} %copy-done.7, f32[16,1,2,3,3]{0,3,4,2,1:T(4,128)S(1)} %get-tuple-element.24, f32[16,1,2,3,3]{0,3,4,2,1:T(4,128)S(1)} %get-tuple-element.23), kind=kOutput, calls=%fused_computation.1 | convolution fusion | flops 995904 | bytes 114624 | tf_op jit(solution)/shard_map/czpyx,iys->iczxps/dot_general | solution.py:701
  15.1 1.1 %copy.57 = f32[4,32,3,9,16,2]{1,0,5,4,3,2:T(4,128)S(1)} copy(f32[4,32,3,9,16,2]{1,3,2,5,4,0:T(8,128)S(1)} %convolution_bitcast_fusion) | data formatting | bytes 884736 | tf_op jit(solution)/shard_map/oczyx,iyh->ioxhcz/transpose | solution.py:717
  16.2 0.7 %reshape.81 = f32[128,864]{0,1:T(8,128)S(1)} reshape(f32[4,32,3,9,16,2]{1,0,5,4,3,2:T(4,128)S(1)} %copy.57) | data formatting | bytes 884736 | tf_op jit(solution)/shard_map/reshape | solution.py:718
  17.0 0.0 copy-start
  17.0 0.8 %reduce_precision.50 = f32[128,864]{0,1:T(8,128)} reduce-precision(f32[128,864]{0,1:T(8,128)S(1)} %reshape.81), exponent_bits=8, mantissa_bits=7 | non-fusion elementwise | flops 110592 | bytes 884736 | tf_op jit(solution)/shard_map/reduce_precision | solution.py:51
  17.8 1.0 %copy.59 = f32[128,864]{1,0:T(8,128)} copy(f32[128,864]{0,1:T(8,128)S(1)} %reshape.81) | data formatting | bytes 884736 | tf_op jit(solution)/shard_map/reshape | solution.py:718
  18.8 0.0 copy-done.4
  18.8 0.1 copy.85
  18.9 0.1 broadcast_in_dim.4
  19.0 0.1 tile.10
  19.1 0.1 tile.12
  19.1 0.5 copy.54
  19.6 1.2 %reshape.80 = f32[288,96]{1,0:T(8,128)} reshape(f32[9,16,2,3,2,16]{5,4,3,2,1,0:T(2,128)S(1)} %copy.54) | data formatting | bytes 221184 | tf_op jit(solution)/shard_map/reshape | solution.py:702
  20.8 0.2 copy.58
  21.0 0.3 fusion
  21.4 0.2 copy.65
  21.6 0.2 reshape.83
  21.8 0.1 copy.66
  21.9 0.1 copy.67
  22.0 0.1 copy.61
  22.1 0.1 copy.62
  22.2 0.1 pad_add_fusion.refs_0_
  22.3 0.1 pad_maximum_fusion.3.refs_8_
  22.4 0.1 pad_maximum_fusion.1.refs_9_
  22.6 0.1 fusion.12
  22.7 14.5 %all-to-all-done = f32[1056,2,128]{2,1,0:T(2,128)S(1)} async-done(((f32[1056,2,128]{2,1,0:T(2,128)}), f32[1056,2,128]{2,1,0:T(2,128)S(1)}, u32[]{:S(2)}, u32[]{:S(2)}) %all-to-all-start) | async-done | bytes 1081376 | tf_op jit(solution)/shard_map/all_to_all | solution.py:733
  37.1 4.1 %join.1 = (f32[2,128,256]{2,1,0:T(8,128)S(1)}, f32[32,8,128]{2,1,0:T(8,128)}, f32[16,128]{1,0:T(8,128)S(1)}) custom-call(s32[2]{0:T(128)S(1)} %pad_add_fusion.refs_0_, f32[32,33,2,128]{3,2,1,0:T(2,128)S(1)} %bitcast.56, f32[2112,128]{1,0:T(8,128)S(1)} %bitcast.57), custom_call_target="tpu_custom_call" | custom-call | tf_op jit(solution)/shard_map/join/pallas_call | solution.py:404
  41.3 3.8 %all-to-all-start.1 = ((f32[32,8,128]{2,1,0:T(8,128)}), f32[32,8,128]{2,1,0:T(8,128)S(1)}, u32[]{:S(2)}, u32[]{:S(2)}) async-start(f32[32,8,128]{2,1,0:T(8,128)} %get-tuple-element.9), calls=%async_computation.1 | async-start | bytes 262144 | tf_op jit(solution)/shard_map/all_to_all | solution.py:739
  45.1 0.1 copy.55
  45.2 0.2 fusion.2.first.refs_5_
  45.5 0.1 broadcast_in_dim.5.bias.refs_7_
  45.5 5.6 %inner.1.refs_4_ = f32[2048,128]{1,0:T(8,128)S(1)} custom-call(f32[2,128,256]{2,1,0:T(8,128)S(1)} %get-tuple-element.8.joined.refs_1_, bf16[288,304]{1,0:T(8,128)(2,1)S(1)} %fusion.2.first.refs_5_, bf16[256,864]{1,0:T(8,128)(2,1)S(1)} %pad_maximum_fusion.second, f32[32,128]{1,0:T(8,128)S(1)} %broadcast_in_dim.5.bias.refs_7_), custom_call_target="tpu_custom_call" | custom-call | tf_op jit(solution)/shard_map/inner/pallas_call | solution.py:483
  51.1 2.0 %all-to-all-done.1.refs_2_ = f32[32,8,128]{2,1,0:T(8,128)S(1)} async-done(((f32[32,8,128]{2,1,0:T(8,128)}), f32[32,8,128]{2,1,0:T(8,128)S(1)}, u32[]{:S(2)}, u32[]{:S(2)}) %all-to-all-start.1) | async-done | bytes 131104 | tf_op jit(solution)/shard_map/all_to_all | solution.py:739
  53.1 3.2 %rim.1 = f32[2048,128]{1,0:T(8,128)} custom-call(s32[2]{0:T(128)S(1)} %pad_add_fusion.refs_0_, f32[2,128,256]{2,1,0:T(8,128)S(1)} %get-tuple-element.8.joined.refs_1_, f32[32,8,128]{2,1,0:T(8,128)S(1)} %all-to-all-done.1.refs_2_, f32[16,128]{1,0:T(8,128)S(1)} %get-tuple-element.10.refs_3_, f32[2048,128]{1,0:T(8,128)S(1)} %inner.1.refs_4_, ...), custom_call_target="tpu_custom_call" | custom-call | tf_op jit(solution)/shard_map/rim/pallas_call | solution.py:661
  (29 shorter events, 0.2 us)
Async XLA Ops:
  0.0 10.2 %copy-start.8 = (f32[16,1,3,3,3]{0,1,4,3,2:T(1,128)S(1)}, f32[16,1,3,3,3]{0,1,4,3,2:T(1,128)}, u32[]{:S(2)}) copy-start(f32[16,1,3,3,3]{0,1,4,3,2:T(1,128)} %param.12) | copy-start | bytes 5188
  0.0 10.2 %copy-start.6 = (f32[32,16,3,3,3]{0,1,4,3,2:T(8,128)S(1)}, f32[32,16,3,3,3]{0,1,4,3,2:T(8,128)}, u32[]{:S(2)}) copy-start(f32[32,16,3,3,3]{0,1,4,3,2:T(8,128)} %param.14) | copy-start | bytes 165892
  2.9 7.4 %copy-start.9 = (f32[4,3,9,1,1,1]{2,1,5,4,3,0:T(4,128)S(1)}, f32[4,3,9,1,1,1]{2,1,5,4,3,0:T(4,128)}, u32[]{:S(2)}) copy-start(f32[4,3,9,1,1,1]{2,1,5,4,3,0:T(4,128)} %constant.27) | copy-start | bytes 1300
  2.9 34.2 %all-to-all-start = ((f32[1056,2,128]{2,1,0:T(2,128)}), f32[1056,2,128]{2,1,0:T(2,128)S(1)}, u32[]{:S(2)}, u32[]{:S(2)}) async-start(f32[1056,2,128]{2,1,0:T(2,128)} %bitcast.58), calls=%async_computation | async-start | bytes 2162688 | tf_op jit(solution)/shard_map/all_to_all | solution.py:733
  10.2 2.8 %copy-start.11 = (f32[3,2,8]{2,0,1:T(4,128)S(1)}, f32[3,2,8]{2,0,1:T(4,128)}, u32[]{:S(2)}) copy-start(f32[3,2,8]{2,0,1:T(4,128)} %constant.23.clone) | copy-start | bytes 580
  10.3 2.8 %copy-start.12 = (f32[16]{0:T(128)S(1)}, f32[16]{0:T(128)}, u32[]{:S(2)}) copy-start(f32[16]{0:T(128)} %param.13) | copy-start | bytes 196
  10.3 2.9 %copy-start.7 = (f32[9,3,16,1,1,1]{2,1,0,5,4,3:T(4,128)S(1)}, f32[9,3,16,1,1,1]{2,1,0,5,4,3:T(4,128)}, u32[]{:S(2)}) copy-start(f32[9,3,16,1,1,1]{2,1,0,5,4,3:T(4,128)} %constant.26) | copy-start | bytes 5188
  10.3 4.8 %copy-start.3 = (f32[32,16,2,3,3]{0,1,4,3,2:T(8,128)}, f32[32,16,2,3,3]{0,1,4,3,2:T(8,128)S(1)}, u32[]{:S(2)}) copy-start(f32[32,16,2,3,3]{0,1,4,3,2:T(8,128)S(1)} %slice.15) | copy-start | bytes 110596
  17.0 1.8 %copy-start.4 = (f32[32,16,2,3,3]{0,1,4,3,2:T(8,128)S(1)}, f32[32,16,2,3,3]{0,1,4,3,2:T(8,128)}, u32[]{:S(2)}) copy-start(f32[32,16,2,3,3]{0,1,4,3,2:T(8,128)} %copy-done.3) | copy-start | bytes 110596
  17.0 2.1 %copy-start = (f32[9,16,2,3,2,16]{5,1,0,3,4,2:T(8,128)S(1)}, f32[9,16,2,3,2,16]{5,1,0,3,4,2:T(8,128)}, u32[]{:S(2)}) copy-start(f32[9,16,2,3,2,16]{5,1,0,3,4,2:T(8,128)} %convolution_bitcast_fusion.1) | copy-start | bytes 331780
  18.8 2.0 %copy-start.2 = (f32[128,864]{0,1:T(8,128)S(1)}, f32[128,864]{0,1:T(8,128)}, u32[]{:S(2)}) copy-start(f32[128,864]{0,1:T(8,128)} %reduce_precision.50) | copy-start | bytes 1327108
  19.1 1.9 %copy-start.10 = (f32[3,3,8,1,1,1]{2,1,0,5,4,3:T(4,128)S(1)}, f32[3,3,8,1,1,1]{2,1,0,5,4,3:T(4,128)}, u32[]{:S(2)}) copy-start(f32[3,3,8,1,1,1]{2,1,0,5,4,3:T(4,128)} %constant.28) | copy-start | bytes 868
  20.8 1.7 %copy-start.5 = (f32[288,96]{1,0:T(8,128)S(1)}, f32[288,96]{1,0:T(8,128)}, u32[]{:S(2)}) copy-start(f32[288,96]{1,0:T(8,128)} %reshape.80) | copy-start | bytes 331780
  20.8 1.8 %copy-start.1 = (f32[128,864]{1,0:T(8,128)S(1)}, f32[128,864]{1,0:T(8,128)}, u32[]{:S(2)}) copy-start(f32[128,864]{1,0:T(8,128)} %copy.59) | copy-start | bytes 1327108
  37.1 8.3 %copy-start.13 = (f32[32]{0:T(128)S(1)}, f32[32]{0:T(128)}, u32[]{:S(2)}) copy-start(f32[32]{0:T(128)} %param.15) | copy-start | bytes 388
  41.3 11.9 %all-to-all-start.1 = ((f32[32,8,128]{2,1,0:T(8,128)}), f32[32,8,128]{2,1,0:T(8,128)S(1)}, u32[]{:S(2)}, u32[]{:S(2)}) async-start(f32[32,8,128]{2,1,0:T(8,128)} %get-tuple-element.9), calls=%async_computation.1 | async-start | bytes 262144 | tf_op jit(solution)/shard_map/all_to_all | solution.py:739

commit v8 on v7

--- a/solution.py
+++ b/solution.py
@@ -234,7 +234,7 @@
     return jnp.where(chosen, 1.0, 0.0)
 
 
-def join_body(per_pair, grid, edge, routes, strips, joined, messages, own_columns, data, place_y, pieces, route_rows, params, sem):
+def join_body(per_pair, grid, edge, routes, strips, joined, messages, own_columns, data, place_y, pieces, route_rows, params, sem, tiles, tile_sems):
     senders = routes.shape[0]
     slots = senders * per_pair
     chunk = 2 * chunk_of(per_pair)
@@ -381,20 +381,22 @@
     at_row = edge[0]
     at_col = edge[1]
     rows, cols = grid
-
-    def send(dy, dx, values):
-        to_row = at_row + dy
-        to_col = at_col + dx
-
-        @pl.when((to_row >= 0) & (to_row < rows) & (to_col >= 0) & (to_col < cols))
-        def _():
-            messages[to_row * cols + to_col] = values
-
-    for dy in (-1, 0, 1):
-        send(dy, 1, right)
-        send(dy, -1, left)
-    send(1, 0, down)
-    send(-1, 0, up)
+    for i, values in enumerate((right, left, down, up)):
+        tiles[i] = values
+    sends = [(dy, 1, 0) for dy in (-1, 0, 1)] + [(dy, -1, 1) for dy in (-1, 0, 1)]
+    sends += [(1, 0, 2), (-1, 0, 3)]
+
+    def each(finish):
+        for n, (dy, dx, i) in enumerate(sends):
+            to_row = at_row + dy
+            to_col = at_col + dx
+            there = (to_row >= 0) & (to_row < rows) & (to_col >= 0) & (to_col < cols)
+            at = jnp.where(there, to_row * cols + to_col, 0)
+            copy = pltpu.make_async_copy(tiles.at[i], messages.at[at], tile_sems.at[n])
+            pl.when(there)(copy.wait if finish else copy.start)
+
+    each(False)
+    each(True)
 
 
 def join(grid, edge, arrived, per_pair):
@@ -404,7 +406,7 @@
     return pl.pallas_call(
         lambda *refs: join_body(per_pair, grid, *refs),
         in_specs=[pl.BlockSpec(memory_space=pltpu.SMEM), pl.BlockSpec(memory_space=pl.ANY), vmem],
-        out_specs=[vmem, vmem, vmem],
+        out_specs=[vmem, pl.BlockSpec(memory_space=pl.ANY), vmem],
         out_shape=[
             jax.ShapeDtypeStruct((BZ, BY, COLS), F32),
             jax.ShapeDtypeStruct((senders, 8, HALF), F32),
@@ -417,6 +419,8 @@
             pltpu.VMEM((slots, SX), F32),
             pltpu.SMEM((senders, 2, SX), F32),
             pltpu.SemaphoreType.DMA,
+            pltpu.VMEM((4, 8, HALF), F32),
+            pltpu.SemaphoreType.DMA((8,)),
         ],
         compiler_params=pltpu.CompilerParams(vmem_limit_bytes=48 * 2**20),
         name="join",

time: 56.6 us -> 56.6 us (level)
  no operation moved by 1% of the time
where the time goes in v8:
time: 56.6 us; the launch traced here: 56.3 us
  waiting for transfers between devices  16.5 us (29%)
  Pallas kernels  15.7 us (28%)
  starting transfers between devices  11.1 us (20%)
  local copies, waits for them, and re-layouts  6.14 us (11%)
  matrix products  4.96 us (9%)
  other arithmetic  1.54 us (3%)
    all_to_all x1, waiting for transfers between devices, body(): lax.all_to_all(outgoing, axes, split_axis=0, concat_axis=0, tiled=True)  14.5 us
    all_to_all x1, starting transfers between devices, body(): lax.all_to_all(outgoing, axes, split_axis=0, concat_axis=0, tiled=True)  7.3 us
    pallas_call x1, Pallas kernels, inner(): pl.pallas_call(inner_body, in_specs=[vmem] * 4, out_specs=vmem, out_shape...  5.56 us
    pallas_call x1, Pallas kernels, join(): pl.pallas_call(lambda *refs: join_body(per_pair, grid, *refs), in_specs=[...  4.08 us
    all_to_all x1, starting transfers between devices, body(): lax.all_to_all(messages, axes, split_axis=0, concat_axis=0, tiled=True)  3.81 us
    pallas_call x1, Pallas kernels, rim(): pl.pallas_call(lambda *refs: rim_body(grid, *refs), in_specs=[pl.BlockSpe...  3.23 us
    pallas_call x1, Pallas kernels, pack_full(): pl.pallas_call(lambda *refs: pack_full_body(per_pair, *refs), in_specs=[p...  2.86 us
    dot_general x1, matrix products, second_table(): jnp.einsum('oczyx,iyh->ioxhcz', weight[:, :, 1:3], jnp.asarray(reach), pr...  2.71 us
  transfers between devices with their start and end apart: 2, of which 2 were waited for; matrix products, arithmetic and copies ran while one was open for 22% of the time, Pallas kernels for 10%

profile of v8, /device:TPU:0, one launch (start us, length us, event | category | flops | bytes accessed | tf_op | source)
XLA Modules:
  0.0 56.3 jit_solution(10403025532701279943)
XLA Ops:
  0.0 2.9 %pack.1 = f32[32,33,2,128]{3,2,1,0:T(2,128)} custom-call(s32[8,64]{1,0:T(8,128)} %bitcast.65, s32[8,64]{1,0:T(8,128)} %bitcast.66, f32[32,32,2,128]{3,2,1,0:T(2,128)} %bitcast.61), custom_call_target="tpu_custom_call" | custom-call | tf_op jit(solution)/shard_map/pack/pallas_call | solution.py:176
  2.9 0.0 copy-start.9
  2.9 7.3 %all-to-all-start = ((f32[1056,2,128]{2,1,0:T(2,128)}), f32[1056,2,128]{2,1,0:T(2,128)S(1)}, u32[]{:S(2)}, u32[]{:S(2)}) async-start(f32[1056,2,128]{2,1,0:T(2,128)} %bitcast.58), calls=%async_computation | async-start | bytes 2162688 | tf_op jit(solution)/shard_map/all_to_all | solution.py:737
  10.2 0.0 copy-done.8
  10.2 0.0 copy-done.6
  10.2 0.0 copy-start.11
  10.3 0.0 copy-start.12
  10.3 0.0 copy-start.7
  10.3 0.0 copy-done.9
  10.3 0.0 copy-start.3
  10.3 2.7 %convolution_bitcast_fusion = f32[4,32,3,9,16,2]{1,3,2,5,4,0:T(8,128)S(1)} fusion(f32[4,3,9,1,1,1]{2,1,5,4,3,0:T(4,128)S(1)} %copy-done.9, f32[32,16,2,3,3]{0,1,4,3,2:T(8,128)S(1)} %slice.15), kind=kOutput, calls=%fused_computation | convolution fusion | flops 3981312 | bytes 479664 | tf_op jit(solution)/shard_map/oczyx,iyh->ioxhcz/dot_general | solution.py:721
  13.0 0.0 copy-done.11
  13.1 0.1 broadcast_multiply_fusion
  13.1 1.9 %convolution_bitcast_fusion.1 = f32[9,16,2,3,2,16]{5,1,0,3,4,2:T(8,128)} fusion(f32[9,3,16,1,1,1]{2,1,0,5,4,3:T(4,128)S(1)} %copy-done.7, f32[16,1,2,3,3]{0,3,4,2,1:T(4,128)S(1)} %get-tuple-element.24, f32[16,1,2,3,3]{0,3,4,2,1:T(4,128)S(1)} %get-tuple-element.23), kind=kOutput, calls=%fused_computation.1 | convolution fusion | flops 995904 | bytes 114624 | tf_op jit(solution)/shard_map/czpyx,iys->iczxps/dot_general | solution.py:705
  15.1 1.1 %copy.57 = f32[4,32,3,9,16,2]{1,0,5,4,3,2:T(4,128)S(1)} copy(f32[4,32,3,9,16,2]{1,3,2,5,4,0:T(8,128)S(1)} %convolution_bitcast_fusion) | data formatting | bytes 884736 | tf_op jit(solution)/shard_map/oczyx,iyh->ioxhcz/transpose | solution.py:721
  16.2 0.7 %reshape.81 = f32[128,864]{0,1:T(8,128)S(1)} reshape(f32[4,32,3,9,16,2]{1,0,5,4,3,2:T(4,128)S(1)} %copy.57) | data formatting | bytes 884736 | tf_op jit(solution)/shard_map/reshape | solution.py:722
  17.0 0.0 copy-start
  17.0 0.8 %reduce_precision.50 = f32[128,864]{0,1:T(8,128)} reduce-precision(f32[128,864]{0,1:T(8,128)S(1)} %reshape.81), exponent_bits=8, mantissa_bits=7 | non-fusion elementwise | flops 110592 | bytes 884736 | tf_op jit(solution)/shard_map/reduce_precision | solution.py:51
  17.8 1.0 %copy.59 = f32[128,864]{1,0:T(8,128)} copy(f32[128,864]{0,1:T(8,128)S(1)} %reshape.81) | data formatting | bytes 884736 | tf_op jit(solution)/shard_map/reshape | solution.py:722
  18.8 0.1 copy.85
  18.9 0.1 broadcast_in_dim.4
  19.0 0.1 tile.10
  19.1 0.1 tile.12
  19.1 0.5 copy.54
  19.6 1.2 %reshape.80 = f32[288,96]{1,0:T(8,128)} reshape(f32[9,16,2,3,2,16]{5,4,3,2,1,0:T(2,128)S(1)} %copy.54) | data formatting | bytes 221184 | tf_op jit(solution)/shard_map/reshape | solution.py:706
  20.8 0.2 copy.58
  21.0 0.0 copy-done.10
  21.0 0.3 fusion
  21.4 0.2 copy.65
  21.6 0.2 reshape.83
  21.8 0.1 copy.66
  21.9 0.1 copy.67
  22.0 0.1 copy.61
  22.1 0.1 copy.62
  22.2 0.1 pad_add_fusion.refs_0_
  22.3 0.1 pad_maximum_fusion.3.refs_8_
  22.4 0.1 pad_maximum_fusion.1.refs_9_
  22.5 0.0 copy-done.5
  22.6 0.1 fusion.12
  22.7 14.5 %all-to-all-done = f32[1056,2,128]{2,1,0:T(2,128)S(1)} async-done(((f32[1056,2,128]{2,1,0:T(2,128)}), f32[1056,2,128]{2,1,0:T(2,128)S(1)}, u32[]{:S(2)}, u32[]{:S(2)}) %all-to-all-start) | async-done | bytes 1081376 | tf_op jit(solution)/shard_map/all_to_all | solution.py:737
  37.1 4.1 %join.1 = (f32[2,128,256]{2,1,0:T(8,128)S(1)}, f32[32,8,128]{2,1,0:T(8,128)}, f32[16,128]{1,0:T(8,128)S(1)}) custom-call(s32[2]{0:T(128)S(1)} %pad_add_fusion.refs_0_, f32[32,33,2,128]{3,2,1,0:T(2,128)S(1)} %bitcast.56, f32[2112,128]{1,0:T(8,128)S(1)} %bitcast.57), custom_call_target="tpu_custom_call" | custom-call | tf_op jit(solution)/shard_map/join/pallas_call | solution.py:406
  41.2 3.8 %all-to-all-start.1 = ((f32[32,8,128]{2,1,0:T(8,128)}), f32[32,8,128]{2,1,0:T(8,128)S(1)}, u32[]{:S(2)}, u32[]{:S(2)}) async-start(f32[32,8,128]{2,1,0:T(8,128)} %get-tuple-element.9), calls=%async_computation.1 | async-start | bytes 262144 | tf_op jit(solution)/shard_map/all_to_all | solution.py:743
  45.1 0.1 copy.55
  45.2 0.2 fusion.2.first.refs_5_
  45.5 0.1 broadcast_in_dim.5.bias.refs_7_
  45.5 5.6 %inner.1.refs_4_ = f32[2048,128]{1,0:T(8,128)S(1)} custom-call(f32[2,128,256]{2,1,0:T(8,128)S(1)} %get-tuple-element.8.joined.refs_1_, bf16[288,304]{1,0:T(8,128)(2,1)S(1)} %fusion.2.first.refs_5_, bf16[256,864]{1,0:T(8,128)(2,1)S(1)} %pad_maximum_fusion.second, f32[32,128]{1,0:T(8,128)S(1)} %broadcast_in_dim.5.bias.refs_7_), custom_call_target="tpu_custom_call" | custom-call | tf_op jit(solution)/shard_map/inner/pallas_call | solution.py:487
  51.1 2.0 %all-to-all-done.1.refs_2_ = f32[32,8,128]{2,1,0:T(8,128)S(1)} async-done(((f32[32,8,128]{2,1,0:T(8,128)}), f32[32,8,128]{2,1,0:T(8,128)S(1)}, u32[]{:S(2)}, u32[]{:S(2)}) %all-to-all-start.1) | async-done | bytes 131104 | tf_op jit(solution)/shard_map/all_to_all | solution.py:743
  53.1 3.2 %rim.1 = f32[2048,128]{1,0:T(8,128)} custom-call(s32[2]{0:T(128)S(1)} %pad_add_fusion.refs_0_, f32[2,128,256]{2,1,0:T(8,128)S(1)} %get-tuple-element.8.joined.refs_1_, f32[32,8,128]{2,1,0:T(8,128)S(1)} %all-to-all-done.1.refs_2_, f32[16,128]{1,0:T(8,128)S(1)} %get-tuple-element.10.refs_3_, f32[2048,128]{1,0:T(8,128)S(1)} %inner.1.refs_4_, ...), custom_call_target="tpu_custom_call" | custom-call | tf_op jit(solution)/shard_map/rim/pallas_call | solution.py:665
  (29 shorter events, 0.2 us)
Async XLA Ops:
  0.0 10.2 %copy-start.8 = (f32[16,1,3,3,3]{0,1,4,3,2:T(1,128)S(1)}, f32[16,1,3,3,3]{0,1,4,3,2:T(1,128)}, u32[]{:S(2)}) copy-start(f32[16,1,3,3,3]{0,1,4,3,2:T(1,128)} %param.12) | copy-start | bytes 5188
  0.0 10.2 %copy-start.6 = (f32[32,16,3,3,3]{0,1,4,3,2:T(8,128)S(1)}, f32[32,16,3,3,3]{0,1,4,3,2:T(8,128)}, u32[]{:S(2)}) copy-start(f32[32,16,3,3,3]{0,1,4,3,2:T(8,128)} %param.14) | copy-start | bytes 165892
  2.9 7.4 %copy-start.9 = (f32[4,3,9,1,1,1]{2,1,5,4,3,0:T(4,128)S(1)}, f32[4,3,9,1,1,1]{2,1,5,4,3,0:T(4,128)}, u32[]{:S(2)}) copy-start(f32[4,3,9,1,1,1]{2,1,5,4,3,0:T(4,128)} %constant.27) | copy-start | bytes 1300
  2.9 34.2 %all-to-all-start = ((f32[1056,2,128]{2,1,0:T(2,128)}), f32[1056,2,128]{2,1,0:T(2,128)S(1)}, u32[]{:S(2)}, u32[]{:S(2)}) async-start(f32[1056,2,128]{2,1,0:T(2,128)} %bitcast.58), calls=%async_computation | async-start | bytes 2162688 | tf_op jit(solution)/shard_map/all_to_all | solution.py:737
  10.2 2.8 %copy-start.11 = (f32[3,2,8]{2,0,1:T(4,128)S(1)}, f32[3,2,8]{2,0,1:T(4,128)}, u32[]{:S(2)}) copy-start(f32[3,2,8]{2,0,1:T(4,128)} %constant.23.clone) | copy-start | bytes 580
  10.3 2.8 %copy-start.12 = (f32[16]{0:T(128)S(1)}, f32[16]{0:T(128)}, u32[]{:S(2)}) copy-start(f32[16]{0:T(128)} %param.13) | copy-start | bytes 196
  10.3 2.9 %copy-start.7 = (f32[9,3,16,1,1,1]{2,1,0,5,4,3:T(4,128)S(1)}, f32[9,3,16,1,1,1]{2,1,0,5,4,3:T(4,128)}, u32[]{:S(2)}) copy-start(f32[9,3,16,1,1,1]{2,1,0,5,4,3:T(4,128)} %constant.26) | copy-start | bytes 5188
  10.3 4.8 %copy-start.3 = (f32[32,16,2,3,3]{0,1,4,3,2:T(8,128)}, f32[32,16,2,3,3]{0,1,4,3,2:T(8,128)S(1)}, u32[]{:S(2)}) copy-start(f32[32,16,2,3,3]{0,1,4,3,2:T(8,128)S(1)} %slice.15) | copy-start | bytes 110596
  17.0 1.8 %copy-start.4 = (f32[32,16,2,3,3]{0,1,4,3,2:T(8,128)S(1)}, f32[32,16,2,3,3]{0,1,4,3,2:T(8,128)}, u32[]{:S(2)}) copy-start(f32[32,16,2,3,3]{0,1,4,3,2:T(8,128)} %copy-done.3) | copy-start | bytes 110596
  17.0 2.1 %copy-start = (f32[9,16,2,3,2,16]{5,1,0,3,4,2:T(8,128)S(1)}, f32[9,16,2,3,2,16]{5,1,0,3,4,2:T(8,128)}, u32[]{:S(2)}) copy-start(f32[9,16,2,3,2,16]{5,1,0,3,4,2:T(8,128)} %convolution_bitcast_fusion.1) | copy-start | bytes 331780
  18.8 2.0 %copy-start.2 = (f32[128,864]{0,1:T(8,128)S(1)}, f32[128,864]{0,1:T(8,128)}, u32[]{:S(2)}) copy-start(f32[128,864]{0,1:T(8,128)} %reduce_precision.50) | copy-start | bytes 1327108
  19.1 1.9 %copy-start.10 = (f32[3,3,8,1,1,1]{2,1,0,5,4,3:T(4,128)S(1)}, f32[3,3,8,1,1,1]{2,1,0,5,4,3:T(4,128)}, u32[]{:S(2)}) copy-start(f32[3,3,8,1,1,1]{2,1,0,5,4,3:T(4,128)} %constant.28) | copy-start | bytes 868
  20.8 1.7 %copy-start.5 = (f32[288,96]{1,0:T(8,128)S(1)}, f32[288,96]{1,0:T(8,128)}, u32[]{:S(2)}) copy-start(f32[288,96]{1,0:T(8,128)} %reshape.80) | copy-start | bytes 331780
  20.8 1.8 %copy-start.1 = (f32[128,864]{1,0:T(8,128)S(1)}, f32[128,864]{1,0:T(8,128)}, u32[]{:S(2)}) copy-start(f32[128,864]{1,0:T(8,128)} %copy.59) | copy-start | bytes 1327108
  37.1 8.3 %copy-start.13 = (f32[32]{0:T(128)S(1)}, f32[32]{0:T(128)}, u32[]{:S(2)}) copy-start(f32[32]{0:T(128)} %param.15) | copy-start | bytes 388
  41.2 11.9 %all-to-all-start.1 = ((f32[32,8,128]{2,1,0:T(8,128)}), f32[32,8,128]{2,1,0:T(8,128)S(1)}, u32[]{:S(2)}, u32[]{:S(2)}) async-start(f32[32,8,128]{2,1,0:T(8,128)} %get-tuple-element.9), calls=%async_computation.1 | async-start | bytes 262144 | tf_op jit(solution)/shard_map/all_to_all | solution.py:743
